TPU v7x, 32 devices: a whole 2x2x4 slice. The times are simulated.
32 devices in a mesh: seq: 8 (over z, x), head: 4 (over y, core).
Axes of the slice: x: 2, y: 2, z: 4, core: 2. Of those that a mesh axis runs over, the one named last changes fastest.
Arguments:
- query_rows: bfloat16 [6144, 4096], P('seq', 'head'), may hold values from -6 to 6
- key_rows: bfloat16 [6144, 4096], P('seq', 'head'), may hold values from -6 to 6
- value_rows: bfloat16 [6144, 4096], P('seq', 'head'), may hold values from -6 to 6
- grad_out: bfloat16 [6144, 4096], P('seq', 'head'), may hold values from -6 to 6
- doc_lengths: int32 [16], replicated, may hold values from 1 to 4224, as said below
Outputs:
- attended: bfloat16 [6144, 4096], P('seq', 'head')
- grad_query: bfloat16 [6144, 4096], P('seq', 'head')
- grad_key: bfloat16 [6144, 4096], P('seq', 'head')
- grad_value: bfloat16 [6144, 4096], P('seq', 'head')
Inputs may be any that keep to these rules, and one draw needn't show every extreme that they name: `doc_lengths`: the 16 lengths sum to 6144; the last document is the longest, exactly 4224 long, and the first is longer than 768.
All inputs are finite; a program needn't handle non-finite values.
Results may differ from a plain program's by a relative error of at most 0.0043.
Values sent between devices are 32-bit elements; how exact they have to be, the bound alone decides.
No kernel may reach another device: no remote copies, remote signals or barrier semaphores. Data moves between devices by JAX's collectives and lax.ppermute only.
A program may use at most 128 MiB of HBM per device.

v0:
```python
import jax
import jax.numpy as jnp
from jax import lax
from jax.sharding import PartitionSpec as P

DH = 128


def prefix(part, axis, combine, identity, reverse):
    count = lax.axis_size(axis)
    place = lax.axis_index(axis)
    ahead = count - 1 - place if reverse else place
    gathered = jax.tree.map(lambda a: lax.all_gather(a, axis), part)
    state = jax.tree.map(lambda a, e: jnp.zeros_like(a) + jnp.asarray(e, a.dtype), part, identity)

    def one(lap, state):
        source = count - 1 - lap if reverse else lap
        return combine(
            state, jax.tree.map(lambda a: lax.dynamic_index_in_dim(a, source, 0, False), gathered)
        )

    return lax.fori_loop(0, ahead, one, state)


def doc_layout(doc_lengths, offset, count):
    starts = jnp.cumsum(doc_lengths, dtype=jnp.int32) - doc_lengths
    positions = offset + jnp.arange(count, dtype=jnp.int32)
    first_start = jnp.max(
        jnp.where(starts[None, :] <= positions[:, None], starts[None, :], 0), axis=1
    )
    counts = (positions - first_start + 1).astype(jnp.float32)
    rowscale = 1.0 / jnp.sqrt(counts * DH)
    order = jnp.arange(count, dtype=jnp.int32)
    same_doc = (first_start[:, None] == first_start[None, :]) & (order[None, :] <= order[:, None])
    head_mask = (first_start < offset).astype(jnp.float32)
    tail_mask = (first_start == first_start[count - 1]).astype(jnp.float32)
    has_start = (first_start[count - 1] >= offset).astype(jnp.float32).reshape(1)
    return (rowscale, same_doc, head_mask, tail_mask, has_start)


def segment_join(earlier, later):
    return (
        jnp.where(later[1] > 0.5, later[0], earlier[0] + later[0]),
        jnp.maximum(earlier[1], later[1]),
    )


def per_device(query_rows, key_rows, value_rows, grad_out, doc_lengths):
    highest = lax.Precision.HIGHEST
    tok_count = query_rows.shape[0]
    head_count = query_rows.shape[1] // DH
    shape3 = (tok_count, head_count, DH)
    query_b = query_rows.reshape(shape3)
    key_b = key_rows.reshape(shape3)
    value_b = value_rows.reshape(shape3)
    grad_b = grad_out.reshape(shape3)
    offset = lax.axis_index("seq") * tok_count
    rowscale, same_doc, head_mask, tail_mask, has_start = doc_layout(doc_lengths, offset, tok_count)
    tail_keys = key_b * tail_mask.astype(jnp.bfloat16)[:, None, None]
    tail_state = jnp.einsum("shi,shj->hij", tail_keys, value_b, preferred_element_type=jnp.float32)
    query_f = query_b.astype(jnp.float32)
    scaled = rowscale[:, None, None] * grad_b.astype(jnp.float32)
    head_grad = jnp.einsum(
        "thi,thj->hij", query_f * head_mask[:, None, None], scaled, precision=highest
    )
    empty = (jnp.zeros_like(tail_state), jnp.zeros((1,), jnp.float32))
    state_in, _ = prefix((tail_state, has_start), "seq", segment_join, empty, False)
    grad_in, _ = prefix((head_grad, has_start), "seq", segment_join, empty, True)
    scores = jnp.einsum("thd,shd->hts", query_b, key_b, preferred_element_type=jnp.float32)
    scores_low = jnp.where(same_doc[None], scores, 0.0).astype(jnp.bfloat16)
    raw_grad = jnp.einsum("thd,shd->hts", grad_b, value_b, preferred_element_type=jnp.float32)
    grad_low = jnp.where(same_doc[None], raw_grad * rowscale[None, :, None], 0.0).astype(
        jnp.bfloat16
    )
    scaled_low = scaled.astype(jnp.bfloat16)
    key_f = key_b.astype(jnp.float32)
    value_f = value_b.astype(jnp.float32)
    carried = jnp.einsum("thi,hij->thj", query_f, state_in, precision=highest)
    attended = rowscale[:, None, None] * (
        jnp.einsum("hts,shd->thd", scores_low, value_b, preferred_element_type=jnp.float32)
        + head_mask[:, None, None] * carried
    )
    grad_query = jnp.einsum(
        "hts,shd->thd", grad_low, key_b, preferred_element_type=jnp.float32
    ) + head_mask[:, None, None] * jnp.einsum("hij,thj->thi", state_in, scaled, precision=highest)
    grad_key = jnp.einsum(
        "hts,thd->shd", grad_low, query_b, preferred_element_type=jnp.float32
    ) + tail_mask[:, None, None] * jnp.einsum("hij,shj->shi", grad_in, value_f, precision=highest)
    grad_value = jnp.einsum(
        "hts,thd->shd", scores_low, scaled_low, preferred_element_type=jnp.float32
    ) + tail_mask[:, None, None] * jnp.einsum("shi,hij->shj", key_f, grad_in, precision=highest)
    flat = (tok_count, head_count * DH)
    return (
        attended.astype(jnp.bfloat16).reshape(flat),
        grad_query.astype(jnp.bfloat16).reshape(flat),
        grad_key.astype(jnp.bfloat16).reshape(flat),
        grad_value.astype(jnp.bfloat16).reshape(flat),
    )


def solution(mesh):
    placed = (P("seq", "head"), P("seq", "head"), P("seq", "head"), P("seq", "head"), P())
    return jax.shard_map(
        per_device,
        mesh=mesh,
        in_specs=placed,
        out_specs=(P("seq", "head"), P("seq", "head"), P("seq", "head"), P("seq", "head")),
        check_vma=False,
    )
```

profile of v0, /device:TPU:26, one launch (start us, length us, event | category | flops | bytes accessed | tf_op | source)
XLA Modules:
  0.0 231.9 jit_solution(16935274124669625014)
XLA Ops:
  12.0 3.2 %copy.86 = bf16[768,1024]{0,1:T(8,128)(2,1)} copy(bf16[768,1024]{1,0:T(8,128)(2,1)} %param.12) | data formatting | bytes 3145728 | tf_op args[3]
  15.2 5.6 %fusion.3 = f32[8,128,128]{2,1,0:T(8,128)} fusion(bf16[768,8,128]{0,2,1:T(8,128)(2,1)S(1)} %bitcast.94, bf16[768,8,128]{0,2,1:T(8,128)(2,1)} %bitcast.98, f32[768]{0:T(1024)S(1)} %get-tuple-element.172, f32[768]{0:T(1024)S(1)} %multiply_rsqrt_fusion), kind=kOutput, calls=%fused_computation.12 | convolution fusion | flops 1211105280 | bytes 3676160 | tf_op jit(solution)/shard_map/thi,thj->hij/dot_general | solution.py:63
  20.8 3.0 %copy.109 = bf16[96,8,8,128]{3,2,1,0:T(8,128)(2,1)} copy(bf16[96,8,8,128]{3,1,2,0:T(8,128)(2,1)} %bitcast.105) | data formatting | bytes 3145728
  23.8 2.1 copy.82
  29.4 17.7 %all-reduce = f32[8]{0:T(128)S(1)} all-reduce(f32[8]{0:T(128)S(1)} %dynamic-update-slice), channel_id=1, replica_groups=mesh['seq'=8,'head'=4] {'seq'}, use_global_device_ids=true, to_apply=%add | all-reduce | flops 8 | bytes 64
  47.4 4.8 %select_convert_fusion.1 = bf16[8,768,768]{2,1,0:T(8,128)(2,1)S(1)} fusion(pred[768,768]{1,0:T(8,128)(4,1)S(1)} %fusion.8, bf16[768,8,128]{0,2,1:T(8,128)(2,1)} %bitcast.95, bf16[768,1024]{1,0:T(8,128)(2,1)} %param.10), kind=kOutput, calls=%fused_computation.5 | convolution fusion | flops 1217396736 | bytes 13172736 | tf_op jit(solution)/shard_map/thd,shd->hts/dot_general | solution.py:69
  52.3 3.1 %fusion.9 = f32[8,128,768]{2,1,0:T(8,128)} fusion(bf16[8,768,768]{2,1,0:T(8,128)(2,1)S(1)} %select_convert_fusion.1, bf16[768,8,128]{0,2,1:T(8,128)(2,1)S(1)} %bitcast.100, f32[768]{0:T(1024)S(1)} %multiply_rsqrt_fusion), kind=kOutput, calls=%fused_computation.21 | convolution fusion | flops 1210318848 | bytes 14158848 | tf_op jit(solution)/shard_map/hts,thd->shd/dot_general | solution.py:89
  55.4 6.1 %select_convert_fusion = bf16[8,768,768]{2,1,0:T(8,128)(2,1)} fusion(f32[768]{0:T(1024)S(1)} %multiply_rsqrt_fusion, pred[768,768]{1,0:T(8,128)(4,1)S(1)} %fusion.8, bf16[768,8,128]{0,2,1:T(8,128)(2,1)S(1)} %bitcast.101, bf16[768,1024]{1,0:T(8,128)(2,1)S(1)} %copy-done), kind=kOutput, calls=%fused_computation.4 | convolution fusion | flops 1222115328 | bytes 13175808 | tf_op jit(solution)/shard_map/thd,shd->hts/dot_general | solution.py:71
  61.4 4.9 %fusion.11 = f32[8,768,128]{1,2,0:T(8,128)} fusion(bf16[8,768,768]{2,1,0:T(8,128)(2,1)S(1)} %select_convert_fusion.1, bf16[768,1024]{1,0:T(8,128)(2,1)S(1)} %copy-done), kind=kOutput, calls=%fused_computation.22 | convolution fusion | flops 1207959552 | bytes 14155776 | tf_op jit(solution)/shard_map/hts,shd->thd/dot_general | solution.py:80
  66.4 26.2 %all-gather.7.cloned.1.call-done = f32[64,128,128]{2,1,0:T(8,128)} async-done(((f32[8,128,128]{2,1,0:T(8,128)}), f32[64,128,128]{2,1,0:T(8,128)}) %all-gather.7.cloned.1.call-update) | async-done | bytes 4194320 | tf_op jit(solution)/shard_map/all_gather | solution.py:13
  92.6 73.5 %all-gather.5.cloned.1.call-done = f32[64,128,128]{2,1,0:T(8,128)} async-done(((f32[8,128,128]{2,1,0:T(8,128)}), f32[64,128,128]{2,1,0:T(8,128)}) %all-gather.5.cloned.1.call-update) | async-done | bytes 4194320 | tf_op jit(solution)/shard_map/all_gather | solution.py:13
  166.2 17.7 %while.26 = (s32[]{:T(128)}, f32[8,128,128]{2,1,0:T(8,128)S(1)}, s32[]{:T(128)}, f32[8,1]{0,1:T(1,128)S(1)}, f32[8,8,128,128]{3,2,1,0:T(8,128)}, /*index=5*/s32[]{:T(128)}, s32[]{:T(128)}, s32[]{:T(128)}) while((s32[]{:T(128)}, f32[8,128,128]{2,1,0:T(8,128)S(1)}, s32[]{:T(128)}, f32[8,1]{0,1:T(1,128)S(1)}, f32[8,8,128,128]{3,2,1,0:T(8,128)}, ...), condition=%wide.region_3.4_spmd, body=%wide.region_2.3_spmd.sunk | while | flops 262150 | bytes 1573005 | solution.py:22
  166.8 1.9 add_select_fusion.4
  169.3 1.9 add_select_fusion.4
  176.8 1.9 add_select_fusion.4
  179.3 1.9 add_select_fusion.4
  183.9 6.1 %fusion.7 = f32[8,768,128]{1,2,0:T(8,128)} fusion(f32[8,128,128]{2,1,0:T(8,128)S(1)} %get-tuple-element.132, bf16[768,8,128]{0,2,1:T(8,128)(2,1)} %bitcast.99, f32[768]{0:T(1024)S(1)} %multiply_rsqrt_fusion), kind=kOutput, calls=%fused_computation.18 | convolution fusion | flops 1209532416 | bytes 5245952 | tf_op jit(solution)/shard_map/hij,thj->thi/dot_general | solution.py:85
  191.5 9.4 %add_convert_fusion.1 = bf16[8,768,128]{1,2,0:T(8,128)(2,1)} fusion(f32[8,768,128]{1,2,0:T(8,128)} %fusion.7, bf16[8,768,768]{2,1,0:T(8,128)(2,1)} %select_convert_fusion, bf16[768,8,128]{0,2,1:T(8,128)(2,1)} %copy-done.5, f32[768]{0:T(1024)S(1)} %get-tuple-element.172), kind=kOutput, calls=%fused_computation.15 | convolution fusion | flops 1210318848 | bytes 15731712 | tf_op jit(solution)/shard_map/hts,shd->thd/dot_general | solution.py:83
  200.9 6.4 %fusion = bf16[768,8,128]{0,2,1:T(8,128)(2,1)} fusion(f32[8,128,768]{2,1,0:T(8,128)S(1)} %fusion.13, bf16[768,8,128]{0,2,1:T(8,128)(2,1)S(1)} %bitcast.97, bf16[8,768,768]{2,1,0:T(8,128)(2,1)} %select_convert_fusion, f32[768]{0:T(1024)S(1)} %get-tuple-element.171), kind=kOutput, calls=%fused_computation.7 | convolution fusion | flops 1210318848 | bytes 15731712 | tf_op jit(solution)/shard_map/hts,thd->shd/dot_general | solution.py:86
  207.3 2.6 %copy.99 = bf16[768,1024]{1,0:T(8,128)(2,1)} copy(bf16[768,1024]{0,1:T(8,128)(2,1)} %bitcast.102) | data formatting | bytes 3145728
  209.9 2.6 %copy.98 = bf16[768,1024]{1,0:T(8,128)(2,1)} copy(bf16[768,1024]{0,1:T(8,128)(2,1)} %bitcast.103) | data formatting | bytes 3145728
  212.5 5.3 %fusion.2 = bf16[768,8,128]{0,2,1:T(8,128)(2,1)} fusion(f32[8,768,128]{1,2,0:T(8,128)} %fusion.11, f32[8,128,128]{2,1,0:T(8,128)S(1)} %get-tuple-element.132, bf16[768,8,128]{0,2,1:T(8,128)(2,1)} %bitcast.96, f32[768]{0:T(1024)S(1)} %get-tuple-element.172, f32[768]{0:T(1024)S(1)} %multiply_rsqrt_fusion), kind=kOutput, calls=%fused_computation.10 | convolution fusion | flops 1211105280 | bytes 6821888 | tf_op jit(solution)/shard_map/thi,hij->thj/dot_general | solution.py:78
  217.9 2.9 %add_convert_fusion = bf16[8,128,768]{2,1,0:T(8,128)(2,1)} fusion(f32[8,128,768]{2,1,0:T(8,128)S(1)} %copy-done.4, f32[8,128,128]{2,1,0:T(8,128)S(1)} %get-tuple-element.133, f32[768]{0:T(1024)S(1)} %get-tuple-element.171, bf16[768,1024]{1,0:T(8,128)(2,1)S(1)} %copy-done.6), kind=kOutput, calls=%fused_computation.11 | convolution fusion | flops 1210318848 | bytes 6818816 | tf_op jit(solution)/shard_map/shi,hij->shj/dot_general | solution.py:91
  220.8 2.7 %copy.100 = bf16[768,1024]{1,0:T(8,128)(2,1)} copy(bf16[768,1024]{0,1:T(8,128)(2,1)} %bitcast.106) | data formatting | bytes 3145728
  (52 shorter events, 20.9 us)
Async XLA Ops:
  7.2 18.8 %copy-start = (bf16[768,1024]{1,0:T(8,128)(2,1)S(1)}, bf16[768,1024]{1,0:T(8,128)(2,1)}, u32[]{:S(2)}) copy-start(bf16[768,1024]{1,0:T(8,128)(2,1)} %param.11) | copy-start | bytes 4718596
  7.2 85.4 %all-gather.7.cloned.1.call-start = ((), (), s32[]{:S(2)}) async-start(), calls=%async_computation.1 | async-start | bytes 4718592 | tf_op jit(solution)/shard_map/all_gather | solution.py:13
  12.0 3.2 %copy-start.1 = (bf16[768,1024]{0,1:T(8,128)(2,1)}, bf16[768,1024]{0,1:T(8,128)(2,1)S(1)}, u32[]{:S(2)}) copy-start(bf16[768,1024]{0,1:T(8,128)(2,1)S(1)} %copy.106) | copy-start | bytes 4718596
  20.8 145.3 %all-gather.5.cloned.1.call-start = ((), (), s32[]{:S(2)}) async-start(), calls=%async_computation | async-start | bytes 4718592 | tf_op jit(solution)/shard_map/all_gather | solution.py:13
  25.9 1.4 copy-start.5
  26.0 2.0 copy-start.8
  47.4 4.9 %copy-start.3 = (bf16[768,1024]{0,1:T(8,128)(2,1)S(1)}, bf16[768,1024]{0,1:T(8,128)(2,1)}, u32[]{:S(2)}) copy-start(bf16[768,1024]{0,1:T(8,128)(2,1)} %copy.86) | copy-start | bytes 4718596
  191.5 9.5 %copy-start.2 = (bf16[768,1024]{0,1:T(8,128)(2,1)S(1)}, bf16[768,1024]{0,1:T(8,128)(2,1)}, u32[]{:S(2)}) copy-start(bf16[768,1024]{0,1:T(8,128)(2,1)} %copy-done.1) | copy-start | bytes 4718596
  212.5 5.4 %copy-start.4 = (f32[8,128,768]{2,1,0:T(8,128)S(1)}, f32[8,128,768]{2,1,0:T(8,128)}, u32[]{:S(2)}) copy-start(f32[8,128,768]{2,1,0:T(8,128)} %fusion.9) | copy-start | bytes 9437188
  212.5 5.4 %copy-start.6 = (bf16[768,1024]{1,0:T(8,128)(2,1)S(1)}, bf16[768,1024]{1,0:T(8,128)(2,1)}, u32[]{:S(2)}) copy-start(bf16[768,1024]{1,0:T(8,128)(2,1)} %param.10) | copy-start | bytes 4718596
  220.8 2.7 %copy-start.7 = (bf16[768,8,128]{0,2,1:T(8,128)(2,1)S(1)}, bf16[768,8,128]{0,2,1:T(8,128)(2,1)}, u32[]{:S(2)}) copy-start(bf16[768,8,128]{0,2,1:T(8,128)(2,1)} %fusion.2) | copy-start | bytes 4718596
Sparse Core Ops, SparseCore 0:
  20.9 71.6 all-gather.6
  94.7 71.3 all-gather.4
where the time goes:
time: 233 us; the launch traced here: 232 us
  waiting for transfers between devices  99.7 us (43%)
  matrix products  57.6 us (25%)
  local copies, waits for them, and re-layouts  22.4 us (10%)
  other arithmetic  19.2 us (8%)
  blocking collectives  17.7 us (8%)
  between operations  14.8 us (6%)
    all_gather x2, waiting for transfers between devices, prefix(): gathered = jax.tree.map(lambda a: lax.all_gather(a, axis), part)  99.7 us
    unnamed x1, blocking collectives  17.7 us
    unnamed x27, local copies, waits for them, and re-layouts  17 us
    select_n x7, other arithmetic, segment_join(): jnp.where(later[1] > 0.5, later[0], earlier[0] + later[0])  13.2 us
    dot_general x1, matrix products, per_device(): jnp.einsum('hts,shd->thd', grad_low, key_b, preferred_element_type=jnp.fl...  9.44 us
    dot_general x1, matrix products, per_device(): jnp.einsum('hts,thd->shd', grad_low, query_b, preferred_element_type=jnp....  6.42 us
    dot_general x1, matrix products, per_device(): jnp.einsum('hij,thj->thi', state_in, scaled, precision=highest)  6.15 us
    dot_general x1, matrix products, per_device(): jnp.einsum('thd,shd->hts', grad_b, value_b, preferred_element_type=jnp.fl...  6.06 us
  transfers between devices with their start and end apart: 2, of which 2 were waited for; matrix products, arithmetic and copies ran while one was open for 12% of the time, Pallas kernels for 0%

commit v1 on v0

v1 whole, which is shorter than its diff:
```python
import functools

import jax
import jax.numpy as jnp
from jax import lax
from jax.experimental import pallas as pl
from jax.experimental.pallas import tpu as pltpu
from jax.sharding import PartitionSpec as P

DH = 128
ROWS = 256
F32 = jnp.float32
LOW = jnp.bfloat16

NT = (((1,), (1,)), ((), ()))
TN = (((0,), (0,)), ((), ()))
NN = (((1,), (0,)), ((), ()))


def dot(a, b, dims):
    return lax.dot_general(a, b, dims, preferred_element_type=F32)


def split(a):
    high = a.astype(LOW)
    return high, (a - high.astype(F32)).astype(LOW)


def layout_columns(lengths, offset, count):
    row = lax.broadcasted_iota(jnp.int32, (count, DH), 0) + offset
    first = jnp.zeros((count, DH), jnp.int32)
    start = jnp.int32(0)
    for j in range(lengths.shape[0]):
        first = jnp.where(row >= start, start, first)
        start = start + lengths[j]
    scale = 1.0 / jnp.sqrt((row - first + 1).astype(F32) * DH)
    return scale, first - offset


def state_kernel(make_layout, lengths, q_ref, k_ref, v_ref, g_ref, *refs):
    count = q_ref.shape[0]
    if make_layout:
        kv_ref, qg_ref, scale_ref, first_ref = refs

        @pl.when(pl.program_id(0) == 0)
        def _():
            scale, first = layout_columns(lengths, lax.axis_index("seq") * count, count)
            scale_ref[...] = scale
            first_ref[...] = first
    else:
        scale_ref, first_ref, kv_ref, qg_ref = refs
    first = first_ref[...]
    row = lax.broadcasted_iota(jnp.int32, (count, DH), 0)
    tail_start = first_ref[count - 1, 0]
    for h in range(kv_ref.shape[0]):
        cols = slice(h * DH, (h + 1) * DH)
        tail = jnp.where(row >= tail_start, k_ref[:, cols], jnp.zeros((), LOW))
        kv_ref[h] = dot(tail, v_ref[:, cols], TN)
        scaled = jnp.where(first < 0, scale_ref[...] * g_ref[:, cols].astype(F32), 0.0)
        high, rest = split(scaled)
        both = dot(q_ref[:, cols], jnp.concatenate([high, rest], axis=1), TN)
        qg_ref[h] = both[:, :DH] + both[:, DH:]


def local_kernel(q_ref, k_ref, v_ref, g_ref, scale_ref, first_ref, a_ref, dq_ref, dk_ref, dv_ref):
    count = q_ref.shape[0]
    for r in range(0, count, ROWS):
        rows = slice(r, r + ROWS)
        wide = r + ROWS
        q, g = q_ref[rows], g_ref[rows]
        k, v = k_ref[:wide], v_ref[:wide]
        scale = scale_ref[rows]
        many = wide // DH
        first_w = jnp.concatenate([first_ref[rows]] * many, axis=1)
        scale_w = jnp.concatenate([scale] * many, axis=1)
        row = lax.broadcasted_iota(jnp.int32, (ROWS, wide), 0) + r
        col = lax.broadcasted_iota(jnp.int32, (ROWS, wide), 1)
        mask = (col >= first_w) & (col <= row)
        scores = jnp.where(mask, dot(q, k, NT), 0.0).astype(LOW)
        grads = jnp.where(mask, dot(g, v, NT) * scale_w, 0.0).astype(LOW)
        scaled = (scale * g.astype(F32)).astype(LOW)
        a_ref[rows] = scale * dot(scores, v, NN)
        dq_ref[rows] = dot(grads, k, NN)
        dk = dot(grads, q, TN)
        dv = dot(scores, scaled, TN)
        if r:
            dk_ref[:r] += dk[:r]
            dv_ref[:r] += dv[:r]
        dk_ref[rows] = dk[r:]
        dv_ref[rows] = dv[r:]


def final_kernel(
    q_ref, k_ref, v_ref, g_ref, a_ref, dq_ref, dk_ref, dv_ref, kv_ref, qg_ref, scale_ref, first_ref, *refs
):
    out_a, out_q, out_k, out_v = refs[-4:]
    count = q_ref.shape[0]
    scale = jnp.where(first_ref[...] < 0, scale_ref[...], 0.0)
    row = lax.broadcasted_iota(jnp.int32, (count, DH), 0)
    tail = row >= first_ref[count - 1, 0]

    def carried(rows_ref, state, dims):
        high, rest = split(state)
        rows = rows_ref[...]
        return dot(rows, high, dims) + dot(rows, rest, dims)

    kv = kv_ref[0]
    qg = qg_ref[0]
    out_a[...] = (a_ref[...] + scale * carried(q_ref, kv, NN)).astype(LOW)
    out_q[...] = (dq_ref[...] + scale * carried(g_ref, kv, NT)).astype(LOW)
    out_k[...] = (dk_ref[...] + jnp.where(tail, carried(v_ref, qg, NT), 0.0)).astype(LOW)
    out_v[...] = (dv_ref[...] + jnp.where(tail, carried(k_ref, qg, NN), 0.0)).astype(LOW)


def head_block(count, base=0):
    return pl.BlockSpec((count, DH), lambda i, *_: (0, base + i))


def whole(count):
    return pl.BlockSpec((count, DH), lambda i, *_: (0, 0))


STATE = pl.BlockSpec((1, DH, DH), lambda i, *_: (i, 0, 0))


def states(arrays, lengths, base, heads, layout):
    count = arrays[0].shape[0]
    shape = jax.ShapeDtypeStruct((heads, DH, DH), F32)
    out_shape = [shape, shape]
    out_specs = [STATE, STATE]
    in_specs = [head_block(count, base)] * 4
    if layout is None:
        out_shape += [jax.ShapeDtypeStruct((count, DH), F32), jax.ShapeDtypeStruct((count, DH), jnp.int32)]
        out_specs += [whole(count)] * 2
    else:
        in_specs += [whole(count)] * 2
    return pl.pallas_call(
        functools.partial(state_kernel, layout is None),
        out_shape=out_shape,
        grid_spec=pltpu.PrefetchScalarGridSpec(
            num_scalar_prefetch=1, grid=(heads,), in_specs=in_specs, out_specs=out_specs
        ),
        name="states",
    )(lengths, *arrays, *(layout or ()))


def local(arrays, layout, base, heads):
    count = arrays[0].shape[0]
    shape = jax.ShapeDtypeStruct((count, heads * DH), F32)
    return pl.pallas_call(
        local_kernel,
        out_shape=[shape] * 4,
        grid=(heads,),
        in_specs=[head_block(count, base)] * 4 + [whole(count)] * 2,
        out_specs=[head_block(count)] * 4,
        name="local",
    )(*arrays, *layout)


def final(arrays, parts, kv, qg, layout, base, outs):
    count, width = arrays[0].shape
    heads = kv.shape[0]
    shape = jax.ShapeDtypeStruct((count, width), LOW)
    extra = tuple(outs or ())
    return pl.pallas_call(
        final_kernel,
        out_shape=[shape] * 4,
        grid=(heads,),
        in_specs=[head_block(count, base)] * 4
        + [head_block(count)] * 4
        + [STATE] * 2
        + [whole(count)] * 2
        + [pl.BlockSpec(memory_space=pl.ANY)] * len(extra),
        out_specs=[head_block(count, base)] * 4,
        input_output_aliases={12 + i: i for i in range(len(extra))},
        name="final",
    )(*arrays, *parts, kv, qg, *layout, *extra)


PAIRS = [(d, d ^ 1) for d in range(8)]
UP_1 = [(0, 2), (2, 4), (3, 5)]
UP_2 = [(0, 2), (4, 6), (5, 7)]
DOWN_1 = [(2, 0), (6, 4), (7, 5)]
DOWN_2 = [(2, 0), (4, 2), (5, 3)]


def choose(place, default, *cases):
    value = default
    for devices, other in cases:
        hit = functools.reduce(jnp.logical_or, [place == d for d in devices])
        value = jnp.where(hit, other, value)
    return value


class Exchange:
    def __init__(self, kv, qg, place, joined):
        half = kv.shape[0] // 2
        self.half, self.place, self.joined = half, place, joined
        self.k = (kv[:half], kv[half:])
        self.q = (qg[:half], qg[half:])
        self.odd = place % 2 == 1
        self.mine_k = jnp.where(self.odd, self.k[1], self.k[0])
        self.mine_q = jnp.where(self.odd, self.q[1], self.q[0])
        self.give_k = jnp.where(self.odd, self.k[0], self.k[1])
        self.give_q = jnp.where(self.odd, self.q[0], self.q[1])

    def swap(self, value):
        return lax.ppermute(value, "seq", PAIRS)

    def step0(self):
        send = choose(self.place, self.give_k, ((0, 1), self.k[0]), ((6, 7), self.give_q))
        self.x0 = self.swap(send)

    def step1(self):
        d = self.place
        self.sum_k = self.mine_k + self.x0
        self.sum_q6 = self.mine_q + self.x0
        link = jnp.where(self.joined, 1.0, 0.0)
        send = choose(
            d, self.give_q, ((0, 1), self.k[1]), ((2,), self.k[0]), ((3,), self.q[0]), ((6,), self.k[1]), ((7,), self.q[1])
        )
        up = choose(d, self.sum_k, ((0,), self.x0 + link * self.k[0]))
        down = choose(d, self.sum_q6, ((2,), self.q[0]))
        self.x1 = self.swap(send)
        self.up1 = lax.ppermute(up, "seq", UP_1)
        self.down1 = lax.ppermute(down, "seq", DOWN_1)

    def step2(self):
        d = self.place
        link = jnp.where(self.joined, 1.0, 0.0)
        self.sum_q = self.mine_q + self.x1
        up = choose(d, self.up1 + self.sum_k, ((0,), self.x1 + link * self.k[1]))
        down = choose(d, self.down1 + self.sum_q, ((2,), self.q[1]))
        send = choose(d, self.up1, ((0,), self.down1), ((1,), self.q[0]), ((4,), self.up1 + self.k[0]))
        self.x2 = self.swap(send)
        self.up2 = lax.ppermute(up, "seq", UP_2)
        self.down2 = lax.ppermute(down, "seq", DOWN_2)

    def step3(self):
        d = self.place
        send = choose(
            d,
            self.down1,
            ((0, 2), self.down2),
            ((1,), self.q[1]),
            ((3,), self.down2 + self.q[1]),
            ((5,), self.down1 + self.q[1]),
            ((6,), self.up2 + self.k[0]),
            ((7,), self.up2),
        )
        self.x3 = self.swap(send)

    def result(self):
        d = self.place
        link = jnp.where(self.joined, 1.0, 0.0)
        zero = jnp.zeros_like(self.x0)
        kv_low = choose(
            d,
            zero,
            ((1,), self.x0),
            ((2, 4), self.up1),
            ((3,), self.x1),
            ((5,), self.x2),
            ((6,), self.up2),
            ((7,), self.x3),
        )
        kv_high = choose(
            d,
            zero,
            ((1,), self.x1),
            ((2,), self.up2),
            ((3,), self.x0),
            ((4,), self.x2),
            ((5,), self.up1 + self.x0),
            ((6,), self.x3),
            ((7,), self.up2 + self.x1),
        )
        qg_low = choose(
            d,
            zero,
            ((0,), self.x2 + link * self.down1),
            ((1,), self.x2),
            ((2,), self.x1 + self.down2),
            ((3,), self.x3),
            ((4,), self.x1 + self.down1),
            ((5,), self.x3),
            ((6,), self.x0),
        )
        qg_high = choose(
            d,
            zero,
            ((0,), self.x3 + link * self.down2),
            ((1,), self.x3),
            ((2,), self.x3),
            ((3,), self.down2),
            ((4,), self.x3),
            ((5,), self.down1),
            ((6,), self.x1),
        )
        return jnp.concatenate([kv_low, kv_high]), jnp.concatenate([qg_low, qg_high])


def gathered_states(kv, qg, starts_here):
    count = lax.axis_size("seq")
    place = lax.axis_index("seq")
    kv_all, qg_all, start_all = lax.all_gather((kv, qg, starts_here), "seq")
    order = jnp.arange(count)
    last_start = jnp.max(jnp.where((order < place) & (start_all > 0.5), order, 0))
    next_start = jnp.min(jnp.where((order > place) & (start_all > 0.5), order, count))
    before = (order < place) & (order >= last_start)
    after = (order > place) & (order <= next_start)

    def total(pick, values):
        return jnp.sum(jnp.where(pick[:, None, None, None], values, 0.0), axis=0)

    return total(before, kv_all), total(after, qg_all)


def per_device(query_rows, key_rows, value_rows, grad_out, doc_lengths):
    arrays = (query_rows, key_rows, value_rows, grad_out)
    count, width = query_rows.shape
    heads = width // DH
    place = lax.axis_index("seq")
    if lax.axis_size("seq") != 8:
        kv, qg, *layout = states(arrays, doc_lengths, 0, heads, None)
        starts_here = (layout[1][count - 1, 0] >= 0).astype(F32)
        parts = local(arrays, layout, 0, heads)
        kv, qg = gathered_states(kv, qg, starts_here)
        return tuple(final(arrays, parts, kv, qg, layout, 0, None))
    joined = doc_lengths[0] >= 2 * count
    chunks = 2
    each = heads // chunks
    kv, qg, *layout = states(arrays, doc_lengths, 0, each, None)
    flows = [Exchange(kv, qg, place, joined)]
    for c in range(1, chunks):
        kv, qg = states(arrays, doc_lengths, c * each, each, layout)
        flows.append(Exchange(kv, qg, place, joined))
    for step in ("step0", "step1", "step2", "step3"):
        for flow in flows:
            getattr(flow, step)()
    outs = None
    parts = [local(arrays, layout, c * each, each) for c in range(chunks)]
    for c, flow in enumerate(flows):
        outs = final(arrays, parts[c], *flow.result(), layout, c * each, outs)
    return tuple(outs)


def solution(mesh):
    placed = P("seq", "head")
    return jax.shard_map(
        per_device,
        mesh=mesh,
        in_specs=(placed, placed, placed, placed, P()),
        out_specs=(placed, placed, placed, placed),
        check_vma=False,
    )
```

time: 233 us -> 89.1 us (0.38)
  the two profiles are of different devices: /device:TPU:26 before, /device:TPU:0 now
where the time goes in v1:
time: 89.1 us; the launch traced here: 88.5 us
  Pallas kernels  44.7 us (50%)
  starting transfers between devices  32.8 us (37%)
  waiting for transfers between devices  5.38 us (6%)
  other arithmetic  4.69 us (5%)
  between operations  1 us (1%)
    pallas_call x2, Pallas kernels, local(): pl.pallas_call(local_kernel, out_shape=[shape] * 4, grid=(heads,), in_spe...  18.8 us
    pallas_call x2, Pallas kernels, final(): pl.pallas_call(final_kernel, out_shape=[shape] * 4, grid=(heads,), in_spe...  14.6 us
    pallas_call x2, Pallas kernels, states(): pl.pallas_call(functools.partial(state_kernel, layout is None), out_shape...  11.2 us
    ppermute x8, starting transfers between devices, swap(): return lax.ppermute(value, 'seq', PAIRS)  9.37 us
    ppermute x2, starting transfers between devices, step1(): self.up1 = lax.ppermute(up, 'seq', UP_1)  9.11 us
    ppermute x2, starting transfers between devices, step2(): self.up2 = lax.ppermute(up, 'seq', UP_2)  9.11 us
    ppermute x8, waiting for transfers between devices, swap(): return lax.ppermute(value, 'seq', PAIRS)  5.08 us
    select_n x10, other arithmetic, choose(): value = jnp.where(hit, other, value)  2.99 us
  transfers between devices with their start and end apart: 16, of which 5 were waited for; matrix products, arithmetic and copies ran while one was open for 3% of the time, Pallas kernels for 27%

profile of v1, /device:TPU:0, one launch (start us, length us, event | category | flops | bytes accessed | tf_op | source)
XLA Modules:
  0.0 88.5 jit_solution(8189387414817834706)
XLA Ops:
  0.7 5.8 %states.2 = (f32[4,128,128]{2,1,0:T(8,128)}, f32[4,128,128]{2,1,0:T(8,128)}, f32[768,128]{1,0:T(8,128)}, s32[768,128]{1,0:T(8,128)}) custom-call(s32[16]{0:T(128)} %lengths.3, bf16[768,1024]{1,0:T(8,128)(2,1)} %q_ref.11, bf16[768,1024]{1,0:T(8,128)(2,1)} %k_ref.11, bf16[768,1024]{1,0:T(8,128)(2,1)} %v_ref.11, bf16[768,1024]{1,0:T(8,128)(2,1)} %g_ref.11), custom_call_target="tpu_custom_call" | custom-call | tf_op jit(solution)/shard_map/states/pallas_call | solution.py:137
  6.5 1.1 %select_select_fusion.9 = (f32[2,128,128]{2,1,0:T(8,128)S(1)}, f32[2,128,128]{2,1,0:T(8,128)S(1)}) fusion(f32[4,128,128]{2,1,0:T(8,128)} %get-tuple-element.35, f32[4,128,128]{2,1,0:T(8,128)} %get-tuple-element.34, pred[]{:T(512)S(6)} %eq.27, pred[]{:T(512)S(6)} %or.8, pred[]{:T(512)S(6)} %eq.25, pred[]{:T(512)S(6)} %eq.24, pred[]{:T(512)S(6)} %eq.23, ...), kind=kLoop, calls=%fused_computation.28 | loop fusion | flops 294912 | bytes 786439 | tf_op jit(solution)/shard_map/jit(_where)/select_n | solution.py:191
  7.6 3.0 %collective-permute-start.8 = (f32[2,128,128]{2,1,0:T(8,128)S(1)}, f32[2,128,128]{2,1,0:T(8,128)S(1)}, u32[]{:S(2)}, u32[]{:S(2)}) collective-permute-start(f32[2,128,128]{2,1,0:T(8,128)S(1)} %get-tuple-element.52), channel_id=1, source_target_pairs={{0,4},{4,0},{8,12},{12,8},{16,20},{20,16},{24,28},{28,24},{1,5},{5... | collective-permute-start | bytes 393224 | tf_op jit(solution)/shard_map/ppermute | solution.py:208
  10.7 5.5 %states.3 = (f32[4,128,128]{2,1,0:T(8,128)}, f32[4,128,128]{2,1,0:T(8,128)}) custom-call(s32[16]{0:T(128)} %lengths.3, bf16[768,1024]{1,0:T(8,128)(2,1)} %q_ref.11, bf16[768,1024]{1,0:T(8,128)(2,1)} %k_ref.11, bf16[768,1024]{1,0:T(8,128)(2,1)} %v_ref.11, bf16[768,1024]{1,0:T(8,128)(2,1)} %g_ref.11, f32[768,128]{1,0:T(8,128)} %get-tuple-element.22.scale_ref.refs_0_, ...), custom_call_target="tpu_custom_call" | custom-call | tf_op jit(solution)/shard_map/states/pallas_call | solution.py:137
  16.2 1.1 %select_select_fusion.15 = (f32[2,128,128]{2,1,0:T(8,128)S(1)}, f32[2,128,128]{2,1,0:T(8,128)S(1)}) fusion(f32[4,128,128]{2,1,0:T(8,128)} %get-tuple-element.29, f32[4,128,128]{2,1,0:T(8,128)} %get-tuple-element.28, pred[]{:T(512)S(6)} %eq.27, pred[]{:T(512)S(6)} %or.8, pred[]{:T(512)S(6)} %eq.25, pred[]{:T(512)S(6)} %eq.24, pred[]{:T(512)S(6)} %eq.23, ...), kind=kLoop, calls=%fused_computation.39 | loop fusion | flops 294912 | bytes 786439 | tf_op jit(solution)/shard_map/jit(_where)/select_n | solution.py:191
  17.3 2.0 %collective-permute-start = (f32[2,128,128]{2,1,0:T(8,128)S(1)}, f32[2,128,128]{2,1,0:T(8,128)S(1)}, u32[]{:S(2)}, u32[]{:S(2)}) collective-permute-start(f32[2,128,128]{2,1,0:T(8,128)S(1)} %get-tuple-element.58), channel_id=1, source_target_pairs={{0,4},{4,0},{8,12},{12,8},{16,20},{20,16},{24,28},{28,24},{1,5},{5... | collective-permute-start | bytes 393224 | tf_op jit(solution)/shard_map/ppermute | solution.py:208
  19.4 9.4 %local.3 = (f32[768,512]{1,0:T(8,128)}, f32[768,512]{1,0:T(8,128)}, f32[768,512]{1,0:T(8,128)}, f32[768,512]{1,0:T(8,128)}) custom-call(bf16[768,1024]{1,0:T(8,128)(2,1)} %q_ref.11, bf16[768,1024]{1,0:T(8,128)(2,1)} %k_ref.11, bf16[768,1024]{1,0:T(8,128)(2,1)} %v_ref.11, bf16[768,1024]{1,0:T(8,128)(2,1)} %g_ref.11, ...), custom_call_target="tpu_custom_call" | custom-call | tf_op jit(solution)/shard_map/local/pallas_call | solution.py:150
  28.8 9.4 %local.2 = (f32[768,512]{1,0:T(8,128)}, f32[768,512]{1,0:T(8,128)}, f32[768,512]{1,0:T(8,128)}, f32[768,512]{1,0:T(8,128)}) custom-call(bf16[768,1024]{1,0:T(8,128)(2,1)} %q_ref.11, bf16[768,1024]{1,0:T(8,128)(2,1)} %k_ref.11, bf16[768,1024]{1,0:T(8,128)(2,1)} %v_ref.11, bf16[768,1024]{1,0:T(8,128)(2,1)} %g_ref.11, ...), custom_call_target="tpu_custom_call" | custom-call | tf_op jit(solution)/shard_map/local/pallas_call | solution.py:150
  38.4 1.3 %collective-permute-start.12 = (f32[2,128,128]{2,1,0:T(8,128)S(1)}, f32[2,128,128]{2,1,0:T(8,128)S(1)}, u32[]{:S(2)}, u32[]{:S(2)}) collective-permute-start(f32[2,128,128]{2,1,0:T(8,128)S(1)} %get-tuple-element.62), channel_id=1, source_target_pairs={{8,0},{24,16},{28,20},{9,1},{25,17},{29,21},{10,2},{26,18},{30,22}... | collective-permute-start | bytes 393224 | tf_op jit(solution)/shard_map/ppermute | solution.py:226
  39.7 4.6 %collective-permute-start.10 = (f32[2,128,128]{2,1,0:T(8,128)S(1)}, f32[2,128,128]{2,1,0:T(8,128)S(1)}, u32[]{:S(2)}, u32[]{:S(2)}) collective-permute-start(f32[2,128,128]{2,1,0:T(8,128)S(1)} %get-tuple-element.63), channel_id=1, source_target_pairs={{0,8},{8,16},{12,20},{1,9},{9,17},{13,21},{2,10},{10,18},{14,22},{... | collective-permute-start | bytes 393224 | tf_op jit(solution)/shard_map/ppermute | solution.py:225
  44.3 1.3 %collective-permute-start.4 = (f32[2,128,128]{2,1,0:T(8,128)S(1)}, f32[2,128,128]{2,1,0:T(8,128)S(1)}, u32[]{:S(2)}, u32[]{:S(2)}) collective-permute-start(f32[2,128,128]{2,1,0:T(8,128)S(1)} %get-tuple-element.66), channel_id=1, source_target_pairs={{8,0},{24,16},{28,20},{9,1},{25,17},{29,21},{10,2},{26,18},{30,22}... | collective-permute-start | bytes 393224 | tf_op jit(solution)/shard_map/ppermute | solution.py:226
  45.6 4.6 %collective-permute-start.2 = (f32[2,128,128]{2,1,0:T(8,128)S(1)}, f32[2,128,128]{2,1,0:T(8,128)S(1)}, u32[]{:S(2)}, u32[]{:S(2)}) collective-permute-start(f32[2,128,128]{2,1,0:T(8,128)S(1)} %get-tuple-element.67), channel_id=1, source_target_pairs={{0,8},{8,16},{12,20},{1,9},{9,17},{13,21},{2,10},{10,18},{14,22},{... | collective-permute-start | bytes 393224 | tf_op jit(solution)/shard_map/ppermute | solution.py:225
  50.3 1.3 %collective-permute-start.13 = (f32[2,128,128]{2,1,0:T(8,128)S(1)}, f32[2,128,128]{2,1,0:T(8,128)S(1)}, u32[]{:S(2)}, u32[]{:S(2)}) collective-permute-start(f32[2,128,128]{2,1,0:T(8,128)S(1)} %get-tuple-element.60), channel_id=1, source_target_pairs={{8,0},{16,8},{20,12},{9,1},{17,9},{21,13},{10,2},{18,10},{22,14},{... | collective-permute-start | bytes 393224 | tf_op jit(solution)/shard_map/ppermute | solution.py:237
  51.6 4.6 %collective-permute-start.11 = (f32[2,128,128]{2,1,0:T(8,128)S(1)}, f32[2,128,128]{2,1,0:T(8,128)S(1)}, u32[]{:S(2)}, u32[]{:S(2)}) collective-permute-start(f32[2,128,128]{2,1,0:T(8,128)S(1)} %get-tuple-element.61), channel_id=1, source_target_pairs={{0,8},{16,24},{20,28},{1,9},{17,25},{21,29},{2,10},{18,26},{22,30}... | collective-permute-start | bytes 393224 | tf_op jit(solution)/shard_map/ppermute | solution.py:236
  56.3 1.3 %collective-permute-start.5 = (f32[2,128,128]{2,1,0:T(8,128)S(1)}, f32[2,128,128]{2,1,0:T(8,128)S(1)}, u32[]{:S(2)}, u32[]{:S(2)}) collective-permute-start(f32[2,128,128]{2,1,0:T(8,128)S(1)} %get-tuple-element.64), channel_id=1, source_target_pairs={{8,0},{16,8},{20,12},{9,1},{17,9},{21,13},{10,2},{18,10},{22,14},{... | collective-permute-start | bytes 393224 | tf_op jit(solution)/shard_map/ppermute | solution.py:237
  57.6 4.6 %collective-permute-start.3 = (f32[2,128,128]{2,1,0:T(8,128)S(1)}, f32[2,128,128]{2,1,0:T(8,128)S(1)}, u32[]{:S(2)}, u32[]{:S(2)}) collective-permute-start(f32[2,128,128]{2,1,0:T(8,128)S(1)} %get-tuple-element.65), channel_id=1, source_target_pairs={{0,8},{16,24},{20,28},{1,9},{17,25},{21,29},{2,10},{18,26},{22,30}... | collective-permute-start | bytes 393224 | tf_op jit(solution)/shard_map/ppermute | solution.py:236
  62.3 2.0 %collective-permute-start.14 = (f32[2,128,128]{2,1,0:T(8,128)S(1)}, f32[2,128,128]{2,1,0:T(8,128)S(1)}, u32[]{:S(2)}, u32[]{:S(2)}) collective-permute-start(f32[2,128,128]{2,1,0:T(8,128)S(1)} %get-tuple-element.45), channel_id=1, source_target_pairs={{0,4},{4,0},{8,12},{12,8},{16,20},{20,16},{24,28},{28,24},{1,5},{5... | collective-permute-start | bytes 393224 | tf_op jit(solution)/shard_map/ppermute | solution.py:208
  64.8 2.0 %collective-permute-start.6 = (f32[2,128,128]{2,1,0:T(8,128)S(1)}, f32[2,128,128]{2,1,0:T(8,128)S(1)}, u32[]{:S(2)}, u32[]{:S(2)}) collective-permute-start(f32[2,128,128]{2,1,0:T(8,128)S(1)} %get-tuple-element.47), channel_id=1, source_target_pairs={{0,4},{4,0},{8,12},{12,8},{16,20},{20,16},{24,28},{28,24},{1,5},{5... | collective-permute-start | bytes 393224 | tf_op jit(solution)/shard_map/ppermute | solution.py:208
  66.8 1.9 %collective-permute-done.15 = f32[2,128,128]{2,1,0:T(8,128)S(1)} collective-permute-done((f32[2,128,128]{2,1,0:T(8,128)S(1)}, f32[2,128,128]{2,1,0:T(8,128)S(1)}, u32[]{:S(2)}, u32[]{:S(2)}) %collective-permute-start.15) | collective-permute-done | bytes 131104 | tf_op jit(solution)/shard_map/ppermute | solution.py:208
  68.7 1.4 %collective-permute-done.14 = f32[2,128,128]{2,1,0:T(8,128)S(1)} collective-permute-done((f32[2,128,128]{2,1,0:T(8,128)S(1)}, f32[2,128,128]{2,1,0:T(8,128)S(1)}, u32[]{:S(2)}, u32[]{:S(2)}) %collective-permute-start.14) | collective-permute-done | bytes 131104 | tf_op jit(solution)/shard_map/ppermute | solution.py:208
  70.2 0.9 pad_maximum_fusion.2
  71.5 1.4 %collective-permute-done.6 = f32[2,128,128]{2,1,0:T(8,128)S(1)} collective-permute-done((f32[2,128,128]{2,1,0:T(8,128)S(1)}, f32[2,128,128]{2,1,0:T(8,128)S(1)}, u32[]{:S(2)}, u32[]{:S(2)}) %collective-permute-start.6) | collective-permute-done | bytes 131104 | tf_op jit(solution)/shard_map/ppermute | solution.py:208
  73.9 7.3 %final.2 = (bf16[768,1024]{1,0:T(8,128)(2,1)}, bf16[768,1024]{1,0:T(8,128)(2,1)}, bf16[768,1024]{1,0:T(8,128)(2,1)}, bf16[768,1024]{1,0:T(8,128)(2,1)}) custom-call(bf16[768,1024]{1,0:T(8,128)(2,1)} %q_ref.11, bf16[768,1024]{1,0:T(8,128)(2,1)} %k_ref.11, bf16[768,1024]{1,0:T(8,128)(2,1)} %v_ref.11, bf16[768,1024]{1,0:T(8,128)(2,1)} %g_ref.11, ...), custom_call_target="tpu_custom_call" | custom-call | tf_op jit(solution)/shard_map/final/pallas_call | solution.py:165
  81.2 7.4 %final.3 = (bf16[768,1024]{1,0:T(8,128)(2,1)}, bf16[768,1024]{1,0:T(8,128)(2,1)}, bf16[768,1024]{1,0:T(8,128)(2,1)}, bf16[768,1024]{1,0:T(8,128)(2,1)}) custom-call(bf16[768,1024]{1,0:T(8,128)(2,1)} %q_ref.11, bf16[768,1024]{1,0:T(8,128)(2,1)} %k_ref.11, ...), custom_call_target="tpu_custom_call", output_to_operand_aliasing={{0}: (12, {}), {1}: (13, {}), {2}: (14, {}), {3}: (15, {})} | custom-call | tf_op jit(solution)/shard_map/final/pallas_call | solution.py:165
  (36 shorter events, 2.6 us)
Async XLA Ops:
  7.6 38.0 %collective-permute-start.8 = (f32[2,128,128]{2,1,0:T(8,128)S(1)}, f32[2,128,128]{2,1,0:T(8,128)S(1)}, u32[]{:S(2)}, u32[]{:S(2)}) collective-permute-start(f32[2,128,128]{2,1,0:T(8,128)S(1)} %get-tuple-element.52), channel_id=1, source_target_pairs={{0,4},{4,0},{8,12},{12,8},{16,20},{20,16},{24,28},{28,24},{1,5},{5... | collective-permute-start | bytes 393224 | tf_op jit(solution)/shard_map/ppermute | solution.py:208
  10.6 27.7 %collective-permute-start.9 = (f32[2,128,128]{2,1,0:T(8,128)S(1)}, f32[2,128,128]{2,1,0:T(8,128)S(1)}, u32[]{:S(2)}, u32[]{:S(2)}) collective-permute-start(f32[2,128,128]{2,1,0:T(8,128)S(1)} %get-tuple-element.53), channel_id=1, source_target_pairs={{0,4},{4,0},{8,12},{12,8},{16,20},{20,16},{24,28},{28,24},{1,5},{5... | collective-permute-start | bytes 393224 | tf_op jit(solution)/shard_map/ppermute | solution.py:208
  17.3 38.8 %collective-permute-start = (f32[2,128,128]{2,1,0:T(8,128)S(1)}, f32[2,128,128]{2,1,0:T(8,128)S(1)}, u32[]{:S(2)}, u32[]{:S(2)}) collective-permute-start(f32[2,128,128]{2,1,0:T(8,128)S(1)} %get-tuple-element.58), channel_id=1, source_target_pairs={{0,4},{4,0},{8,12},{12,8},{16,20},{20,16},{24,28},{28,24},{1,5},{5... | collective-permute-start | bytes 393224 | tf_op jit(solution)/shard_map/ppermute | solution.py:208
  19.3 24.9 %collective-permute-start.1 = (f32[2,128,128]{2,1,0:T(8,128)S(1)}, f32[2,128,128]{2,1,0:T(8,128)S(1)}, u32[]{:S(2)}, u32[]{:S(2)}) collective-permute-start(f32[2,128,128]{2,1,0:T(8,128)S(1)} %get-tuple-element.59), channel_id=1, source_target_pairs={{0,4},{4,0},{8,12},{12,8},{16,20},{20,16},{24,28},{28,24},{1,5},{5... | collective-permute-start | bytes 393224 | tf_op jit(solution)/shard_map/ppermute | solution.py:208
  28.8 9.5 %copy-start.4 = (s32[16]{0:T(128)S(1)}, s32[16]{0:T(128)}, u32[]{:S(2)}) copy-start(s32[16]{0:T(128)} %lengths.3) | copy-start | bytes 196
  28.8 9.5 %copy-start.1 = (f32[4,128,128]{2,1,0:T(8,128)S(1)}, f32[4,128,128]{2,1,0:T(8,128)}, u32[]{:S(2)}) copy-start(f32[4,128,128]{2,1,0:T(8,128)} %get-tuple-element.34) | copy-start | bytes 786436
  28.8 9.5 %copy-start.3 = (f32[4,128,128]{2,1,0:T(8,128)S(1)}, f32[4,128,128]{2,1,0:T(8,128)}, u32[]{:S(2)}) copy-start(f32[4,128,128]{2,1,0:T(8,128)} %get-tuple-element.35) | copy-start | bytes 786436
  28.8 15.4 %copy-start = (f32[4,128,128]{2,1,0:T(8,128)S(1)}, f32[4,128,128]{2,1,0:T(8,128)}, u32[]{:S(2)}) copy-start(f32[4,128,128]{2,1,0:T(8,128)} %get-tuple-element.28) | copy-start | bytes 786436
  28.8 15.4 %copy-start.2 = (f32[4,128,128]{2,1,0:T(8,128)S(1)}, f32[4,128,128]{2,1,0:T(8,128)}, u32[]{:S(2)}) copy-start(f32[4,128,128]{2,1,0:T(8,128)} %get-tuple-element.29) | copy-start | bytes 786436
  38.4 11.8 %collective-permute-start.12 = (f32[2,128,128]{2,1,0:T(8,128)S(1)}, f32[2,128,128]{2,1,0:T(8,128)S(1)}, u32[]{:S(2)}, u32[]{:S(2)}) collective-permute-start(f32[2,128,128]{2,1,0:T(8,128)S(1)} %get-tuple-element.62), channel_id=1, source_target_pairs={{8,0},{24,16},{28,20},{9,1},{25,17},{29,21},{10,2},{26,18},{30,22}... | collective-permute-start | bytes 393224 | tf_op jit(solution)/shard_map/ppermute | solution.py:226
  39.7 10.5 %collective-permute-start.10 = (f32[2,128,128]{2,1,0:T(8,128)S(1)}, f32[2,128,128]{2,1,0:T(8,128)S(1)}, u32[]{:S(2)}, u32[]{:S(2)}) collective-permute-start(f32[2,128,128]{2,1,0:T(8,128)S(1)} %get-tuple-element.63), channel_id=1, source_target_pairs={{0,8},{8,16},{12,20},{1,9},{9,17},{13,21},{2,10},{10,18},{14,22},{... | collective-permute-start | bytes 393224 | tf_op jit(solution)/shard_map/ppermute | solution.py:225
  44.3 11.8 %collective-permute-start.4 = (f32[2,128,128]{2,1,0:T(8,128)S(1)}, f32[2,128,128]{2,1,0:T(8,128)S(1)}, u32[]{:S(2)}, u32[]{:S(2)}) collective-permute-start(f32[2,128,128]{2,1,0:T(8,128)S(1)} %get-tuple-element.66), channel_id=1, source_target_pairs={{8,0},{24,16},{28,20},{9,1},{25,17},{29,21},{10,2},{26,18},{30,22}... | collective-permute-start | bytes 393224 | tf_op jit(solution)/shard_map/ppermute | solution.py:226
  45.6 10.5 %collective-permute-start.2 = (f32[2,128,128]{2,1,0:T(8,128)S(1)}, f32[2,128,128]{2,1,0:T(8,128)S(1)}, u32[]{:S(2)}, u32[]{:S(2)}) collective-permute-start(f32[2,128,128]{2,1,0:T(8,128)S(1)} %get-tuple-element.67), channel_id=1, source_target_pairs={{0,8},{8,16},{12,20},{1,9},{9,17},{13,21},{2,10},{10,18},{14,22},{... | collective-permute-start | bytes 393224 | tf_op jit(solution)/shard_map/ppermute | solution.py:225
  50.3 11.8 %collective-permute-start.13 = (f32[2,128,128]{2,1,0:T(8,128)S(1)}, f32[2,128,128]{2,1,0:T(8,128)S(1)}, u32[]{:S(2)}, u32[]{:S(2)}) collective-permute-start(f32[2,128,128]{2,1,0:T(8,128)S(1)} %get-tuple-element.60), channel_id=1, source_target_pairs={{8,0},{16,8},{20,12},{9,1},{17,9},{21,13},{10,2},{18,10},{22,14},{... | collective-permute-start | bytes 393224 | tf_op jit(solution)/shard_map/ppermute | solution.py:237
  51.6 10.5 %collective-permute-start.11 = (f32[2,128,128]{2,1,0:T(8,128)S(1)}, f32[2,128,128]{2,1,0:T(8,128)S(1)}, u32[]{:S(2)}, u32[]{:S(2)}) collective-permute-start(f32[2,128,128]{2,1,0:T(8,128)S(1)} %get-tuple-element.61), channel_id=1, source_target_pairs={{0,8},{16,24},{20,28},{1,9},{17,25},{21,29},{2,10},{18,26},{22,30}... | collective-permute-start | bytes 393224 | tf_op jit(solution)/shard_map/ppermute | solution.py:236
  56.3 8.1 %collective-permute-start.5 = (f32[2,128,128]{2,1,0:T(8,128)S(1)}, f32[2,128,128]{2,1,0:T(8,128)S(1)}, u32[]{:S(2)}, u32[]{:S(2)}) collective-permute-start(f32[2,128,128]{2,1,0:T(8,128)S(1)} %get-tuple-element.64), channel_id=1, source_target_pairs={{8,0},{16,8},{20,12},{9,1},{17,9},{21,13},{10,2},{18,10},{22,14},{... | collective-permute-start | bytes 393224 | tf_op jit(solution)/shard_map/ppermute | solution.py:237
  57.6 7.1 %collective-permute-start.3 = (f32[2,128,128]{2,1,0:T(8,128)S(1)}, f32[2,128,128]{2,1,0:T(8,128)S(1)}, u32[]{:S(2)}, u32[]{:S(2)}) collective-permute-start(f32[2,128,128]{2,1,0:T(8,128)S(1)} %get-tuple-element.65), channel_id=1, source_target_pairs={{0,8},{16,24},{20,28},{1,9},{17,25},{21,29},{2,10},{18,26},{22,30}... | collective-permute-start | bytes 393224 | tf_op jit(solution)/shard_map/ppermute | solution.py:236
  62.2 6.4 %collective-permute-start.15 = (f32[2,128,128]{2,1,0:T(8,128)S(1)}, f32[2,128,128]{2,1,0:T(8,128)S(1)}, u32[]{:S(2)}, u32[]{:S(2)}) collective-permute-start(f32[2,128,128]{2,1,0:T(8,128)S(1)} %get-tuple-element.44), channel_id=1, source_target_pairs={{0,4},{4,0},{8,12},{12,8},{16,20},{20,16},{24,28},{28,24},{1,5},{5... | collective-permute-start | bytes 393224 | tf_op jit(solution)/shard_map/ppermute | solution.py:208
  62.3 7.8 %collective-permute-start.14 = (f32[2,128,128]{2,1,0:T(8,128)S(1)}, f32[2,128,128]{2,1,0:T(8,128)S(1)}, u32[]{:S(2)}, u32[]{:S(2)}) collective-permute-start(f32[2,128,128]{2,1,0:T(8,128)S(1)} %get-tuple-element.45), channel_id=1, source_target_pairs={{0,4},{4,0},{8,12},{12,8},{16,20},{20,16},{24,28},{28,24},{1,5},{5... | collective-permute-start | bytes 393224 | tf_op jit(solution)/shard_map/ppermute | solution.py:208
  64.7 6.8 %collective-permute-start.7 = (f32[2,128,128]{2,1,0:T(8,128)S(1)}, f32[2,128,128]{2,1,0:T(8,128)S(1)}, u32[]{:S(2)}, u32[]{:S(2)}) collective-permute-start(f32[2,128,128]{2,1,0:T(8,128)S(1)} %get-tuple-element.46), channel_id=1, source_target_pairs={{0,4},{4,0},{8,12},{12,8},{16,20},{20,16},{24,28},{28,24},{1,5},{5... | collective-permute-start | bytes 393224 | tf_op jit(solution)/shard_map/ppermute | solution.py:208
  64.8 8.1 %collective-permute-start.6 = (f32[2,128,128]{2,1,0:T(8,128)S(1)}, f32[2,128,128]{2,1,0:T(8,128)S(1)}, u32[]{:S(2)}, u32[]{:S(2)}) collective-permute-start(f32[2,128,128]{2,1,0:T(8,128)S(1)} %get-tuple-element.47), channel_id=1, source_target_pairs={{0,4},{4,0},{8,12},{12,8},{16,20},{20,16},{24,28},{28,24},{1,5},{5... | collective-permute-start | bytes 393224 | tf_op jit(solution)/shard_map/ppermute | solution.py:208

commit v2 on v0

v2 whole, which is shorter than its diff:
```python
import functools

import jax
import jax.numpy as jnp
from jax import lax
from jax.experimental import pallas as pl
from jax.experimental.pallas import tpu as pltpu
from jax.sharding import PartitionSpec as P

DH = 128
ROWS = 256
VMEM_LIMIT = 24 << 20
F32 = jnp.float32
LOW = jnp.bfloat16

NT = (((1,), (1,)), ((), ()))
TN = (((0,), (0,)), ((), ()))
NN = (((1,), (0,)), ((), ()))


def dot(a, b, dims):
    return lax.dot_general(a, b, dims, preferred_element_type=F32)


def split(a):
    high = a.astype(LOW)
    return high, (a - high.astype(F32)).astype(LOW)


def write_layout(lengths, offset, scale_ref, first_ref):
    count = scale_ref.shape[0]
    tiles = count // DH
    shape = (tiles, DH)
    row = lax.broadcasted_iota(jnp.int32, shape, 0) * DH + lax.broadcasted_iota(jnp.int32, shape, 1) + offset
    first = jnp.zeros(shape, jnp.int32)
    start = jnp.int32(0)
    for j in range(lengths.shape[0]):
        first = jnp.where(row >= start, start, first)
        start = start + lengths[j]
    scale = 1.0 / jnp.sqrt((row - first + 1).astype(F32) * DH)
    first = (first - offset).astype(F32)
    for t in range(tiles):
        rows = slice(t * DH, (t + 1) * DH)
        scale_ref[rows] = jnp.broadcast_to(scale[t : t + 1], (DH, DH)).T
        first_ref[rows] = jnp.broadcast_to(first[t : t + 1], (DH, DH)).T


def row_index(rows, base):
    return (lax.broadcasted_iota(jnp.int32, (rows, DH), 0) + base).astype(F32)


def key_values(k, v, first_ref, base, rows):
    start = first_ref[base + rows - 1 : base + rows]
    tail = jnp.where(row_index(rows, base) >= start, k, jnp.zeros((), LOW))
    return dot(tail, v, TN)


def query_grads(q, g, scale_ref, first_ref, base, rows):
    span = slice(base, base + rows)
    scaled = jnp.where(first_ref[span] < base, scale_ref[span] * g.astype(F32), 0.0)
    both = dot(q, jnp.concatenate(split(scaled), axis=1), TN)
    return both[:, :DH] + both[:, DH:]


def first_kernel(lengths, q_ref, k_ref, v_ref, g_ref, send_ref, scale_ref, first_ref):
    count = q_ref.shape[0]
    place = lax.axis_index("seq")

    @pl.when(pl.program_id(0) == 0)
    def _():
        write_layout(lengths, place * count, scale_ref, first_ref)

    @pl.when(place < 6)
    def _():
        send_ref[0] = key_values(k_ref[...], v_ref[...], first_ref, 0, count)

    @pl.when(place >= 6)
    def _():
        send_ref[0] = query_grads(q_ref[...], g_ref[...], scale_ref, first_ref, 0, count)


def goes_on(first_ref, base):
    return jnp.where(first_ref[base + ROWS - 1 : base + ROWS] < base, 1.0, 0.0)


def states_kernel(make_layout, lengths, q_ref, k_ref, v_ref, g_ref, *refs):
    count = q_ref.shape[0]
    if make_layout:
        kv_ref, qg_ref, inner_kv_ref, inner_qg_ref, scale_ref, first_ref = refs

        @pl.when(pl.program_id(0) == 0)
        def _():
            write_layout(lengths, lax.axis_index("seq") * count, scale_ref, first_ref)
    else:
        scale_ref, first_ref, kv_ref, qg_ref, inner_kv_ref, inner_qg_ref = refs
    bases = range(0, count, ROWS)
    total = None
    for c, base in enumerate(bases):
        span = slice(base, base + ROWS)
        part = key_values(k_ref[span], v_ref[span], first_ref, base, ROWS)
        total = part if total is None else total * goes_on(first_ref, base) + part
        if c < len(bases) - 1:
            inner_kv_ref[0, c] = total
    kv_ref[0] = total
    total = None
    for c, base in reversed(list(enumerate(bases))):
        span = slice(base, base + ROWS)
        part = query_grads(q_ref[span], g_ref[span], scale_ref, first_ref, base, ROWS)
        total = part if total is None else total * goes_on(first_ref, base) + part
        if c:
            inner_qg_ref[0, c - 1] = total
    qg_ref[0] = total


def local_kernel(q_ref, k_ref, v_ref, g_ref, scale_ref, first_ref, a_ref, dq_ref, dk_ref, dv_ref):
    count = q_ref.shape[0]
    many = ROWS // DH
    row = lax.broadcasted_iota(jnp.int32, (ROWS, ROWS), 0)
    col = lax.broadcasted_iota(jnp.int32, (ROWS, ROWS), 1)
    causal = col <= row
    col = col.astype(F32)
    for base in range(0, count, ROWS):
        rows = slice(base, base + ROWS)
        q, g, k, v = q_ref[rows], g_ref[rows], k_ref[rows], v_ref[rows]
        scale = scale_ref[rows]
        start = jnp.concatenate([first_ref[rows] - base] * many, axis=1)
        scale_w = jnp.concatenate([scale] * many, axis=1)
        mask = (col >= start) & causal
        scores = jnp.where(mask, dot(q, k, NT), 0.0).astype(LOW)
        grads = jnp.where(mask, dot(g, v, NT) * scale_w, 0.0).astype(LOW)
        scaled = (scale * g.astype(F32)).astype(LOW)
        a_ref[rows] = scale * dot(scores, v, NN)
        dq_ref[rows] = dot(grads, k, NN)
        dk_ref[rows] = dot(grads, q, TN)
        dv_ref[rows] = dot(scores, scaled, TN)


def final_kernel(
    q_ref, k_ref, v_ref, g_ref, a_ref, dq_ref, dk_ref, dv_ref, kv_ref, qg_ref, inner_kv_ref, inner_qg_ref,
    scale_ref, first_ref, *refs
):
    out_a, out_q, out_k, out_v = refs[-4:]
    count = q_ref.shape[0]
    bases = list(range(0, count, ROWS))

    def carried(rows, state, axis):
        both = jnp.concatenate(split(state), axis=axis)
        return dot(jnp.concatenate([rows, rows], axis=1), both, NT if axis else NN)

    kv_in = kv_ref[0]
    qg_in = qg_ref[0]
    keep = None
    for c, base in enumerate(bases):
        rows = slice(base, base + ROWS)
        if c == 0:
            state = kv_in
        else:
            went = goes_on(first_ref, bases[c - 1])
            keep = went if keep is None else keep * went
            state = kv_in * keep + inner_kv_ref[0, c - 1]
        scale = jnp.where(first_ref[rows] < base, scale_ref[rows], 0.0)
        out_a[rows] = (a_ref[rows] + scale * carried(q_ref[rows], state, 0)).astype(LOW)
        out_q[rows] = (dq_ref[rows] + scale * carried(g_ref[rows], state, 1)).astype(LOW)
    keep = None
    for c, base in reversed(list(enumerate(bases))):
        rows = slice(base, base + ROWS)
        if base == bases[-1]:
            state = qg_in
        else:
            went = goes_on(first_ref, bases[c + 1])
            keep = went if keep is None else keep * went
            state = qg_in * keep + inner_qg_ref[0, c]
        tail = row_index(ROWS, base) >= first_ref[base + ROWS - 1 : base + ROWS]
        out_k[rows] = (dk_ref[rows] + jnp.where(tail, carried(v_ref[rows], state, 1), 0.0)).astype(LOW)
        out_v[rows] = (dv_ref[rows] + jnp.where(tail, carried(k_ref[rows], state, 0), 0.0)).astype(LOW)


def head_block(count, base=None):
    return pl.BlockSpec((count, DH), lambda i, *_: (0, i if base is None else base() + i))


def whole(count):
    return pl.BlockSpec((count, DH), lambda i, *_: (0, 0))


def state_block(base=None):
    return pl.BlockSpec((1, DH, DH), lambda i, *_: (i if base is None else base() + i, 0, 0))


def inner_block(chunks, base=None):
    return pl.BlockSpec((1, chunks - 1, DH, DH), lambda i, *_: (i if base is None else base() + i, 0, 0, 0))


PARAMS = pltpu.CompilerParams(vmem_limit_bytes=VMEM_LIMIT)


def layout_shapes(count):
    return [jax.ShapeDtypeStruct((count, DH), F32)] * 2


def first_send(arrays, lengths, heads, base):
    count = arrays[0].shape[0]
    send, *layout = pl.pallas_call(
        first_kernel,
        out_shape=[jax.ShapeDtypeStruct((heads, DH, DH), F32)] + layout_shapes(count),
        grid_spec=pltpu.PrefetchScalarGridSpec(
            num_scalar_prefetch=1,
            grid=(heads,),
            in_specs=[head_block(count, base)] * 4,
            out_specs=[state_block()] + [whole(count)] * 2,
        ),
        compiler_params=PARAMS,
        name="first",
    )(lengths, *arrays)
    return send, tuple(layout)


def states(arrays, lengths, layout):
    count, width = arrays[0].shape
    heads = width // DH
    chunks = count // ROWS
    inner = jax.ShapeDtypeStruct((heads, chunks - 1, DH, DH), F32)
    out_shape = [jax.ShapeDtypeStruct((heads, DH, DH), F32)] * 2 + [inner] * 2
    out_specs = [state_block()] * 2 + [inner_block(chunks)] * 2
    in_specs = [head_block(count)] * 4
    if layout is None:
        out_shape += layout_shapes(count)
        out_specs += [whole(count)] * 2
    else:
        in_specs += [whole(count)] * 2
    return pl.pallas_call(
        functools.partial(states_kernel, layout is None),
        out_shape=out_shape,
        grid_spec=pltpu.PrefetchScalarGridSpec(
            num_scalar_prefetch=1, grid=(heads,), in_specs=in_specs, out_specs=out_specs
        ),
        compiler_params=PARAMS,
        name="states",
    )(lengths, *arrays, *(layout or ()))


def local(arrays, layout, heads, base):
    count = arrays[0].shape[0]
    shape = jax.ShapeDtypeStruct((count, heads * DH), F32)
    return pl.pallas_call(
        local_kernel,
        out_shape=[shape] * 4,
        grid=(heads,),
        in_specs=[head_block(count, base)] * 4 + [whole(count)] * 2,
        out_specs=[head_block(count)] * 4,
        compiler_params=PARAMS,
        name="local",
    )(*arrays, *layout)


def final(arrays, parts, kv, qg, inner, layout, base, outs):
    count, width = arrays[0].shape
    heads = kv.shape[0]
    chunks = count // ROWS
    shape = jax.ShapeDtypeStruct((count, width), LOW)
    extra = tuple(outs or ())
    return pl.pallas_call(
        final_kernel,
        out_shape=[shape] * 4,
        grid=(heads,),
        in_specs=[head_block(count, base)] * 4
        + [head_block(count)] * 4
        + [state_block()] * 2
        + [inner_block(chunks, base)] * 2
        + [whole(count)] * 2
        + [pl.BlockSpec(memory_space=pl.ANY)] * len(extra),
        out_specs=[head_block(count, base)] * 4,
        input_output_aliases={14 + i: i for i in range(len(extra))},
        compiler_params=PARAMS,
        name="final",
    )(*arrays, *parts, kv, qg, *inner, *layout, *extra)


PAIRS = [(d, d ^ 1) for d in range(8)]
UP_1 = [(0, 2), (2, 4), (3, 5)]
UP_2 = [(0, 2), (4, 6), (5, 7)]
DOWN_1 = [(2, 0), (6, 4), (7, 5)]
DOWN_2 = [(2, 0), (4, 2), (5, 3)]


def choose(place, default, *cases):
    value = default
    for devices, other in cases:
        hit = functools.reduce(jnp.logical_or, [place == d for d in devices])
        value = jnp.where(hit, other, value)
    return value


def permute(value, pairs):
    return lax.ppermute(value, "seq", pairs)


def on_eight(arrays, lengths):
    count, width = arrays[0].shape
    half = width // DH // 2
    d = lax.axis_index("seq")
    link = jnp.where(lengths[0] >= 2 * count, 1.0, 0.0)
    odd = d % 2 == 1

    def own():
        return lax.rem(lax.axis_index("seq"), 2) * half

    def other():
        return half - own()

    def given():
        place = lax.axis_index("seq")
        return jnp.where(place < 2, 0, half - lax.rem(place, 2) * half)

    send, layout = first_send(arrays, lengths, half, given)
    x0 = permute(send, PAIRS)
    kv, qg, *inner = states(arrays, lengths, layout)
    x0, kv, qg = lax.optimization_barrier((x0, kv, qg))
    k, q = (kv[:half], kv[half:]), (qg[:half], qg[half:])
    mine_k = jnp.where(odd, k[1], k[0])
    mine_q = jnp.where(odd, q[1], q[0])

    sum_k = mine_k + x0
    up = choose(d, sum_k, ((0,), x0 + link * k[0]))
    down = choose(d, mine_q + x0, ((2,), q[1]))
    up1 = permute(up, UP_1)
    down1 = permute(down, DOWN_1)
    send = choose(
        d, jnp.where(odd, q[0], q[1]), ((0, 1, 6), k[1]), ((2,), k[0]), ((3,), q[0]), ((7,), q[1])
    )
    x1 = permute(send, PAIRS)
    x0, *local_layout = lax.optimization_barrier((x0, *layout))
    own_parts = local(arrays, local_layout, half, own)
    up1, down1, x1, *own_parts = lax.optimization_barrier((up1, down1, x1, *own_parts))

    up = choose(d, up1 + sum_k, ((0,), x1 + link * k[1]))
    down = choose(d, down1 + mine_q + x1, ((2,), q[0]))
    up2 = permute(up, UP_2)
    down2 = permute(down, DOWN_2)
    send = choose(d, up1, ((0,), down1), ((1,), q[0]), ((4,), up1 + k[0]))
    x2 = permute(send, PAIRS)
    up1, *local_layout = lax.optimization_barrier((up1, *layout))
    other_parts = local(arrays, local_layout, half, other)
    up2, down2, x2, *other_parts = lax.optimization_barrier((up2, down2, x2, *other_parts))

    send = choose(
        d,
        down1,
        ((0, 2), down2),
        ((1,), q[1]),
        ((3,), down2 + q[1]),
        ((5,), down1 + q[1]),
        ((6,), up2 + k[0]),
        ((7,), up2),
    )
    x3 = permute(send, PAIRS)
    zero = jnp.zeros_like(x0)
    kv_own = choose(
        d, up1, ((0,), zero), ((1,), x1), ((3,), x0), ((5,), up1 + x0), ((6,), up2), ((7,), up2 + x1)
    )
    qg_own = choose(
        d,
        x0,
        ((0,), x2 + link * down2),
        ((1,), x2),
        ((2,), x1 + down2),
        ((3,), down2),
        ((4,), x1 + down1),
        ((5,), down1),
        ((7,), zero),
    )
    outs = final(arrays, own_parts, kv_own, qg_own, inner, layout, own, None)
    kv_other = choose(d, x3, ((0,), zero), ((1,), x0), ((2,), up2), ((3,), x1), ((4, 5), x2))
    qg_other = choose(d, x3, ((0,), x3 + link * down1), ((6,), x1), ((7,), zero))
    return tuple(final(arrays, other_parts, kv_other, qg_other, inner, layout, other, outs))


def on_any(arrays, lengths):
    count, width = arrays[0].shape
    heads = width // DH
    kv, qg, inner_kv, inner_qg, *layout = states(arrays, lengths, None)
    parts = local(arrays, layout, heads, None)
    starts_here = (layout[1][count - 1, 0] >= 0).astype(F32)
    kv_all, qg_all, start_all = lax.all_gather((kv, qg, starts_here), "seq")
    place = lax.axis_index("seq")
    devices = lax.axis_size("seq")
    order = jnp.arange(devices)
    last_start = jnp.max(jnp.where((order < place) & (start_all > 0.5), order, 0))
    next_start = jnp.min(jnp.where((order > place) & (start_all > 0.5), order, devices))

    def total(pick, values):
        return jnp.sum(jnp.where(pick[:, None, None, None], values, 0.0), axis=0)

    before = total((order < place) & (order >= last_start), kv_all)
    after = total((order > place) & (order <= next_start), qg_all)
    return tuple(final(arrays, parts, before, after, (inner_kv, inner_qg), layout, None, None))


def per_device(query_rows, key_rows, value_rows, grad_out, doc_lengths):
    arrays = (query_rows, key_rows, value_rows, grad_out)
    if lax.axis_size("seq") == 8:
        return on_eight(arrays, doc_lengths)
    return on_any(arrays, doc_lengths)


def solution(mesh):
    placed = P("seq", "head")
    return jax.shard_map(
        per_device,
        mesh=mesh,
        in_specs=(placed, placed, placed, placed, P()),
        out_specs=(placed, placed, placed, placed),
        check_vma=False,
    )
```

time: 233 us -> 104 us (0.45)
  the two profiles are of different devices: /device:TPU:26 before, /device:TPU:0 now
where the time goes in v2:
time: 104 us; the launch traced here: 103 us
  local copies, waits for them, and re-layouts  37.3 us (36%)
  Pallas kernels  33 us (32%)
  starting transfers between devices  15.9 us (15%)
  other arithmetic  8.88 us (9%)
  waiting for transfers between devices  6.98 us (7%)
    unnamed x94, local copies, waits for them, and re-layouts  37.3 us
    ppermute x8, starting transfers between devices, permute(): return lax.ppermute(value, 'seq', pairs)  15.9 us
    pallas_call x2, Pallas kernels, local(): pl.pallas_call(local_kernel, out_shape=[shape] * 4, grid=(heads,), in_spe...  13.5 us
    pallas_call x2, Pallas kernels, final(): pl.pallas_call(final_kernel, out_shape=[shape] * 4, grid=(heads,), in_spe...  10.6 us
    select_n x4, other arithmetic, choose(): value = jnp.where(hit, other, value)  8.88 us
    ppermute x8, waiting for transfers between devices, permute(): return lax.ppermute(value, 'seq', pairs)  6.98 us
    pallas_call x1, Pallas kernels, states(): pl.pallas_call(functools.partial(states_kernel, layout is None), out_shap...  5.02 us
    pallas_call x1, Pallas kernels, first_send(): pl.pallas_call(first_kernel, out_shape=[jax.ShapeDtypeStruct((heads, DH,...  3.83 us
  transfers between devices with their start and end apart: 8, of which 1 were waited for; matrix products, arithmetic and copies ran while one was open for 0% of the time, Pallas kernels for 18%

profile of v2, /device:TPU:0, one launch (start us, length us, event | category | flops | bytes accessed | tf_op | source)
XLA Modules:
  0.0 103.1 jit_solution(4219068587745209996)
XLA Ops:
  2.0 1.4 %copy-done.2 = bf16[768,1024]{1,0:T(8,128)(2,1)S(1)} copy-done((bf16[768,1024]{1,0:T(8,128)(2,1)S(1)}, bf16[768,1024]{1,0:T(8,128)(2,1)}, u32[]{:S(2)}) %copy-start.2) | copy-done | bytes 1572888
  3.5 1.4 %copy-done.4 = bf16[768,1024]{1,0:T(8,128)(2,1)S(1)} copy-done((bf16[768,1024]{1,0:T(8,128)(2,1)S(1)}, bf16[768,1024]{1,0:T(8,128)(2,1)}, u32[]{:S(2)}) %copy-start.4) | copy-done | bytes 1572888
  4.9 1.4 %copy-done.9 = bf16[768,1024]{1,0:T(8,128)(2,1)S(1)} copy-done((bf16[768,1024]{1,0:T(8,128)(2,1)S(1)}, bf16[768,1024]{1,0:T(8,128)(2,1)}, u32[]{:S(2)}) %copy-start.9) | copy-done | bytes 1572888
  6.9 3.8 %first.1 = (f32[4,128,128]{2,1,0:T(8,128)}, f32[768,128]{1,0:T(8,128)S(1)}, f32[768,128]{1,0:T(8,128)S(1)}) custom-call(s32[16]{0:T(128)S(1)} %copy-done.45, bf16[768,1024]{1,0:T(8,128)(2,1)S(1)} %copy-done, bf16[768,1024]{1,0:T(8,128)(2,1)S(1)} %copy-done.2, bf16[768,1024]{1,0:T(8,128)(2,1)S(1)} %copy-done.4, bf16[768,1024]{1,0:T(8,128)(2,1)S(1)} %copy-done.9), custom_call_target="tpu_custom_call" | custom-call | tf_op jit(solution)/shard_map/first/pallas_call | solution.py:203
  11.5 3.0 %collective-permute-start = (f32[4,128,128]{2,1,0:T(8,128)}, f32[4,128,128]{2,1,0:T(8,128)}, u32[]{:S(2)}, u32[]{:S(2)}) collective-permute-start(f32[4,128,128]{2,1,0:T(8,128)} %get-tuple-element.46), channel_id=1, source_target_pairs={{0,4},{4,0},{8,12},{12,8},{16,20},{20,16},{24,28},{28,24},{1,5},{5... | collective-permute-start | bytes 786440 | tf_op jit(solution)/shard_map/ppermute | solution.py:295
  16.0 1.4 %copy-done.10 = bf16[768,1024]{1,0:T(8,128)(2,1)S(1)} copy-done((bf16[768,1024]{1,0:T(8,128)(2,1)S(1)}, bf16[768,1024]{1,0:T(8,128)(2,1)}, u32[]{:S(2)}) %copy-start.10) | copy-done | bytes 1572888
  18.4 5.0 %states.1 = (f32[8,128,128]{2,1,0:T(8,128)S(1)}, f32[8,128,128]{2,1,0:T(8,128)S(1)}, f32[8,2,128,128]{3,2,1,0:T(8,128)S(1)}, f32[8,2,128,128]{3,2,1,0:T(8,128)S(1)}) custom-call(s32[16]{0:T(128)S(1)} %copy-done.46, bf16[768,1024]{1,0:T(8,128)(2,1)S(1)} %copy-done.1, bf16[768,1024]{1,0:T(8,128)(2,1)S(1)} %copy-done.3, bf16[768,1024]{1,0:T(8,128)(2,1)S(1)} %copy-done.5, ...), custom_call_target="tpu_custom_call" | custom-call | tf_op jit(solution)/shard_map/states/pallas_call | solution.py:231
  26.3 1.9 %select_select_fusion.5 = (f32[4,128,128]{2,1,0:T(8,128)}, f32[4,128,128]{2,1,0:T(8,128)}, f32[4,128,128]{2,1,0:T(8,128)}) fusion(f32[8,128,128]{2,1,0:T(8,128)S(1)} %get-tuple-element.52, f32[8,128,128]{2,1,0:T(8,128)S(1)} %get-tuple-element.53, pred[]{:T(512)S(6)} %or.13, pred[]{:T(512)S(6)} %eq.24, pred[]{:T(512)S(6)} %eq.23, pred[]{:T(512)S(6)} %eq.22, ...), kind=kLoop, calls=%fused_computation.10 | loop fusion | flops 851968 | bytes 2097162 | tf_op jit(solution)/shard_map/jit(_where)/select_n | solution.py:290
  29.5 6.0 %collective-permute-start.1 = (f32[4,128,128]{2,1,0:T(8,128)}, f32[4,128,128]{2,1,0:T(8,128)}, u32[]{:S(2)}, u32[]{:S(2)}) collective-permute-start(f32[4,128,128]{2,1,0:T(8,128)} %get-tuple-element.97), channel_id=1, source_target_pairs={{0,8},{8,16},{12,20},{1,9},{9,17},{13,21},{2,10},{10,18},{14,22},{... | collective-permute-start | bytes 786440 | tf_op jit(solution)/shard_map/ppermute | solution.py:295
  35.4 1.4 %copy-done.6 = bf16[768,1024]{1,0:T(8,128)(2,1)S(1)} copy-done((bf16[768,1024]{1,0:T(8,128)(2,1)S(1)}, bf16[768,1024]{1,0:T(8,128)(2,1)}, u32[]{:S(2)}) %copy-start.6) | copy-done | bytes 1572888
  36.9 1.4 %copy-done.11 = bf16[768,1024]{1,0:T(8,128)(2,1)S(1)} copy-done((bf16[768,1024]{1,0:T(8,128)(2,1)S(1)}, bf16[768,1024]{1,0:T(8,128)(2,1)}, u32[]{:S(2)}) %copy-start.11) | copy-done | bytes 1572888
  39.3 6.7 %local.2 = (f32[768,512]{1,0:T(8,128)S(1)}, f32[768,512]{1,0:T(8,128)S(1)}, f32[768,512]{1,0:T(8,128)S(1)}, f32[768,512]{1,0:T(8,128)S(1)}) custom-call(bf16[768,1024]{1,0:T(8,128)(2,1)S(1)} %copy-done.1, bf16[768,1024]{1,0:T(8,128)(2,1)S(1)} %copy-done.3, bf16[768,1024]{1,0:T(8,128)(2,1)S(1)} %copy-done.6, bf16[768,1024]{1,0:T(8,128)(2,1)S(1)} %copy-done.11, ...), custom_call_target="tpu_custom_call" | custom-call | tf_op jit(solution)/shard_map/local/pallas_call | solution.py:245
  49.5 2.8 %select_select_fusion.4 = (f32[4,128,128]{2,1,0:T(8,128)}, f32[4,128,128]{2,1,0:T(8,128)}, f32[4,128,128]{2,1,0:T(8,128)}) fusion(f32[4,128,128]{2,1,0:T(8,128)} %collective-permute-done.2, f32[4,128,128]{2,1,0:T(8,128)} %collective-permute-done.1, f32[8,128,128]{2,1,0:T(8,128)S(1)} %copy-done.27, f32[8,128,128]{2,1,0:T(8,128)S(1)} %copy-done.24, ...), kind=kLoop, calls=%fused_computation.7 | loop fusion | flops 917504 | bytes 2883593 | tf_op jit(solution)/shard_map/jit(_where)/select_n | solution.py:290
  52.3 4.4 %collective-permute-start.4 = (f32[4,128,128]{2,1,0:T(8,128)}, f32[4,128,128]{2,1,0:T(8,128)}, u32[]{:S(2)}, u32[]{:S(2)}) collective-permute-start(f32[4,128,128]{2,1,0:T(8,128)} %get-tuple-element.93), channel_id=1, source_target_pairs={{0,8},{16,24},{20,28},{1,9},{17,25},{21,29},{2,10},{18,26},{22,30}... | collective-permute-start | bytes 786440 | tf_op jit(solution)/shard_map/ppermute | solution.py:295
  59.4 1.4 %copy-done.12 = bf16[768,1024]{1,0:T(8,128)(2,1)S(1)} copy-done((bf16[768,1024]{1,0:T(8,128)(2,1)S(1)}, bf16[768,1024]{1,0:T(8,128)(2,1)}, u32[]{:S(2)}) %copy-start.12) | copy-done | bytes 1572888
  61.8 6.8 %local.3 = (f32[768,512]{1,0:T(8,128)S(1)}, f32[768,512]{1,0:T(8,128)S(1)}, f32[768,512]{1,0:T(8,128)S(1)}, f32[768,512]{1,0:T(8,128)S(1)}) custom-call(bf16[768,1024]{1,0:T(8,128)(2,1)S(1)} %copy-done.1, bf16[768,1024]{1,0:T(8,128)(2,1)S(1)} %copy-done.3, bf16[768,1024]{1,0:T(8,128)(2,1)S(1)} %copy-done.7, bf16[768,1024]{1,0:T(8,128)(2,1)S(1)} %copy-done.12, ...), custom_call_target="tpu_custom_call" | custom-call | tf_op jit(solution)/shard_map/local/pallas_call | solution.py:245
  72.1 2.4 %select_select_fusion.3 = f32[4,128,128]{2,1,0:T(8,128)} fusion(f32[4,128,128]{2,1,0:T(8,128)} %collective-permute-done.4, f32[4,128,128]{2,1,0:T(8,128)} %collective-permute-done.5, f32[4,128,128]{2,1,0:T(8,128)} %collective-permute-done.2, f32[8,128,128]{2,1,0:T(8,128)S(1)} %copy-done.28, f32[8,128,128]{2,1,0:T(8,128)S(1)} %copy-done.25, pred[]{:T(512)S(6)} %or.15, ...), kind=kLoop, calls=%fused_computation.6 | loop fusion | flops 589824 | bytes 1572870 | tf_op jit(solution)/shard_map/jit(_where)/select_n | solution.py:290
  74.6 7.0 %collective-permute-done.7 = f32[4,128,128]{2,1,0:T(8,128)} collective-permute-done((f32[4,128,128]{2,1,0:T(8,128)}, f32[4,128,128]{2,1,0:T(8,128)}, u32[]{:S(2)}, u32[]{:S(2)}) %collective-permute-start.7) | collective-permute-done | bytes 262176 | tf_op jit(solution)/shard_map/ppermute | solution.py:295
  81.5 1.8 %select_select_fusion = (f32[4,128,128]{2,1,0:T(8,128)S(1)}, f32[4,128,128]{2,1,0:T(8,128)S(1)}, f32[4,128,128]{2,1,0:T(8,128)S(1)}, f32[4,128,128]{2,1,0:T(8,128)S(1)}) fusion(f32[4,128,128]{2,1,0:T(8,128)} %collective-permute-done.2, f32[4,128,128]{2,1,0:T(8,128)} %collective-permute-done.5, f32[4,128,128]{2,1,0:T(8,128)} %collective-permute-done.6, ...), kind=kLoop, calls=%fused_computation.3 | loop fusion | flops 1900544 | bytes 3145741 | tf_op jit(solution)/shard_map/jit(_where)/select_n | solution.py:290
  88.2 1.4 %copy-done.32 = f32[768,512]{1,0:T(8,128)S(1)} copy-done((f32[768,512]{1,0:T(8,128)S(1)}, f32[768,512]{1,0:T(8,128)}, u32[]{:S(2)}) %copy-start.32) | copy-done | bytes 1572888
  89.6 1.4 %copy-done.34 = f32[768,512]{1,0:T(8,128)S(1)} copy-done((f32[768,512]{1,0:T(8,128)S(1)}, f32[768,512]{1,0:T(8,128)}, u32[]{:S(2)}) %copy-start.34) | copy-done | bytes 1572888
  91.0 1.4 %copy-done.36 = f32[768,512]{1,0:T(8,128)S(1)} copy-done((f32[768,512]{1,0:T(8,128)S(1)}, f32[768,512]{1,0:T(8,128)}, u32[]{:S(2)}) %copy-start.36) | copy-done | bytes 1572888
  92.4 5.3 %final.2 = (bf16[768,1024]{1,0:T(8,128)(2,1)}, bf16[768,1024]{1,0:T(8,128)(2,1)}, bf16[768,1024]{1,0:T(8,128)(2,1)}, bf16[768,1024]{1,0:T(8,128)(2,1)}) custom-call(bf16[768,1024]{1,0:T(8,128)(2,1)S(1)} %copy-done.1, bf16[768,1024]{1,0:T(8,128)(2,1)S(1)} %copy-done.3, bf16[768,1024]{1,0:T(8,128)(2,1)S(1)} %copy-done.8, bf16[768,1024]{1,0:T(8,128)(2,1)S(1)} %copy-done.13, ...), custom_call_target="tpu_custom_call" | custom-call | tf_op jit(solution)/shard_map/final/pallas_call | solution.py:262
  97.7 5.3 %final.3 = (bf16[768,1024]{1,0:T(8,128)(2,1)}, bf16[768,1024]{1,0:T(8,128)(2,1)}, bf16[768,1024]{1,0:T(8,128)(2,1)}, bf16[768,1024]{1,0:T(8,128)(2,1)}) custom-call(bf16[768,1024]{1,0:T(8,128)(2,1)S(1)} %copy-done.1, bf16[768,1024]{1,0:T(8,128)(2,1)S(1)} %copy-done.3, ...), custom_call_target="tpu_custom_call", output_to_operand_aliasing={{0}: (14, {}), {1}: (15, {}), {2}: (16, {}), {3}: (17, {})} | custom-call | tf_op jit(solution)/shard_map/final/pallas_call | solution.py:262
  (96 shorter events, 25.9 us)
Async XLA Ops:
  6.9 7.6 %copy-start.46 = (s32[16]{0:T(128)S(1)}, s32[16]{0:T(128)}, u32[]{:S(2)}) copy-start(s32[16]{0:T(128)} %lengths.3) | copy-start | bytes 196
  6.9 7.6 %copy-start.1 = (bf16[768,1024]{1,0:T(8,128)(2,1)S(1)}, bf16[768,1024]{1,0:T(8,128)(2,1)}, u32[]{:S(2)}) copy-start(bf16[768,1024]{1,0:T(8,128)(2,1)} %q_ref.11) | copy-start | bytes 4718596
  6.9 7.6 %copy-start.3 = (bf16[768,1024]{1,0:T(8,128)(2,1)S(1)}, bf16[768,1024]{1,0:T(8,128)(2,1)}, u32[]{:S(2)}) copy-start(bf16[768,1024]{1,0:T(8,128)(2,1)} %k_ref.11) | copy-start | bytes 4718596
  11.5 13.9 %collective-permute-start = (f32[4,128,128]{2,1,0:T(8,128)}, f32[4,128,128]{2,1,0:T(8,128)}, u32[]{:S(2)}, u32[]{:S(2)}) collective-permute-start(f32[4,128,128]{2,1,0:T(8,128)} %get-tuple-element.46), channel_id=1, source_target_pairs={{0,4},{4,0},{8,12},{12,8},{16,20},{20,16},{24,28},{28,24},{1,5},{5... | collective-permute-start | bytes 786440 | tf_op jit(solution)/shard_map/ppermute | solution.py:295
  25.5 2.7 %copy-start.26 = (f32[8,128,128]{2,1,0:T(8,128)}, f32[8,128,128]{2,1,0:T(8,128)S(1)}, u32[]{:S(2)}) copy-start(f32[8,128,128]{2,1,0:T(8,128)S(1)} %get-tuple-element.53) | copy-start | bytes 1572868
  28.2 21.3 %collective-permute-start.3 = (f32[4,128,128]{2,1,0:T(8,128)}, f32[4,128,128]{2,1,0:T(8,128)}, u32[]{:S(2)}, u32[]{:S(2)}) collective-permute-start(f32[4,128,128]{2,1,0:T(8,128)} %get-tuple-element.95), channel_id=1, source_target_pairs={{0,4},{4,0},{8,12},{12,8},{16,20},{20,16},{24,28},{28,24},{1,5},{5... | collective-permute-start | bytes 786440 | tf_op jit(solution)/shard_map/ppermute | solution.py:295
  28.2 21.3 %collective-permute-start.2 = (f32[4,128,128]{2,1,0:T(8,128)}, f32[4,128,128]{2,1,0:T(8,128)}, u32[]{:S(2)}, u32[]{:S(2)}) collective-permute-start(f32[4,128,128]{2,1,0:T(8,128)} %get-tuple-element.96), channel_id=1, source_target_pairs={{8,0},{24,16},{28,20},{9,1},{25,17},{29,21},{10,2},{26,18},{30,22}... | collective-permute-start | bytes 786440 | tf_op jit(solution)/shard_map/ppermute | solution.py:295
  29.5 20.0 %collective-permute-start.1 = (f32[4,128,128]{2,1,0:T(8,128)}, f32[4,128,128]{2,1,0:T(8,128)}, u32[]{:S(2)}, u32[]{:S(2)}) collective-permute-start(f32[4,128,128]{2,1,0:T(8,128)} %get-tuple-element.97), channel_id=1, source_target_pairs={{0,8},{8,16},{12,20},{1,9},{9,17},{13,21},{2,10},{10,18},{14,22},{... | collective-permute-start | bytes 786440 | tf_op jit(solution)/shard_map/ppermute | solution.py:295
  39.3 10.2 %copy-start.24 = (f32[8,128,128]{2,1,0:T(8,128)S(1)}, f32[8,128,128]{2,1,0:T(8,128)}, u32[]{:S(2)}) copy-start(f32[8,128,128]{2,1,0:T(8,128)} %copy-done.23) | copy-start | bytes 1572868
  39.3 10.2 %copy-start.27 = (f32[8,128,128]{2,1,0:T(8,128)S(1)}, f32[8,128,128]{2,1,0:T(8,128)}, u32[]{:S(2)}) copy-start(f32[8,128,128]{2,1,0:T(8,128)} %copy-done.26) | copy-start | bytes 1572868
  49.4 2.8 %copy-start.29 = (f32[768,512]{1,0:T(8,128)}, f32[768,512]{1,0:T(8,128)S(1)}, u32[]{:S(2)}) copy-start(f32[768,512]{1,0:T(8,128)S(1)} %get-tuple-element.79.a_ref) | copy-start | bytes 4718596
  52.3 19.8 %collective-permute-start.6 = (f32[4,128,128]{2,1,0:T(8,128)}, f32[4,128,128]{2,1,0:T(8,128)}, u32[]{:S(2)}, u32[]{:S(2)}) collective-permute-start(f32[4,128,128]{2,1,0:T(8,128)} %get-tuple-element.92), channel_id=1, source_target_pairs={{0,4},{4,0},{8,12},{12,8},{16,20},{20,16},{24,28},{28,24},{1,5},{5... | collective-permute-start | bytes 786440 | tf_op jit(solution)/shard_map/ppermute | solution.py:295
  52.3 19.8 %collective-permute-start.4 = (f32[4,128,128]{2,1,0:T(8,128)}, f32[4,128,128]{2,1,0:T(8,128)}, u32[]{:S(2)}, u32[]{:S(2)}) collective-permute-start(f32[4,128,128]{2,1,0:T(8,128)} %get-tuple-element.93), channel_id=1, source_target_pairs={{0,8},{16,24},{20,28},{1,9},{17,25},{21,29},{2,10},{18,26},{22,30}... | collective-permute-start | bytes 786440 | tf_op jit(solution)/shard_map/ppermute | solution.py:295
  56.7 15.4 %collective-permute-start.5 = (f32[4,128,128]{2,1,0:T(8,128)}, f32[4,128,128]{2,1,0:T(8,128)}, u32[]{:S(2)}, u32[]{:S(2)}) collective-permute-start(f32[4,128,128]{2,1,0:T(8,128)} %get-tuple-element.94), channel_id=1, source_target_pairs={{8,0},{16,8},{20,12},{9,1},{17,9},{21,13},{10,2},{18,10},{22,14},{... | collective-permute-start | bytes 786440 | tf_op jit(solution)/shard_map/ppermute | solution.py:295
  61.8 10.3 %copy-start.25 = (f32[8,128,128]{2,1,0:T(8,128)S(1)}, f32[8,128,128]{2,1,0:T(8,128)}, u32[]{:S(2)}) copy-start(f32[8,128,128]{2,1,0:T(8,128)} %copy-done.23) | copy-start | bytes 1572868
  61.8 10.3 %copy-start.28 = (f32[8,128,128]{2,1,0:T(8,128)S(1)}, f32[8,128,128]{2,1,0:T(8,128)}, u32[]{:S(2)}) copy-start(f32[8,128,128]{2,1,0:T(8,128)} %copy-done.26) | copy-start | bytes 1572868
  72.1 2.5 %copy-start.37 = (f32[768,512]{1,0:T(8,128)}, f32[768,512]{1,0:T(8,128)S(1)}, u32[]{:S(2)}) copy-start(f32[768,512]{1,0:T(8,128)S(1)} %get-tuple-element.69.a_ref) | copy-start | bytes 4718596
  74.6 7.0 %collective-permute-start.7 = (f32[4,128,128]{2,1,0:T(8,128)}, f32[4,128,128]{2,1,0:T(8,128)}, u32[]{:S(2)}, u32[]{:S(2)}) collective-permute-start(f32[4,128,128]{2,1,0:T(8,128)} %select_select_fusion.3), channel_id=1, source_target_pairs={{0,4},{4,0},{8,12},{12,8},{16,20},{20,16},{24,28},{28,24},{1,5},{5... | collective-permute-start | bytes 786440 | tf_op jit(solution)/shard_map/ppermute | solution.py:295
  74.6 8.7 %copy-start.8 = (bf16[768,1024]{1,0:T(8,128)(2,1)S(1)}, bf16[768,1024]{1,0:T(8,128)(2,1)}, u32[]{:S(2)}) copy-start(bf16[768,1024]{1,0:T(8,128)(2,1)} %v_ref.11) | copy-start | bytes 4718596
  74.6 8.7 %copy-start.13 = (bf16[768,1024]{1,0:T(8,128)(2,1)S(1)}, bf16[768,1024]{1,0:T(8,128)(2,1)}, u32[]{:S(2)}) copy-start(bf16[768,1024]{1,0:T(8,128)(2,1)} %g_ref.11) | copy-start | bytes 4718596
  92.4 5.3 %copy-start.38 = (f32[768,512]{1,0:T(8,128)S(1)}, f32[768,512]{1,0:T(8,128)}, u32[]{:S(2)}) copy-start(f32[768,512]{1,0:T(8,128)} %copy-done.37) | copy-start | bytes 4718596
  92.4 5.3 %copy-start.40 = (f32[768,512]{1,0:T(8,128)S(1)}, f32[768,512]{1,0:T(8,128)}, u32[]{:S(2)}) copy-start(f32[768,512]{1,0:T(8,128)} %copy-done.39) | copy-start | bytes 4718596
  92.4 5.3 %copy-start.42 = (f32[768,512]{1,0:T(8,128)S(1)}, f32[768,512]{1,0:T(8,128)}, u32[]{:S(2)}) copy-start(f32[768,512]{1,0:T(8,128)} %copy-done.41) | copy-start | bytes 4718596
  92.4 5.3 %copy-start.44 = (f32[768,512]{1,0:T(8,128)S(1)}, f32[768,512]{1,0:T(8,128)}, u32[]{:S(2)}) copy-start(f32[768,512]{1,0:T(8,128)} %copy-done.43) | copy-start | bytes 4718596
  (31 other events, 37.3 us)

commit v3 on v2

--- a/solution.py
+++ b/solution.py
@@ -9,7 +9,6 @@
 
 DH = 128
 ROWS = 256
-VMEM_LIMIT = 24 << 20
 F32 = jnp.float32
 LOW = jnp.bfloat16
 
@@ -49,90 +48,104 @@
     return (lax.broadcasted_iota(jnp.int32, (rows, DH), 0) + base).astype(F32)
 
 
-def key_values(k, v, first_ref, base, rows):
-    start = first_ref[base + rows - 1 : base + rows]
-    tail = jnp.where(row_index(rows, base) >= start, k, jnp.zeros((), LOW))
+def key_values(k, v, start, base):
+    tail = jnp.where(row_index(k.shape[0], base) >= start, k, jnp.zeros((), LOW))
     return dot(tail, v, TN)
 
 
-def query_grads(q, g, scale_ref, first_ref, base, rows):
-    span = slice(base, base + rows)
-    scaled = jnp.where(first_ref[span] < base, scale_ref[span] * g.astype(F32), 0.0)
+def query_grads(q, g, scale, first, base):
+    scaled = jnp.where(first < base, scale * g.astype(F32), 0.0)
     both = dot(q, jnp.concatenate(split(scaled), axis=1), TN)
     return both[:, :DH] + both[:, DH:]
 
 
+def columns(h):
+    return slice(h * DH, (h + 1) * DH)
+
+
 def first_kernel(lengths, q_ref, k_ref, v_ref, g_ref, send_ref, scale_ref, first_ref):
-    count = q_ref.shape[0]
+    count = scale_ref.shape[0]
     place = lax.axis_index("seq")
-
-    @pl.when(pl.program_id(0) == 0)
+    step = pl.program_id(0)
+    base = pl.multiple_of(step * ROWS, ROWS)
+    span = pl.ds(base, ROWS)
+
+    @pl.when(step == 0)
     def _():
         write_layout(lengths, place * count, scale_ref, first_ref)
+        send_ref[...] = jnp.zeros_like(send_ref)
 
     @pl.when(place < 6)
     def _():
-        send_ref[0] = key_values(k_ref[...], v_ref[...], first_ref, 0, count)
+        start = first_ref[count - 1 : count]
+        for h in range(send_ref.shape[0]):
+            cols = columns(h)
+            send_ref[h] += key_values(k_ref[:, cols], v_ref[:, cols], start, base)
 
     @pl.when(place >= 6)
     def _():
-        send_ref[0] = query_grads(q_ref[...], g_ref[...], scale_ref, first_ref, 0, count)
-
-
-def goes_on(first_ref, base):
-    return jnp.where(first_ref[base + ROWS - 1 : base + ROWS] < base, 1.0, 0.0)
+        for h in range(send_ref.shape[0]):
+            cols = columns(h)
+            send_ref[h] += query_grads(q_ref[:, cols], g_ref[:, cols], scale_ref[span], first_ref[span], 0.0)
 
 
 def states_kernel(make_layout, lengths, q_ref, k_ref, v_ref, g_ref, *refs):
-    count = q_ref.shape[0]
+    step = pl.program_id(0)
+    last = pl.num_programs(0) - 1
     if make_layout:
         kv_ref, qg_ref, inner_kv_ref, inner_qg_ref, scale_ref, first_ref = refs
-
-        @pl.when(pl.program_id(0) == 0)
+        count = scale_ref.shape[0]
+
+        @pl.when(step == 0)
         def _():
             write_layout(lengths, lax.axis_index("seq") * count, scale_ref, first_ref)
     else:
         scale_ref, first_ref, kv_ref, qg_ref, inner_kv_ref, inner_qg_ref = refs
-    bases = range(0, count, ROWS)
-    total = None
-    for c, base in enumerate(bases):
-        span = slice(base, base + ROWS)
-        part = key_values(k_ref[span], v_ref[span], first_ref, base, ROWS)
-        total = part if total is None else total * goes_on(first_ref, base) + part
-        if c < len(bases) - 1:
-            inner_kv_ref[0, c] = total
-    kv_ref[0] = total
-    total = None
-    for c, base in reversed(list(enumerate(bases))):
-        span = slice(base, base + ROWS)
-        part = query_grads(q_ref[span], g_ref[span], scale_ref, first_ref, base, ROWS)
-        total = part if total is None else total * goes_on(first_ref, base) + part
-        if c:
-            inner_qg_ref[0, c - 1] = total
-    qg_ref[0] = total
+
+    @pl.when(step == 0)
+    def _():
+        kv_ref[...] = jnp.zeros_like(kv_ref)
+        qg_ref[...] = jnp.zeros_like(qg_ref)
+
+    down = pl.multiple_of(step * ROWS, ROWS)
+    start = first_ref[pl.ds(down + ROWS - 1, 1)]
+    keep = jnp.where(start < down.astype(F32), 1.0, 0.0)
+    up = pl.multiple_of((last - step) * ROWS, ROWS)
+    up_f = up.astype(F32)
+    up_keep = jnp.where(first_ref[pl.ds(up + ROWS - 1, 1)] < up_f, 1.0, 0.0)
+    scale, first = scale_ref[pl.ds(up, ROWS)], first_ref[pl.ds(up, ROWS)]
+    for h in range(kv_ref.shape[0]):
+        cols = columns(h)
+        kv_ref[h] = kv_ref[h] * keep + key_values(k_ref[:, cols], v_ref[:, cols], start, down)
+        qg_ref[h] = qg_ref[h] * up_keep + query_grads(q_ref[:, cols], g_ref[:, cols], scale, first, up_f)
+
+    @pl.when(step < last)
+    def _():
+        inner_kv_ref[0] = kv_ref[...]
+        inner_qg_ref[0] = qg_ref[...]
 
 
 def local_kernel(q_ref, k_ref, v_ref, g_ref, scale_ref, first_ref, a_ref, dq_ref, dk_ref, dv_ref):
-    count = q_ref.shape[0]
     many = ROWS // DH
+    base = (pl.program_id(0) * ROWS).astype(F32)
     row = lax.broadcasted_iota(jnp.int32, (ROWS, ROWS), 0)
     col = lax.broadcasted_iota(jnp.int32, (ROWS, ROWS), 1)
     causal = col <= row
     col = col.astype(F32)
-    for base in range(0, count, ROWS):
-        rows = slice(base, base + ROWS)
-        q, g, k, v = q_ref[rows], g_ref[rows], k_ref[rows], v_ref[rows]
-        scale = scale_ref[rows]
-        start = jnp.concatenate([first_ref[rows] - base] * many, axis=1)
+    for h in range(a_ref.shape[1] // DH):
+        cols = columns(h)
+        q, g, k, v = q_ref[:, cols], g_ref[:, cols], k_ref[:, cols], v_ref[:, cols]
+        scale = scale_ref[...]
+        start = jnp.concatenate([first_ref[...] - base] * many, axis=1)
         scale_w = jnp.concatenate([scale] * many, axis=1)
         mask = (col >= start) & causal
         scores = jnp.where(mask, dot(q, k, NT), 0.0).astype(LOW)
         grads = jnp.where(mask, dot(g, v, NT) * scale_w, 0.0).astype(LOW)
         scaled = (scale * g.astype(F32)).astype(LOW)
-        a_ref[rows] = scale * dot(scores, v, NN)
-        dq_ref[rows] = dot(grads, k, NN)
-        dk_ref[rows] = dot(grads, q, TN)
-        dv_ref[rows] = dot(scores, scaled, TN)
+        a_ref[:, cols] = scale * dot(scores, v, NN)
+        dq_ref[:, cols] = dot(grads, k, NN)
+        dk_ref[:, cols] = dot(grads, q, TN)
+        dv_ref[:, cols] = dot(scores, scaled, TN)
 
 
 def final_kernel(
@@ -140,76 +153,74 @@
     scale_ref, first_ref, *refs
 ):
     out_a, out_q, out_k, out_v = refs[-4:]
-    count = q_ref.shape[0]
-    bases = list(range(0, count, ROWS))
+    count = scale_ref.shape[0]
+    step = pl.program_id(0)
+    last = pl.num_programs(0) - 1
+    base = pl.multiple_of(step * ROWS, ROWS)
+    base_f = base.astype(F32)
+    span = pl.ds(base, ROWS)
 
     def carried(rows, state, axis):
         both = jnp.concatenate(split(state), axis=axis)
         return dot(jnp.concatenate([rows, rows], axis=1), both, NT if axis else NN)
 
-    kv_in = kv_ref[0]
-    qg_in = qg_ref[0]
-    keep = None
-    for c, base in enumerate(bases):
-        rows = slice(base, base + ROWS)
-        if c == 0:
-            state = kv_in
-        else:
-            went = goes_on(first_ref, bases[c - 1])
-            keep = went if keep is None else keep * went
-            state = kv_in * keep + inner_kv_ref[0, c - 1]
-        scale = jnp.where(first_ref[rows] < base, scale_ref[rows], 0.0)
-        out_a[rows] = (a_ref[rows] + scale * carried(q_ref[rows], state, 0)).astype(LOW)
-        out_q[rows] = (dq_ref[rows] + scale * carried(g_ref[rows], state, 1)).astype(LOW)
-    keep = None
-    for c, base in reversed(list(enumerate(bases))):
-        rows = slice(base, base + ROWS)
-        if base == bases[-1]:
-            state = qg_in
-        else:
-            went = goes_on(first_ref, bases[c + 1])
-            keep = went if keep is None else keep * went
-            state = qg_in * keep + inner_qg_ref[0, c]
-        tail = row_index(ROWS, base) >= first_ref[base + ROWS - 1 : base + ROWS]
-        out_k[rows] = (dk_ref[rows] + jnp.where(tail, carried(v_ref[rows], state, 1), 0.0)).astype(LOW)
-        out_v[rows] = (dv_ref[rows] + jnp.where(tail, carried(k_ref[rows], state, 0), 0.0)).astype(LOW)
-
-
-def head_block(count, base=None):
-    return pl.BlockSpec((count, DH), lambda i, *_: (0, i if base is None else base() + i))
+    first = first_ref[span]
+    scale = jnp.where(first < base_f, scale_ref[span], 0.0)
+    tail = row_index(ROWS, base) >= first_ref[pl.ds(base + ROWS - 1, 1)]
+    before = jnp.where(step > 0, 1.0, 0.0)
+    after = jnp.where(step < last, 1.0, 0.0)
+    whole_start = first_ref[pl.ds(jnp.maximum(base - 1, 0), 1)]
+    kv_keep = jnp.where((whole_start < 0) | (step == 0), 1.0, 0.0)
+    qg_keep = jnp.where(first_ref[count - 1 : count] < base_f + ROWS, 1.0, 0.0)
+    for h in range(kv_ref.shape[0]):
+        cols = columns(h)
+        kv = kv_ref[h] * kv_keep + inner_kv_ref[0, h] * before
+        qg = qg_ref[h] * qg_keep + inner_qg_ref[0, h] * after
+        out_a[:, cols] = (a_ref[:, cols] + scale * carried(q_ref[:, cols], kv, 0)).astype(LOW)
+        out_q[:, cols] = (dq_ref[:, cols] + scale * carried(g_ref[:, cols], kv, 1)).astype(LOW)
+        out_k[:, cols] = (dk_ref[:, cols] + jnp.where(tail, carried(v_ref[:, cols], qg, 1), 0.0)).astype(LOW)
+        out_v[:, cols] = (dv_ref[:, cols] + jnp.where(tail, carried(k_ref[:, cols], qg, 0), 0.0)).astype(LOW)
+
+
+def at(part):
+    return 0 if part is None else part()
+
+
+def row_block(width, part=None, flip=None):
+    return pl.BlockSpec((ROWS, width), lambda i, *_: (i if flip is None else flip - i, at(part)))
+
+
+def layout_block():
+    return pl.BlockSpec((ROWS, DH), lambda i, *_: (i, 0))
 
 
 def whole(count):
     return pl.BlockSpec((count, DH), lambda i, *_: (0, 0))
 
 
-def state_block(base=None):
-    return pl.BlockSpec((1, DH, DH), lambda i, *_: (i if base is None else base() + i, 0, 0))
-
-
-def inner_block(chunks, base=None):
-    return pl.BlockSpec((1, chunks - 1, DH, DH), lambda i, *_: (i if base is None else base() + i, 0, 0, 0))
-
-
-PARAMS = pltpu.CompilerParams(vmem_limit_bytes=VMEM_LIMIT)
+def state_block(heads):
+    return pl.BlockSpec((heads, DH, DH), lambda i, *_: (0, 0, 0))
+
+
+def inner_block(heads, place, part=None):
+    return pl.BlockSpec((1, heads, DH, DH), lambda i, *_: (place(i), at(part), 0, 0))
 
 
 def layout_shapes(count):
     return [jax.ShapeDtypeStruct((count, DH), F32)] * 2
 
 
-def first_send(arrays, lengths, heads, base):
+def first_send(arrays, lengths, heads, part):
     count = arrays[0].shape[0]
     send, *layout = pl.pallas_call(
         first_kernel,
         out_shape=[jax.ShapeDtypeStruct((heads, DH, DH), F32)] + layout_shapes(count),
         grid_spec=pltpu.PrefetchScalarGridSpec(
             num_scalar_prefetch=1,
-            grid=(heads,),
-            in_specs=[head_block(count, base)] * 4,
-            out_specs=[state_block()] + [whole(count)] * 2,
+            grid=(count // ROWS,),
+            in_specs=[row_block(heads * DH, part)] * 4,
+            out_specs=[state_block(heads)] + [whole(count)] * 2,
         ),
-        compiler_params=PARAMS,
         name="first",
     )(lengths, *arrays)
     return send, tuple(layout)
@@ -219,10 +230,14 @@
     count, width = arrays[0].shape
     heads = width // DH
     chunks = count // ROWS
-    inner = jax.ShapeDtypeStruct((heads, chunks - 1, DH, DH), F32)
+    inner = jax.ShapeDtypeStruct((chunks - 1, heads, DH, DH), F32)
     out_shape = [jax.ShapeDtypeStruct((heads, DH, DH), F32)] * 2 + [inner] * 2
-    out_specs = [state_block()] * 2 + [inner_block(chunks)] * 2
-    in_specs = [head_block(count)] * 4
+    out_specs = [state_block(heads)] * 2 + [
+        inner_block(heads, lambda i: jnp.minimum(i, chunks - 2)),
+        inner_block(heads, lambda i: jnp.maximum(chunks - 2 - i, 0)),
+    ]
+    back = row_block(width, None, chunks - 1)
+    in_specs = [back, row_block(width), row_block(width), back]
     if layout is None:
         out_shape += layout_shapes(count)
         out_specs += [whole(count)] * 2
@@ -232,28 +247,26 @@
         functools.partial(states_kernel, layout is None),
         out_shape=out_shape,
         grid_spec=pltpu.PrefetchScalarGridSpec(
-            num_scalar_prefetch=1, grid=(heads,), in_specs=in_specs, out_specs=out_specs
+            num_scalar_prefetch=1, grid=(chunks,), in_specs=in_specs, out_specs=out_specs
         ),
-        compiler_params=PARAMS,
         name="states",
     )(lengths, *arrays, *(layout or ()))
 
 
-def local(arrays, layout, heads, base):
+def local(arrays, layout, heads, part):
     count = arrays[0].shape[0]
     shape = jax.ShapeDtypeStruct((count, heads * DH), F32)
     return pl.pallas_call(
         local_kernel,
         out_shape=[shape] * 4,
-        grid=(heads,),
-        in_specs=[head_block(count, base)] * 4 + [whole(count)] * 2,
-        out_specs=[head_block(count)] * 4,
-        compiler_params=PARAMS,
+        grid=(count // ROWS,),
+        in_specs=[row_block(heads * DH, part)] * 4 + [layout_block()] * 2,
+        out_specs=[row_block(heads * DH)] * 4,
         name="local",
     )(*arrays, *layout)
 
 
-def final(arrays, parts, kv, qg, inner, layout, base, outs):
+def final(arrays, parts, kv, qg, inner, layout, part, outs):
     count, width = arrays[0].shape
     heads = kv.shape[0]
     chunks = count // ROWS
@@ -262,16 +275,18 @@
     return pl.pallas_call(
         final_kernel,
         out_shape=[shape] * 4,
-        grid=(heads,),
-        in_specs=[head_block(count, base)] * 4
-        + [head_block(count)] * 4
-        + [state_block()] * 2
-        + [inner_block(chunks, base)] * 2
+        grid=(chunks,),
+        in_specs=[row_block(heads * DH, part)] * 4
+        + [row_block(heads * DH)] * 4
+        + [state_block(heads)] * 2
+        + [
+            inner_block(heads, lambda i: jnp.maximum(i - 1, 0), part),
+            inner_block(heads, lambda i: jnp.minimum(i, chunks - 2), part),
+        ]
         + [whole(count)] * 2
         + [pl.BlockSpec(memory_space=pl.ANY)] * len(extra),
-        out_specs=[head_block(count, base)] * 4,
+        out_specs=[row_block(heads * DH, part)] * 4,
         input_output_aliases={14 + i: i for i in range(len(extra))},
-        compiler_params=PARAMS,
         name="final",
     )(*arrays, *parts, kv, qg, *inner, *layout, *extra)
 
@@ -303,14 +318,13 @@
     odd = d % 2 == 1
 
     def own():
-        return lax.rem(lax.axis_index("seq"), 2) * half
+        return lax.rem(lax.axis_index("seq"), 2)
 
     def other():
-        return half - own()
+        return 1 - own()
 
     def given():
-        place = lax.axis_index("seq")
-        return jnp.where(place < 2, 0, half - lax.rem(place, 2) * half)
+        return jnp.where(lax.axis_index("seq") < 2, 0, other())
 
     send, layout = first_send(arrays, lengths, half, given)
     x0 = permute(send, PAIRS)
@@ -370,6 +384,7 @@
         ((7,), zero),
     )
     outs = final(arrays, own_parts, kv_own, qg_own, inner, layout, own, None)
+    x3, *outs = lax.optimization_barrier((x3, *outs))
     kv_other = choose(d, x3, ((0,), zero), ((1,), x0), ((2,), up2), ((3,), x1), ((4, 5), x2))
     qg_other = choose(d, x3, ((0,), x3 + link * down1), ((6,), x1), ((7,), zero))
     return tuple(final(arrays, other_parts, kv_other, qg_other, inner, layout, other, outs))

time: 104 us -> 62.6 us (0.60)
  local copies, waits for them, and re-layouts: 37.3 us -> 0.02 us
  Pallas kernels: 33 us -> 42.4 us
  waiting for transfers between devices: 6.98 us -> 0.02 us
  other arithmetic: 8.88 us -> 4.1 us
  starting transfers between devices: 15.9 us -> 14.6 us
    unnamed x94 -> x6, local copies, waits for them, and re-layouts: 37.3 us -> 0.02 us
    ppermute x8, waiting for transfers between devices: 6.98 us -> 0.02 us  [permute(): return lax.ppermute(value, 'seq', pairs)]
    pallas_call x4, Pallas kernels: 24.1 us -> 29.9 us  [the longest x2 15 us: local(): pl.pallas_call(local_kernel, out_shape=[shape] * 4, grid=(count // ROWS,)...]
    select_n x4, other arithmetic: 8.88 us -> 4.1 us  [choose(): value = jnp.where(hit, other, value)]
    pallas_call x1, Pallas kernels: 5.02 us -> 7.41 us  [states(): pl.pallas_call(functools.partial(states_kernel, layout is None), out_shap...]
    ppermute x8, starting transfers between devices: 15.9 us -> 14.6 us  [permute(): return lax.ppermute(value, 'seq', pairs)]
    pallas_call x1, Pallas kernels: 3.83 us -> 5.03 us  [first_send(): pl.pallas_call(first_kernel, out_shape=[jax.ShapeDtypeStruct((heads, DH,...]
  transfers between devices with their start and end apart: 8 -> 8, of which waited for: 1 -> 0; matrix products, arithmetic and copies ran while one was open for 0% -> 0% of each run, Pallas kernels for 18% -> 48%
where the time goes in v3:
time: 62.6 us; the launch traced here: 62 us
  Pallas kernels  42.4 us (68%)
  starting transfers between devices  14.6 us (23%)
  other arithmetic  4.1 us (7%)
  between operations  0.82 us (1%)
    pallas_call x2, Pallas kernels, local(): pl.pallas_call(local_kernel, out_shape=[shape] * 4, grid=(count // ROWS,)...  15 us
    pallas_call x2, Pallas kernels, final(): pl.pallas_call(final_kernel, out_shape=[shape] * 4, grid=(chunks,), in_sp...  14.9 us
    ppermute x8, starting transfers between devices, permute(): return lax.ppermute(value, 'seq', pairs)  14.6 us
    pallas_call x1, Pallas kernels, states(): pl.pallas_call(functools.partial(states_kernel, layout is None), out_shap...  7.41 us
    pallas_call x1, Pallas kernels, first_send(): pl.pallas_call(first_kernel, out_shape=[jax.ShapeDtypeStruct((heads, DH,...  5.03 us
    select_n x4, other arithmetic, choose(): value = jnp.where(hit, other, value)  4.1 us
  transfers between devices with their start and end apart: 8, of which 0 were waited for; matrix products, arithmetic and copies ran while one was open for 0% of the time, Pallas kernels for 48%

profile of v3, /device:TPU:0, one launch (start us, length us, event | category | flops | bytes accessed | tf_op | source)
XLA Modules:
  0.0 62.0 jit_solution(7865610072168775607)
XLA Ops:
  0.6 0.0 copy-start.2
  0.6 5.0 %first.1 = (f32[4,128,128]{2,1,0:T(8,128)}, f32[768,128]{1,0:T(8,128)}, f32[768,128]{1,0:T(8,128)}) custom-call(s32[16]{0:T(128)} %lengths.3, bf16[768,1024]{1,0:T(8,128)(2,1)} %q_ref.11, bf16[768,1024]{1,0:T(8,128)(2,1)} %k_ref.11, bf16[768,1024]{1,0:T(8,128)(2,1)} %v_ref.11, bf16[768,1024]{1,0:T(8,128)(2,1)} %g_ref.11), custom_call_target="tpu_custom_call" | custom-call | tf_op jit(solution)/shard_map/first/pallas_call | solution.py:215
  5.7 3.0 %collective-permute-start = (f32[4,128,128]{2,1,0:T(8,128)}, f32[4,128,128]{2,1,0:T(8,128)S(1)}, u32[]{:S(2)}, u32[]{:S(2)}) collective-permute-start(f32[4,128,128]{2,1,0:T(8,128)} %get-tuple-element.51), channel_id=1, source_target_pairs={{0,4},{4,0},{8,12},{12,8},{16,20},{20,16},{24,28},{28,24},{1,5},{5... | collective-permute-start | bytes 786440 | tf_op jit(solution)/shard_map/ppermute | solution.py:310
  8.7 7.4 %states.1 = (f32[8,128,128]{2,1,0:T(8,128)}, f32[8,128,128]{2,1,0:T(8,128)}, f32[2,8,128,128]{3,2,1,0:T(8,128)}, f32[2,8,128,128]{3,2,1,0:T(8,128)}) custom-call(s32[16]{0:T(128)} %lengths.3, bf16[768,1024]{1,0:T(8,128)(2,1)} %q_ref.11, bf16[768,1024]{1,0:T(8,128)(2,1)} %k_ref.11, bf16[768,1024]{1,0:T(8,128)(2,1)} %v_ref.11, bf16[768,1024]{1,0:T(8,128)(2,1)} %g_ref.11, ...), custom_call_target="tpu_custom_call" | custom-call | tf_op jit(solution)/shard_map/states/pallas_call | solution.py:246
  16.1 0.0 collective-permute-done
  16.1 1.3 %select_select_fusion.5 = (f32[4,128,128]{2,1,0:T(8,128)S(1)}, f32[4,128,128]{2,1,0:T(8,128)S(1)}, f32[4,128,128]{2,1,0:T(8,128)S(1)}) fusion(f32[8,128,128]{2,1,0:T(8,128)} %get-tuple-element.57, f32[8,128,128]{2,1,0:T(8,128)} %get-tuple-element.58, pred[]{:T(512)S(6)} %or.13, pred[]{:T(512)S(6)} %eq.24, pred[]{:T(512)S(6)} %eq.23, pred[]{:T(512)S(6)} %eq.22, ...), kind=kLoop, calls=%fused_computation.10 | loop fusion | flops 851968 | bytes 2097162 | tf_op jit(solution)/shard_map/jit(_where)/select_n | solution.py:305
  17.4 0.8 %collective-permute-start.3 = (f32[4,128,128]{2,1,0:T(8,128)S(1)}, f32[4,128,128]{2,1,0:T(8,128)S(1)}, u32[]{:S(2)}, u32[]{:S(2)}) collective-permute-start(f32[4,128,128]{2,1,0:T(8,128)S(1)} %get-tuple-element.106), channel_id=1, source_target_pairs={{0,4},{4,0},{8,12},{12,8},{16,20},{20,16},{24,28},{28,24},{1,5},{5... | collective-permute-start | bytes 786440 | tf_op jit(solution)/shard_map/ppermute | solution.py:310
  18.3 1.3 %collective-permute-start.2 = (f32[4,128,128]{2,1,0:T(8,128)S(1)}, f32[4,128,128]{2,1,0:T(8,128)S(1)}, u32[]{:S(2)}, u32[]{:S(2)}) collective-permute-start(f32[4,128,128]{2,1,0:T(8,128)S(1)} %get-tuple-element.107), channel_id=1, source_target_pairs={{8,0},{24,16},{28,20},{9,1},{25,17},{29,21},{10,2},{26,18},{30,22}... | collective-permute-start | bytes 786440 | tf_op jit(solution)/shard_map/ppermute | solution.py:310
  19.6 4.6 %collective-permute-start.1 = (f32[4,128,128]{2,1,0:T(8,128)S(1)}, f32[4,128,128]{2,1,0:T(8,128)S(1)}, u32[]{:S(2)}, u32[]{:S(2)}) collective-permute-start(f32[4,128,128]{2,1,0:T(8,128)S(1)} %get-tuple-element.108), channel_id=1, source_target_pairs={{0,8},{8,16},{12,20},{1,9},{9,17},{13,21},{2,10},{10,18},{14,22},{... | collective-permute-start | bytes 786440 | tf_op jit(solution)/shard_map/ppermute | solution.py:310
  24.2 0.0 copy-start
  24.2 0.0 copy-start.1
  24.2 7.6 %local.2 = (f32[768,512]{1,0:T(8,128)}, f32[768,512]{1,0:T(8,128)}, f32[768,512]{1,0:T(8,128)}, f32[768,512]{1,0:T(8,128)}) custom-call(bf16[768,1024]{1,0:T(8,128)(2,1)} %q_ref.11, bf16[768,1024]{1,0:T(8,128)(2,1)} %k_ref.11, bf16[768,1024]{1,0:T(8,128)(2,1)} %v_ref.11, bf16[768,1024]{1,0:T(8,128)(2,1)} %g_ref.11, ...), custom_call_target="tpu_custom_call" | custom-call | tf_op jit(solution)/shard_map/local/pallas_call | solution.py:259
  31.7 0.0 collective-permute-done.3
  31.7 0.0 collective-permute-done.2
  31.8 0.8 %select_select_fusion.4 = (f32[4,128,128]{2,1,0:T(8,128)}, f32[4,128,128]{2,1,0:T(8,128)S(1)}, f32[4,128,128]{2,1,0:T(8,128)S(1)}) fusion(f32[4,128,128]{2,1,0:T(8,128)S(1)} %collective-permute-done.2, f32[4,128,128]{2,1,0:T(8,128)S(1)} %collective-permute-done.1, f32[8,128,128]{2,1,0:T(8,128)S(1)} %copy-done.1, f32[8,128,128]{2,1,0:T(8,128)S(1)} %copy-done, ...), kind=kLoop, calls=%fused_computation.7 | loop fusion | flops 917504 | bytes 2883593 | tf_op jit(solution)/shard_map/jit(_where)/select_n | solution.py:305
  32.6 3.6 %collective-permute-start.4 = (f32[4,128,128]{2,1,0:T(8,128)S(1)}, f32[4,128,128]{2,1,0:T(8,128)S(1)}, u32[]{:S(2)}, u32[]{:S(2)}) collective-permute-start(f32[4,128,128]{2,1,0:T(8,128)S(1)} %get-tuple-element.99), channel_id=1, source_target_pairs={{0,8},{16,24},{20,28},{1,9},{17,25},{21,29},{2,10},{18,26},{22,30}... | collective-permute-start | bytes 786440 | tf_op jit(solution)/shard_map/ppermute | solution.py:310
  36.3 1.3 %collective-permute-start.5 = (f32[4,128,128]{2,1,0:T(8,128)S(1)}, f32[4,128,128]{2,1,0:T(8,128)S(1)}, u32[]{:S(2)}, u32[]{:S(2)}) collective-permute-start(f32[4,128,128]{2,1,0:T(8,128)S(1)} %get-tuple-element.100), channel_id=1, source_target_pairs={{8,0},{16,8},{20,12},{9,1},{17,9},{21,13},{10,2},{18,10},{22,14},{... | collective-permute-start | bytes 786440 | tf_op jit(solution)/shard_map/ppermute | solution.py:310
  37.6 7.5 %local.3 = (f32[768,512]{1,0:T(8,128)}, f32[768,512]{1,0:T(8,128)}, f32[768,512]{1,0:T(8,128)}, f32[768,512]{1,0:T(8,128)}) custom-call(bf16[768,1024]{1,0:T(8,128)(2,1)} %q_ref.11, bf16[768,1024]{1,0:T(8,128)(2,1)} %k_ref.11, bf16[768,1024]{1,0:T(8,128)(2,1)} %v_ref.11, bf16[768,1024]{1,0:T(8,128)(2,1)} %g_ref.11, ...), custom_call_target="tpu_custom_call" | custom-call | tf_op jit(solution)/shard_map/local/pallas_call | solution.py:259
  45.1 0.0 collective-permute-done.4
  45.1 1.0 %select_select_fusion.1 = (f32[4,128,128]{2,1,0:T(8,128)}, f32[4,128,128]{2,1,0:T(8,128)}, f32[4,128,128]{2,1,0:T(8,128)S(1)}) fusion(f32[4,128,128]{2,1,0:T(8,128)S(1)} %collective-permute-done.2, f32[4,128,128]{2,1,0:T(8,128)S(1)} %collective-permute-done.5, f32[4,128,128]{2,1,0:T(8,128)S(1)} %collective-permute-done.6, ...), kind=kLoop, calls=%fused_computation.4 | loop fusion | flops 1835008 | bytes 3145741 | tf_op jit(solution)/shard_map/jit(_where)/select_n | solution.py:305
  46.2 0.0 collective-permute-start.7
  46.2 7.4 %final.2 = (bf16[768,1024]{1,0:T(8,128)(2,1)}, bf16[768,1024]{1,0:T(8,128)(2,1)}, bf16[768,1024]{1,0:T(8,128)(2,1)}, bf16[768,1024]{1,0:T(8,128)(2,1)}) custom-call(bf16[768,1024]{1,0:T(8,128)(2,1)} %q_ref.11, bf16[768,1024]{1,0:T(8,128)(2,1)} %k_ref.11, bf16[768,1024]{1,0:T(8,128)(2,1)} %v_ref.11, bf16[768,1024]{1,0:T(8,128)(2,1)} %g_ref.11, ...), custom_call_target="tpu_custom_call" | custom-call | tf_op jit(solution)/shard_map/final/pallas_call | solution.py:275
  53.6 0.9 %fusion.1 = (f32[4,128,128]{2,1,0:T(8,128)}, f32[4,128,128]{2,1,0:T(8,128)}) fusion(f32[4,128,128]{2,1,0:T(8,128)S(1)} %collective-permute-done.3, f32[4,128,128]{2,1,0:T(8,128)S(1)} %collective-permute-done.7, f32[4,128,128]{2,1,0:T(8,128)S(1)} %collective-permute-done.2, f32[]{:T(128)} %bitcast, pred[]{:T(512)S(6)} %eq.26, pred[]{:T(512)S(6)} %eq.23, ...), kind=kLoop, calls=%fused_computation.2 | loop fusion | flops 655360 | bytes 2097163 | tf_op jit(solution)/shard_map/jit(_where)/select_n | solution.py:305
  54.5 7.4 %final.3 = (bf16[768,1024]{1,0:T(8,128)(2,1)}, bf16[768,1024]{1,0:T(8,128)(2,1)}, bf16[768,1024]{1,0:T(8,128)(2,1)}, bf16[768,1024]{1,0:T(8,128)(2,1)}) custom-call(bf16[768,1024]{1,0:T(8,128)(2,1)} %q_ref.11, bf16[768,1024]{1,0:T(8,128)(2,1)} %k_ref.11, ...), custom_call_target="tpu_custom_call", output_to_operand_aliasing={{0}: (14, {}), {1}: (15, {}), {2}: (16, {}), {3}: (17, {})} | custom-call | tf_op jit(solution)/shard_map/final/pallas_call | solution.py:275
  (8 shorter events, 0.0 us)
Async XLA Ops:
  0.6 8.0 %copy-start.2 = (s32[16]{0:T(128)S(1)}, s32[16]{0:T(128)}, u32[]{:S(2)}) copy-start(s32[16]{0:T(128)} %lengths.3) | copy-start | bytes 196
  5.7 10.4 %collective-permute-start = (f32[4,128,128]{2,1,0:T(8,128)}, f32[4,128,128]{2,1,0:T(8,128)S(1)}, u32[]{:S(2)}, u32[]{:S(2)}) collective-permute-start(f32[4,128,128]{2,1,0:T(8,128)} %get-tuple-element.51), channel_id=1, source_target_pairs={{0,4},{4,0},{8,12},{12,8},{16,20},{20,16},{24,28},{28,24},{1,5},{5... | collective-permute-start | bytes 786440 | tf_op jit(solution)/shard_map/ppermute | solution.py:310
  17.4 14.3 %collective-permute-start.3 = (f32[4,128,128]{2,1,0:T(8,128)S(1)}, f32[4,128,128]{2,1,0:T(8,128)S(1)}, u32[]{:S(2)}, u32[]{:S(2)}) collective-permute-start(f32[4,128,128]{2,1,0:T(8,128)S(1)} %get-tuple-element.106), channel_id=1, source_target_pairs={{0,4},{4,0},{8,12},{12,8},{16,20},{20,16},{24,28},{28,24},{1,5},{5... | collective-permute-start | bytes 786440 | tf_op jit(solution)/shard_map/ppermute | solution.py:310
  18.3 13.5 %collective-permute-start.2 = (f32[4,128,128]{2,1,0:T(8,128)S(1)}, f32[4,128,128]{2,1,0:T(8,128)S(1)}, u32[]{:S(2)}, u32[]{:S(2)}) collective-permute-start(f32[4,128,128]{2,1,0:T(8,128)S(1)} %get-tuple-element.107), channel_id=1, source_target_pairs={{8,0},{24,16},{28,20},{9,1},{25,17},{29,21},{10,2},{26,18},{30,22}... | collective-permute-start | bytes 786440 | tf_op jit(solution)/shard_map/ppermute | solution.py:310
  19.6 12.2 %collective-permute-start.1 = (f32[4,128,128]{2,1,0:T(8,128)S(1)}, f32[4,128,128]{2,1,0:T(8,128)S(1)}, u32[]{:S(2)}, u32[]{:S(2)}) collective-permute-start(f32[4,128,128]{2,1,0:T(8,128)S(1)} %get-tuple-element.108), channel_id=1, source_target_pairs={{0,8},{8,16},{12,20},{1,9},{9,17},{13,21},{2,10},{10,18},{14,22},{... | collective-permute-start | bytes 786440 | tf_op jit(solution)/shard_map/ppermute | solution.py:310
  24.2 7.6 %copy-start = (f32[8,128,128]{2,1,0:T(8,128)S(1)}, f32[8,128,128]{2,1,0:T(8,128)}, u32[]{:S(2)}) copy-start(f32[8,128,128]{2,1,0:T(8,128)} %get-tuple-element.57) | copy-start | bytes 1572868
  24.2 7.6 %copy-start.1 = (f32[8,128,128]{2,1,0:T(8,128)S(1)}, f32[8,128,128]{2,1,0:T(8,128)}, u32[]{:S(2)}) copy-start(f32[8,128,128]{2,1,0:T(8,128)} %get-tuple-element.58) | copy-start | bytes 1572868
  32.6 12.5 %collective-permute-start.6 = (f32[4,128,128]{2,1,0:T(8,128)}, f32[4,128,128]{2,1,0:T(8,128)S(1)}, u32[]{:S(2)}, u32[]{:S(2)}) collective-permute-start(f32[4,128,128]{2,1,0:T(8,128)} %get-tuple-element.98), channel_id=1, source_target_pairs={{0,4},{4,0},{8,12},{12,8},{16,20},{20,16},{24,28},{28,24},{1,5},{5... | collective-permute-start | bytes 786440 | tf_op jit(solution)/shard_map/ppermute | solution.py:310
  32.6 12.5 %collective-permute-start.4 = (f32[4,128,128]{2,1,0:T(8,128)S(1)}, f32[4,128,128]{2,1,0:T(8,128)S(1)}, u32[]{:S(2)}, u32[]{:S(2)}) collective-permute-start(f32[4,128,128]{2,1,0:T(8,128)S(1)} %get-tuple-element.99), channel_id=1, source_target_pairs={{0,8},{16,24},{20,28},{1,9},{17,25},{21,29},{2,10},{18,26},{22,30}... | collective-permute-start | bytes 786440 | tf_op jit(solution)/shard_map/ppermute | solution.py:310
  36.3 8.8 %collective-permute-start.5 = (f32[4,128,128]{2,1,0:T(8,128)S(1)}, f32[4,128,128]{2,1,0:T(8,128)S(1)}, u32[]{:S(2)}, u32[]{:S(2)}) collective-permute-start(f32[4,128,128]{2,1,0:T(8,128)S(1)} %get-tuple-element.100), channel_id=1, source_target_pairs={{8,0},{16,8},{20,12},{9,1},{17,9},{21,13},{10,2},{18,10},{22,14},{... | collective-permute-start | bytes 786440 | tf_op jit(solution)/shard_map/ppermute | solution.py:310
  46.2 7.5 %collective-permute-start.7 = (f32[4,128,128]{2,1,0:T(8,128)S(1)}, f32[4,128,128]{2,1,0:T(8,128)S(1)}, u32[]{:S(2)}, u32[]{:S(2)}) collective-permute-start(f32[4,128,128]{2,1,0:T(8,128)S(1)} %get-tuple-element.105), channel_id=1, source_target_pairs={{0,4},{4,0},{8,12},{12,8},{16,20},{20,16},{24,28},{28,24},{1,5},{5... | collective-permute-start | bytes 786440 | tf_op jit(solution)/shard_map/ppermute | solution.py:310

commit v4 on v0

v4 whole, which is shorter than its diff:
```python
import functools

import jax
import jax.numpy as jnp
from jax import lax
from jax.experimental import pallas as pl
from jax.experimental.pallas import tpu as pltpu
from jax.sharding import PartitionSpec as P

DH = 128
ROWS = 256
VMEM_LIMIT = 16 << 20
F32 = jnp.float32
LOW = jnp.bfloat16

NT = (((1,), (1,)), ((), ()))
TN = (((0,), (0,)), ((), ()))
NN = (((1,), (0,)), ((), ()))


def dot(a, b, dims):
    return lax.dot_general(a, b, dims, preferred_element_type=F32)


def split(a):
    high = a.astype(LOW)
    return high, (a - high.astype(F32)).astype(LOW)


def write_layout(lengths, offset, scale_ref, first_ref):
    count = scale_ref.shape[0]
    tiles = count // DH
    shape = (tiles, DH)
    row = lax.broadcasted_iota(jnp.int32, shape, 0) * DH + lax.broadcasted_iota(jnp.int32, shape, 1) + offset
    first = jnp.zeros(shape, jnp.int32)
    start = jnp.int32(0)
    for j in range(lengths.shape[0]):
        first = jnp.where(row >= start, start, first)
        start = start + lengths[j]
    scale = 1.0 / jnp.sqrt((row - first + 1).astype(F32) * DH)
    first = (first - offset).astype(F32)
    for t in range(tiles):
        rows = slice(t * DH, (t + 1) * DH)
        scale_ref[rows] = jnp.broadcast_to(scale[t : t + 1], (DH, DH)).T
        first_ref[rows] = jnp.broadcast_to(first[t : t + 1], (DH, DH)).T


def row_index(rows, base):
    return (lax.broadcasted_iota(jnp.int32, (rows, DH), 0) + base).astype(F32)


def key_values(k, v, start, base):
    tail = jnp.where(row_index(k.shape[0], base) >= start, k, jnp.zeros((), LOW))
    return dot(tail, v, TN)


def query_grads(q, g, scale, first, base):
    scaled = jnp.where(first < base, scale * g.astype(F32), 0.0)
    both = dot(q, jnp.concatenate(split(scaled), axis=1), TN)
    return both[:, :DH] + both[:, DH:]


def columns(h):
    return slice(h * DH, (h + 1) * DH)


def first_kernel(
    lengths_hbm, q_hbm, k_hbm, v_hbm, g_hbm, send_ref, scale_ref, first_ref, link_ref, lengths, left, right, sems, sem
):
    lengths_copy = pltpu.make_async_copy(lengths_hbm, lengths, sem)
    lengths_copy.start()
    count = scale_ref.shape[0]
    place = lax.axis_index("seq")
    width = left.shape[1]
    part = jnp.where(place < 2, 0, 1 - lax.rem(place, 2)) * width
    pieces = width // (2 * DH)

    def copies(sources):
        made = []
        for piece in range(pieces):
            for n, (source, target) in enumerate(zip(sources, (left, right))):
                column = pl.multiple_of(part + piece * 2 * DH, DH)
                made.append(
                    pltpu.make_async_copy(
                        source.at[:, pl.ds(column, 2 * DH)],
                        target.at[:, piece * 2 * DH : (piece + 1) * 2 * DH],
                        sems.at[n, piece],
                    )
                )
        return made

    def run(sources, total):
        made = copies(sources)
        for piece in range(pieces):
            made[2 * piece].wait()
            made[2 * piece + 1].wait()
            for h in (2 * piece, 2 * piece + 1):
                send_ref[h] = total(left[:, columns(h)], right[:, columns(h)])

    keys = place < 6

    @pl.when(keys)
    def _():
        for copy in copies((k_hbm, v_hbm)):
            copy.start()

    @pl.when(jnp.logical_not(keys))
    def _():
        for copy in copies((q_hbm, g_hbm)):
            copy.start()

    lengths_copy.wait()
    write_layout(lengths, place * count, scale_ref, first_ref)
    link_ref[...] = jnp.full(link_ref.shape, jnp.where(lengths[0] >= 2 * count, 1.0, 0.0), F32)

    @pl.when(keys)
    def _():
        start = first_ref[count - 1 : count]
        run((k_hbm, v_hbm), lambda k, v: key_values(k, v, start, 0))

    @pl.when(jnp.logical_not(keys))
    def _():
        run((q_hbm, g_hbm), lambda q, g: query_grads(q, g, scale_ref[...], first_ref[...], 0.0))


def states_kernel(q_hbm, k_hbm, v_hbm, g_hbm, scale_ref, first_ref, *refs):
    kv_ref, qg_ref, inner_kv_ref, inner_qg_ref, q_ref, k_ref, v_ref, g_ref, sems = refs
    count = q_ref.shape[0]
    chunks = count // ROWS
    steps = []
    for step in range(chunks):
        down, up = step * ROWS, (chunks - 1 - step) * ROWS
        made = []
        for n, (source, target, base) in enumerate(
            ((k_hbm, k_ref, down), (v_hbm, v_ref, down), (q_hbm, q_ref, up), (g_hbm, g_ref, up))
        ):
            rows = slice(base, base + ROWS)
            made.append(pltpu.make_async_copy(source.at[rows], target.at[rows], sems.at[n, step]))
        steps.append(made)
    for made in steps:
        for copy in made:
            copy.start()
    for step, made in enumerate(steps):
        for copy in made:
            copy.wait()
        down, up = step * ROWS, (chunks - 1 - step) * ROWS
        rows, back = slice(down, down + ROWS), slice(up, up + ROWS)
        start = first_ref[down + ROWS - 1 : down + ROWS]
        keep = jnp.where(start < down, 1.0, 0.0)
        up_keep = jnp.where(first_ref[up + ROWS - 1 : up + ROWS] < up, 1.0, 0.0)
        for h in range(kv_ref.shape[0]):
            cols = columns(h)
            kv = key_values(k_ref[rows, cols], v_ref[rows, cols], start, down)
            qg = query_grads(q_ref[back, cols], g_ref[back, cols], scale_ref[back], first_ref[back], up)
            if step:
                kv = inner_kv_ref[step - 1, h] * keep + kv
                qg = inner_qg_ref[chunks - 1 - step, h] * up_keep + qg
            if step < chunks - 1:
                inner_kv_ref[step, h] = kv
                inner_qg_ref[chunks - 2 - step, h] = qg
            else:
                kv_ref[h] = kv
                qg_ref[h] = qg


def part_columns(part, width, h):
    return pl.ds(pl.multiple_of(part * width + h * DH, DH), DH)


def local_kernel(pick, q_ref, k_ref, v_ref, g_ref, scale_ref, first_ref, tie_ref, a_ref, dq_ref, dk_ref, dv_ref):
    del tie_ref
    many = ROWS // DH
    count, width = a_ref.shape
    part = pick()
    row = lax.broadcasted_iota(jnp.int32, (ROWS, ROWS), 0)
    col = lax.broadcasted_iota(jnp.int32, (ROWS, ROWS), 1)
    causal = col <= row
    col = col.astype(F32)

    def chunk(c, _):
        base = pl.multiple_of(c * ROWS, ROWS)
        rows = pl.ds(base, ROWS)
        base = base.astype(F32)
        for h in range(width // DH):
            cols = part_columns(part, width, h)
            to = columns(h)
            q, g, k, v = q_ref[rows, cols], g_ref[rows, cols], k_ref[rows, cols], v_ref[rows, cols]
            scale = scale_ref[rows]
            start = jnp.concatenate([first_ref[rows] - base] * many, axis=1)
            scale_w = jnp.concatenate([scale] * many, axis=1)
            mask = (col >= start) & causal
            scores = jnp.where(mask, dot(q, k, NT), 0.0).astype(LOW)
            grads = jnp.where(mask, dot(g, v, NT) * scale_w, 0.0).astype(LOW)
            scaled = (scale * g.astype(F32)).astype(LOW)
            a_ref[rows, to] = scale * dot(scores, v, NN)
            dq_ref[rows, to] = dot(grads, k, NN)
            dk_ref[rows, to] = dot(grads, q, TN)
            dv_ref[rows, to] = dot(scores, scaled, TN)
        return 0

    lax.fori_loop(0, count // ROWS, chunk, 0)


def final_kernel(
    gather, pick, inputs, aliased, q_ref, k_ref, v_ref, g_ref, a_ref, dq_ref, dk_ref, dv_ref,
    inner_kv_ref, inner_qg_ref, scale_ref, first_ref, *refs
):
    taken = refs[:inputs]
    outs = refs[inputs + aliased : inputs + aliased + 4]
    *kept, kv_ref, qg_ref, sems = refs[inputs + aliased + 4 :]
    out_a, out_q, out_k, out_v = kept
    gather(kv_ref, qg_ref, *taken)
    count, width = out_a.shape
    chunks = count // ROWS
    heads = kv_ref.shape[0]
    part = pick()

    def carried(rows, state, axis):
        both = jnp.concatenate(split(state), axis=axis)
        return dot(jnp.concatenate([rows, rows], axis=1), both, NT if axis else NN)

    copies = []
    for c in range(chunks):
        base = c * ROWS
        rows = slice(base, base + ROWS)
        first = first_ref[rows]
        scale = jnp.where(first < base, scale_ref[rows], 0.0)
        tail = row_index(ROWS, base) >= first_ref[base + ROWS - 1 : base + ROWS]
        for h in range(heads):
            cols = part_columns(part, width, h)
            to = columns(h)
            kv, qg = kv_ref[h], qg_ref[h]
            if c:
                kept_on = jnp.where(first_ref[base - 1 : base] < 0, 1.0, 0.0)
                kv = kv * kept_on + inner_kv_ref[c - 1, part * heads + h]
            if c < chunks - 1:
                kept_on = jnp.where(first_ref[count - 1 : count] < base + ROWS, 1.0, 0.0)
                qg = qg * kept_on + inner_qg_ref[c, part * heads + h]
            out_a[rows, to] = (a_ref[rows, to] + scale * carried(q_ref[rows, cols], kv, 0)).astype(LOW)
            out_q[rows, to] = (dq_ref[rows, to] + scale * carried(g_ref[rows, cols], kv, 1)).astype(LOW)
            out_k[rows, to] = (dk_ref[rows, to] + jnp.where(tail, carried(v_ref[rows, cols], qg, 1), 0.0)).astype(LOW)
            out_v[rows, to] = (dv_ref[rows, to] + jnp.where(tail, carried(k_ref[rows, cols], qg, 0), 0.0)).astype(LOW)
        for n, (kept_ref, out) in enumerate(zip(kept, outs)):
            target = out.at[rows, pl.ds(pl.multiple_of(part * width, DH), width)]
            copies.append(pltpu.make_async_copy(kept_ref.at[rows], target, sems.at[n, c]))
            copies[-1].start()
    for copy in copies:
        copy.wait()


IN_VMEM = pl.BlockSpec(memory_space=pltpu.VMEM)
IN_HBM = pl.BlockSpec(memory_space=pltpu.HBM)
PARAMS = pltpu.CompilerParams(vmem_limit_bytes=VMEM_LIMIT)


def call(kernel, name, out_shape, in_specs, out_specs, scratch=(), aliases=None):
    return pl.pallas_call(
        kernel,
        out_shape=out_shape,
        in_specs=in_specs,
        out_specs=out_specs,
        scratch_shapes=scratch,
        input_output_aliases=aliases or {},
        compiler_params=PARAMS,
        name=name,
    )


def sums_shape(heads, *lead):
    return jax.ShapeDtypeStruct((*lead, heads, DH, DH), F32)


def first_send(arrays, lengths, heads):
    count = arrays[0].shape[0]
    width = heads * DH
    row = jax.ShapeDtypeStruct((count, DH), F32)
    return call(
        first_kernel,
        "first",
        [sums_shape(heads), row, row, jax.ShapeDtypeStruct((DH, DH), F32)],
        [IN_HBM] * 5,
        [IN_VMEM] * 4,
        [pltpu.SMEM(lengths.shape, jnp.int32)]
        + [pltpu.VMEM((count, width), LOW)] * 2
        + [pltpu.SemaphoreType.DMA((2, heads // 2)), pltpu.SemaphoreType.DMA(())],
    )(lengths, *arrays)


def states(arrays, layout):
    count, width = arrays[0].shape
    heads = width // DH
    chunks = count // ROWS
    outs = call(
        states_kernel,
        "states",
        [sums_shape(heads)] * 2
        + [sums_shape(heads, chunks - 1)] * 2
        + [jax.ShapeDtypeStruct((count, width), LOW)] * 4,
        [IN_HBM] * 4 + [IN_VMEM] * 2,
        [IN_VMEM] * 8,
        [pltpu.SemaphoreType.DMA((4, chunks))],
    )(*arrays, *layout)
    return outs[:4], outs[4:]


def local(arrays, layout, heads, pick, tie):
    count = arrays[0].shape[0]
    shape = jax.ShapeDtypeStruct((count, heads * DH), F32)
    return call(
        functools.partial(local_kernel, pick),
        "local",
        [shape] * 4,
        [IN_VMEM] * 6 + [pl.BlockSpec(memory_space=pl.ANY)],
        [IN_VMEM] * 4,
    )(*arrays, *layout, tie)


def final(arrays, parts, inner, layout, gather, pick, taken, outs):
    count, width = arrays[0].shape
    chunks, part_width = count // ROWS, parts[0].shape[1]
    heads = part_width // DH
    extra = tuple(outs or ())
    at = 12 + len(taken)
    return call(
        functools.partial(final_kernel, gather, pick, len(taken), len(extra)),
        "final",
        [jax.ShapeDtypeStruct((count, width), LOW)] * 4,
        [IN_VMEM] * at + [IN_HBM] * len(extra),
        [IN_HBM] * 4,
        [pltpu.VMEM((count, part_width), LOW)] * 4
        + [pltpu.VMEM((heads, DH, DH), F32)] * 2
        + [pltpu.SemaphoreType.DMA((4, chunks))],
        {at + i: i for i in range(len(extra))},
    )(*arrays, *parts, *inner, *layout, *taken, *extra)


PAIRS = [(d, d ^ 1) for d in range(8)]
PAIRS_2 = [(0, 1), (1, 0), (4, 5), (5, 4)]
UP_1 = [(0, 2), (2, 4), (3, 5)]
UP_2 = [(0, 2), (4, 6), (5, 7)]
DOWN_1 = [(2, 0), (6, 4), (7, 5)]
DOWN_2 = [(2, 0), (4, 2), (5, 3)]


def put(ref, *cases):
    place = lax.axis_index("seq")
    for devices, value in cases:
        hit = functools.reduce(jnp.logical_or, [place == d for d in devices])

        @pl.when(hit)
        def _():
            ref[...] = value()


def permute(value, pairs):
    return lax.ppermute(value, "seq", pairs)


def select(kernel, name, outs, *taken):
    heads = taken[0].shape[0]
    return call(kernel, name, [sums_shape(heads)] * outs, [IN_VMEM] * len(taken), [IN_VMEM] * outs)(*taken)


def own():
    return lax.rem(lax.axis_index("seq"), 2)


def other():
    return 1 - own()


def on_eight(arrays, lengths):
    count, width = arrays[0].shape
    heads = width // DH
    half = heads // 2
    low, high = slice(0, half), slice(half, heads)

    def select_1(x0, link, kv, qg, up, down, send):
        put(
            up,
            ((0,), lambda: x0[...] + link[...] * kv[low]),
            ((2, 4), lambda: x0[...] + kv[low]),
            ((3, 5), lambda: x0[...] + kv[high]),
        )
        put(
            down,
            ((2,), lambda: qg[high]),
            ((6,), lambda: x0[...] + qg[low]),
            ((7,), lambda: x0[...] + qg[high]),
        )
        put(
            send,
            ((0, 1, 6), lambda: kv[high]),
            ((2,), lambda: kv[low]),
            ((3, 5), lambda: qg[low]),
            ((4, 7), lambda: qg[high]),
        )

    def select_2(x0, x1, link, up1, down1, kv, qg, up, down, send):
        put(
            up,
            ((0,), lambda: x1[...] + link[...] * kv[high]),
            ((4,), lambda: up1[...] + (x0[...] + kv[low])),
            ((5,), lambda: up1[...] + (x0[...] + kv[high])),
        )
        put(
            down,
            ((2,), lambda: qg[low]),
            ((4,), lambda: down1[...] + (x1[...] + qg[low])),
            ((5,), lambda: down1[...] + (x1[...] + qg[high])),
        )
        put(
            send,
            ((0,), lambda: down1[...]),
            ((1,), lambda: qg[low]),
            ((4,), lambda: up1[...] + kv[low]),
            ((5,), lambda: up1[...]),
        )

    def select_3(down1, up2, down2, kv, qg, send):
        put(
            send,
            ((0, 2), lambda: down2[...]),
            ((1,), lambda: qg[high]),
            ((3,), lambda: down2[...] + qg[high]),
            ((4,), lambda: down1[...]),
            ((5,), lambda: down1[...] + qg[high]),
            ((6,), lambda: up2[...] + kv[low]),
            ((7,), lambda: up2[...]),
        )

    def gather_own(kv, qg, link, x0, x1, x2, up1, down1, up2, down2):
        put(
            kv,
            ((0,), lambda: jnp.zeros_like(kv)),
            ((1,), lambda: x1[...]),
            ((2, 4), lambda: up1[...]),
            ((3,), lambda: x0[...]),
            ((5,), lambda: up1[...] + x0[...]),
            ((6,), lambda: up2[...]),
            ((7,), lambda: up2[...] + x1[...]),
        )
        put(
            qg,
            ((0,), lambda: x2[...] + link[...] * down2[...]),
            ((1,), lambda: x2[...]),
            ((2,), lambda: x1[...] + down2[...]),
            ((3,), lambda: down2[...]),
            ((4,), lambda: x1[...] + down1[...]),
            ((5,), lambda: down1[...]),
            ((6,), lambda: x0[...]),
            ((7,), lambda: jnp.zeros_like(qg)),
        )

    def gather_other(kv, qg, link, x0, x1, x2, x3, down1, up2):
        put(
            kv,
            ((0,), lambda: jnp.zeros_like(kv)),
            ((1,), lambda: x0[...]),
            ((2,), lambda: up2[...]),
            ((3,), lambda: x1[...]),
            ((4, 5), lambda: x2[...]),
            ((6, 7), lambda: x3[...]),
        )
        put(
            qg,
            ((0,), lambda: x3[...] + link[...] * down1[...]),
            ((1, 2, 3, 4, 5), lambda: x3[...]),
            ((6,), lambda: x1[...]),
            ((7,), lambda: jnp.zeros_like(qg)),
        )

    send, *layout, link = first_send(arrays, lengths, half)
    x0 = permute(send, PAIRS)
    (kv, qg, *inner), arrays = states(arrays, layout)
    x0, kv, qg = lax.optimization_barrier((x0, kv, qg))
    up, down, send = select(select_1, "select1", 3, x0, link, kv, qg)
    x1, up1, down1 = permute(send, PAIRS), permute(up, UP_1), permute(down, DOWN_1)
    own_parts = local(arrays, layout, half, own, send)
    x1, up1, down1, *own_parts = lax.optimization_barrier((x1, up1, down1, *own_parts))
    up, down, send = select(select_2, "select2", 3, x0, x1, link, up1, down1, kv, qg)
    x2, up2, down2 = permute(send, PAIRS_2), permute(up, UP_2), permute(down, DOWN_2)
    other_parts = local(arrays, layout, half, other, send)
    x2, up2, down2, *other_parts = lax.optimization_barrier((x2, up2, down2, *other_parts))
    (send,) = select(select_3, "select3", 1, down1, up2, down2, kv, qg)
    x3 = permute(send, PAIRS)
    outs = final(
        arrays, own_parts, inner, layout, gather_own, own, (link, x0, x1, x2, up1, down1, up2, down2), None
    )
    x3, *outs = lax.optimization_barrier((x3, *outs))
    return tuple(
        final(
            arrays, other_parts, inner, layout, gather_other, other, (link, x0, x1, x2, x3, down1, up2), outs
        )
    )


def on_any(arrays, lengths):
    count, width = arrays[0].shape
    heads = width // DH
    _, *layout, _ = first_send(arrays, lengths, heads // 2)
    (kv, qg, *inner), arrays = states(arrays, layout)
    parts = local(arrays, layout, heads, lambda: jnp.int32(0), kv)
    starts_here = (layout[1][count - 1, 0] >= 0).astype(F32)
    kv_all, qg_all, start_all = lax.all_gather((kv, qg, starts_here), "seq")
    place = lax.axis_index("seq")
    devices = lax.axis_size("seq")
    order = jnp.arange(devices)
    last_start = jnp.max(jnp.where((order < place) & (start_all > 0.5), order, 0))
    next_start = jnp.min(jnp.where((order > place) & (start_all > 0.5), order, devices))

    def total(pick, values):
        return jnp.sum(jnp.where(pick[:, None, None, None], values, 0.0), axis=0)

    def gather(kv_ref, qg_ref, before, after):
        kv_ref[...] = before[...]
        qg_ref[...] = after[...]

    before = total((order < place) & (order >= last_start), kv_all)
    after = total((order > place) & (order <= next_start), qg_all)
    return tuple(final(arrays, parts, inner, layout, gather, lambda: jnp.int32(0), (before, after), None))


def per_device(query_rows, key_rows, value_rows, grad_out, doc_lengths):
    *arrays, doc_lengths = (
        pltpu.with_memory_space_constraint(a, pltpu.HBM)
        for a in (query_rows, key_rows, value_rows, grad_out, doc_lengths)
    )
    if lax.axis_size("seq") == 8:
        return on_eight(arrays, doc_lengths)
    return on_any(arrays, doc_lengths)


def solution(mesh):
    placed = P("seq", "head")
    return jax.shard_map(
        per_device,
        mesh=mesh,
        in_specs=(placed, placed, placed, placed, P()),
        out_specs=(placed, placed, placed, placed),
        check_vma=False,
    )
```

time: 233 us -> 47 us (0.20)
  the two profiles are of different devices: /device:TPU:26 before, /device:TPU:0 now
where the time goes in v4:
time: 47 us; the launch traced here: 46.7 us
  Pallas kernels  20.8 us (44%)
  starting transfers between devices  14.2 us (30%)
  waiting for transfers between devices  11 us (23%)
  between operations  0.77 us (2%)
    ppermute x8, starting transfers between devices, permute(): return lax.ppermute(value, 'seq', pairs)  14.2 us
    ppermute x8, waiting for transfers between devices, permute(): return lax.ppermute(value, 'seq', pairs)  11 us
    pallas_call x2, Pallas kernels, local(): call(functools.partial(local_kernel, pick), 'local', [shape] * 4, [IN_VME...  8.99 us
    pallas_call x2, Pallas kernels, final(): call(functools.partial(final_kernel, gather, pick, len(taken), len(extra)...  6 us
    pallas_call x1, Pallas kernels, states(): call(states_kernel, 'states', [sums_shape(heads)] * 2 + [sums_shape(heads...  3.75 us
    pallas_call x1, Pallas kernels, first_send(): call(first_kernel, 'first', [sums_shape(heads), row, row, jax.ShapeDtypeS...  1.83 us
  transfers between devices with their start and end apart: 8, of which 4 were waited for; matrix products, arithmetic and copies ran while one was open for 0% of the time, Pallas kernels for 34%

profile of v4, /device:TPU:0, one launch (start us, length us, event | category | flops | bytes accessed | tf_op | source)
XLA Modules:
  0.0 46.7 jit_solution(16727256336801517250)
XLA Ops:
  0.6 1.8 %first.1 = (f32[4,128,128]{2,1,0:T(8,128)S(1)}, f32[768,128]{1,0:T(8,128)S(1)}, f32[768,128]{1,0:T(8,128)S(1)}, f32[128,128]{1,0:T(8,128)S(1)}) custom-call(s32[16]{0:T(128)} %lengths_hbm.1, bf16[768,1024]{1,0:T(8,128)(2,1)} %q_hbm.3, bf16[768,1024]{1,0:T(8,128)(2,1)} %k_hbm.3, bf16[768,1024]{1,0:T(8,128)(2,1)} %v_hbm.3, bf16[768,1024]{1,0:T(8,128)(2,1)} %g_hbm.3), custom_call_target="tpu_custom_call" | custom-call | tf_op jit(solution)/shard_map/first/pallas_call | solution.py:277
  2.5 3.0 %collective-permute-start = (f32[4,128,128]{2,1,0:T(8,128)S(1)}, f32[4,128,128]{2,1,0:T(8,128)S(1)}, u32[]{:S(2)}, u32[]{:S(2)}) collective-permute-start(f32[4,128,128]{2,1,0:T(8,128)S(1)} %get-tuple-element.62), channel_id=1, source_target_pairs={{0,4},{4,0},{8,12},{12,8},{16,20},{20,16},{24,28},{28,24},{1,5},{5... | collective-permute-start | bytes 786440 | tf_op jit(solution)/shard_map/ppermute | solution.py:356
  5.5 3.8 %states.1 = (f32[8,128,128]{2,1,0:T(8,128)S(1)}, f32[8,128,128]{2,1,0:T(8,128)S(1)}, f32[2,8,128,128]{3,2,1,0:T(8,128)S(1)}, f32[2,8,128,128]{3,2,1,0:T(8,128)S(...) custom-call(bf16[768,1024]{1,0:T(8,128)(2,1)} %q_hbm.3, ...), custom_call_target="tpu_custom_call" | custom-call | tf_op jit(solution)/shard_map/states/pallas_call | solution.py:293
  9.3 2.5 %collective-permute-done.x0.refs_1_ = f32[4,128,128]{2,1,0:T(8,128)S(1)} collective-permute-done((f32[4,128,128]{2,1,0:T(8,128)S(1)}, f32[4,128,128]{2,1,0:T(8,128)S(1)}, u32[]{:S(2)}, u32[]{:S(2)}) %collective-permute-start) | collective-permute-done | bytes 262176 | tf_op jit(solution)/shard_map/ppermute | solution.py:356
  11.8 0.1 select1.1
  11.9 1.7 %collective-permute-start.1 = (f32[4,128,128]{2,1,0:T(8,128)S(1)}, f32[4,128,128]{2,1,0:T(8,128)S(1)}, u32[]{:S(2)}, u32[]{:S(2)}) collective-permute-start(f32[4,128,128]{2,1,0:T(8,128)S(1)} %get-tuple-element.69.tie_ref), channel_id=1, source_target_pairs={{0,4},{4,0},{8,12},{12,8},{16,20},{20,16},{24,28},{28,24},{1,5},{5... | collective-permute-start | bytes 786440 | tf_op jit(solution)/shard_map/ppermute | solution.py:356
  13.6 3.5 %collective-permute-start.2 = (f32[4,128,128]{2,1,0:T(8,128)S(1)}, f32[4,128,128]{2,1,0:T(8,128)S(1)}, u32[]{:S(2)}, u32[]{:S(2)}) collective-permute-start(f32[4,128,128]{2,1,0:T(8,128)S(1)} %get-tuple-element.70), channel_id=1, source_target_pairs={{0,8},{8,16},{12,20},{1,9},{9,17},{13,21},{2,10},{10,18},{14,22},{... | collective-permute-start | bytes 786440 | tf_op jit(solution)/shard_map/ppermute | solution.py:356
  17.2 1.3 %collective-permute-start.3 = (f32[4,128,128]{2,1,0:T(8,128)S(1)}, f32[4,128,128]{2,1,0:T(8,128)S(1)}, u32[]{:S(2)}, u32[]{:S(2)}) collective-permute-start(f32[4,128,128]{2,1,0:T(8,128)S(1)} %get-tuple-element.71), channel_id=1, source_target_pairs={{8,0},{24,16},{28,20},{9,1},{25,17},{29,21},{10,2},{26,18},{30,22}... | collective-permute-start | bytes 786440 | tf_op jit(solution)/shard_map/ppermute | solution.py:356
  18.5 4.5 %local.2 = (f32[768,512]{1,0:T(8,128)S(1)}, f32[768,512]{1,0:T(8,128)S(1)}, f32[768,512]{1,0:T(8,128)S(1)}, f32[768,512]{1,0:T(8,128)S(1)}) custom-call(bf16[768,1024]{1,0:T(8,128)(2,1)S(1)} %get-tuple-element.58.q_ref, bf16[768,1024]{1,0:T(8,128)(2,1)S(1)} %get-tuple-element.59.k_ref, bf16[768,1024]{1,0:T(8,128)(2,1)S(1)} %get-tuple-element.60.v_ref, ...), custom_call_target="tpu_custom_call" | custom-call | tf_op jit(solution)/shard_map/local/pallas_call | solution.py:309
  23.0 0.0 collective-permute-done.1.x1.refs_2_
  23.0 0.0 collective-permute-done.2.up1.refs_4_
  23.0 2.7 %collective-permute-done.3.down1.refs_5_ = f32[4,128,128]{2,1,0:T(8,128)S(1)} collective-permute-done((f32[4,128,128]{2,1,0:T(8,128)S(1)}, f32[4,128,128]{2,1,0:T(8,128)S(1)}, u32[]{:S(2)}, u32[]{:S(2)}) %collective-permute-start.3) | collective-permute-done | bytes 262176 | tf_op jit(solution)/shard_map/ppermute | solution.py:356
  25.7 0.1 select2.1
  25.8 1.9 %collective-permute-start.4 = (f32[4,128,128]{2,1,0:T(8,128)S(1)}, f32[4,128,128]{2,1,0:T(8,128)S(1)}, u32[]{:S(2)}, u32[]{:S(2)}) collective-permute-start(f32[4,128,128]{2,1,0:T(8,128)S(1)} %get-tuple-element.79.tie_ref), channel_id=1, source_target_pairs={{0,4},{4,0},{16,20},{20,16},{1,5},{5,1},{17,21},{21,17},{2,6},{6,2... | collective-permute-start | bytes 786440 | tf_op jit(solution)/shard_map/ppermute | solution.py:356
  27.7 1.3 %collective-permute-start.5 = (f32[4,128,128]{2,1,0:T(8,128)S(1)}, f32[4,128,128]{2,1,0:T(8,128)S(1)}, u32[]{:S(2)}, u32[]{:S(2)}) collective-permute-start(f32[4,128,128]{2,1,0:T(8,128)S(1)} %get-tuple-element.80), channel_id=1, source_target_pairs={{0,8},{16,24},{20,28},{1,9},{17,25},{21,29},{2,10},{18,26},{22,30}... | collective-permute-start | bytes 786440 | tf_op jit(solution)/shard_map/ppermute | solution.py:356
  29.0 1.3 %collective-permute-start.6 = (f32[4,128,128]{2,1,0:T(8,128)S(1)}, f32[4,128,128]{2,1,0:T(8,128)S(1)}, u32[]{:S(2)}, u32[]{:S(2)}) collective-permute-start(f32[4,128,128]{2,1,0:T(8,128)S(1)} %get-tuple-element.81), channel_id=1, source_target_pairs={{8,0},{16,8},{20,12},{9,1},{17,9},{21,13},{10,2},{18,10},{22,14},{... | collective-permute-start | bytes 786440 | tf_op jit(solution)/shard_map/ppermute | solution.py:356
  30.3 4.5 %local.3 = (f32[768,512]{1,0:T(8,128)S(1)}, f32[768,512]{1,0:T(8,128)S(1)}, f32[768,512]{1,0:T(8,128)S(1)}, f32[768,512]{1,0:T(8,128)S(1)}) custom-call(bf16[768,1024]{1,0:T(8,128)(2,1)S(1)} %get-tuple-element.58.q_ref, bf16[768,1024]{1,0:T(8,128)(2,1)S(1)} %get-tuple-element.59.k_ref, bf16[768,1024]{1,0:T(8,128)(2,1)S(1)} %get-tuple-element.60.v_ref, ...), custom_call_target="tpu_custom_call" | custom-call | tf_op jit(solution)/shard_map/local/pallas_call | solution.py:309
  34.8 0.0 collective-permute-done.4.refs_3_
  34.8 0.0 collective-permute-done.5.up2.refs_6_
  34.8 2.4 %collective-permute-done.6.down2.refs_7_ = f32[4,128,128]{2,1,0:T(8,128)S(1)} collective-permute-done((f32[4,128,128]{2,1,0:T(8,128)S(1)}, f32[4,128,128]{2,1,0:T(8,128)S(1)}, u32[]{:S(2)}, u32[]{:S(2)}) %collective-permute-start.6) | collective-permute-done | bytes 262176 | tf_op jit(solution)/shard_map/ppermute | solution.py:356
  37.3 0.1 collective-permute-start.7
  37.4 3.0 %final.2 = (bf16[768,1024]{1,0:T(8,128)(2,1)}, bf16[768,1024]{1,0:T(8,128)(2,1)}, bf16[768,1024]{1,0:T(8,128)(2,1)}, bf16[768,1024]{1,0:T(8,128)(2,1)}) custom-call(bf16[768,1024]{1,0:T(8,128)(2,1)S(1)} %get-tuple-element.58.q_ref, bf16[768,1024]{1,0:T(8,128)(2,1)S(1)} %get-tuple-element.59.k_ref, bf16[768,1024]{1,0:T(8,128)(2,1)S(1)} %get-tuple-element.60.v_ref, ...), custom_call_target="tpu_custom_call" | custom-call | tf_op jit(solution)/shard_map/final/pallas_call | solution.py:324
  40.5 3.3 %collective-permute-done.7.refs_4_ = f32[4,128,128]{2,1,0:T(8,128)S(1)} collective-permute-done((f32[4,128,128]{2,1,0:T(8,128)S(1)}, f32[4,128,128]{2,1,0:T(8,128)S(1)}, u32[]{:S(2)}, u32[]{:S(2)}) %collective-permute-start.7) | collective-permute-done | bytes 262176 | tf_op jit(solution)/shard_map/ppermute | solution.py:356
  43.8 2.9 %final.3 = (bf16[768,1024]{1,0:T(8,128)(2,1)}, bf16[768,1024]{1,0:T(8,128)(2,1)}, bf16[768,1024]{1,0:T(8,128)(2,1)}, bf16[768,1024]{1,0:T(8,128)(2,1)}) custom-call(bf16[768,1024]{1,0:T(8,128)(2,1)S(1)} %get-tuple-element.58.q_ref, ...), custom_call_target="tpu_custom_call", output_to_operand_aliasing={{0}: (19, {}), {1}: (20, {}), {2}: (21, {}), {3}: (22, {})} | custom-call | tf_op jit(solution)/shard_map/final/pallas_call | solution.py:324
  (1 shorter events, 0.0 us)
Async XLA Ops:
  2.5 9.3 %collective-permute-start = (f32[4,128,128]{2,1,0:T(8,128)S(1)}, f32[4,128,128]{2,1,0:T(8,128)S(1)}, u32[]{:S(2)}, u32[]{:S(2)}) collective-permute-start(f32[4,128,128]{2,1,0:T(8,128)S(1)} %get-tuple-element.62), channel_id=1, source_target_pairs={{0,4},{4,0},{8,12},{12,8},{16,20},{20,16},{24,28},{28,24},{1,5},{5... | collective-permute-start | bytes 786440 | tf_op jit(solution)/shard_map/ppermute | solution.py:356
  11.9 11.1 %collective-permute-start.1 = (f32[4,128,128]{2,1,0:T(8,128)S(1)}, f32[4,128,128]{2,1,0:T(8,128)S(1)}, u32[]{:S(2)}, u32[]{:S(2)}) collective-permute-start(f32[4,128,128]{2,1,0:T(8,128)S(1)} %get-tuple-element.69.tie_ref), channel_id=1, source_target_pairs={{0,4},{4,0},{8,12},{12,8},{16,20},{20,16},{24,28},{28,24},{1,5},{5... | collective-permute-start | bytes 786440 | tf_op jit(solution)/shard_map/ppermute | solution.py:356
  13.6 9.4 %collective-permute-start.2 = (f32[4,128,128]{2,1,0:T(8,128)S(1)}, f32[4,128,128]{2,1,0:T(8,128)S(1)}, u32[]{:S(2)}, u32[]{:S(2)}) collective-permute-start(f32[4,128,128]{2,1,0:T(8,128)S(1)} %get-tuple-element.70), channel_id=1, source_target_pairs={{0,8},{8,16},{12,20},{1,9},{9,17},{13,21},{2,10},{10,18},{14,22},{... | collective-permute-start | bytes 786440 | tf_op jit(solution)/shard_map/ppermute | solution.py:356
  17.2 8.5 %collective-permute-start.3 = (f32[4,128,128]{2,1,0:T(8,128)S(1)}, f32[4,128,128]{2,1,0:T(8,128)S(1)}, u32[]{:S(2)}, u32[]{:S(2)}) collective-permute-start(f32[4,128,128]{2,1,0:T(8,128)S(1)} %get-tuple-element.71), channel_id=1, source_target_pairs={{8,0},{24,16},{28,20},{9,1},{25,17},{29,21},{10,2},{26,18},{30,22}... | collective-permute-start | bytes 786440 | tf_op jit(solution)/shard_map/ppermute | solution.py:356
  25.8 9.0 %collective-permute-start.4 = (f32[4,128,128]{2,1,0:T(8,128)S(1)}, f32[4,128,128]{2,1,0:T(8,128)S(1)}, u32[]{:S(2)}, u32[]{:S(2)}) collective-permute-start(f32[4,128,128]{2,1,0:T(8,128)S(1)} %get-tuple-element.79.tie_ref), channel_id=1, source_target_pairs={{0,4},{4,0},{16,20},{20,16},{1,5},{5,1},{17,21},{21,17},{2,6},{6,2... | collective-permute-start | bytes 786440 | tf_op jit(solution)/shard_map/ppermute | solution.py:356
  27.7 7.1 %collective-permute-start.5 = (f32[4,128,128]{2,1,0:T(8,128)S(1)}, f32[4,128,128]{2,1,0:T(8,128)S(1)}, u32[]{:S(2)}, u32[]{:S(2)}) collective-permute-start(f32[4,128,128]{2,1,0:T(8,128)S(1)} %get-tuple-element.80), channel_id=1, source_target_pairs={{0,8},{16,24},{20,28},{1,9},{17,25},{21,29},{2,10},{18,26},{22,30}... | collective-permute-start | bytes 786440 | tf_op jit(solution)/shard_map/ppermute | solution.py:356
  29.0 8.3 %collective-permute-start.6 = (f32[4,128,128]{2,1,0:T(8,128)S(1)}, f32[4,128,128]{2,1,0:T(8,128)S(1)}, u32[]{:S(2)}, u32[]{:S(2)}) collective-permute-start(f32[4,128,128]{2,1,0:T(8,128)S(1)} %get-tuple-element.81), channel_id=1, source_target_pairs={{8,0},{16,8},{20,12},{9,1},{17,9},{21,13},{10,2},{18,10},{22,14},{... | collective-permute-start | bytes 786440 | tf_op jit(solution)/shard_map/ppermute | solution.py:356
  37.3 6.4 %collective-permute-start.7 = (f32[4,128,128]{2,1,0:T(8,128)S(1)}, f32[4,128,128]{2,1,0:T(8,128)S(1)}, u32[]{:S(2)}, u32[]{:S(2)}) collective-permute-start(f32[4,128,128]{2,1,0:T(8,128)S(1)} %select3.1), channel_id=1, source_target_pairs={{0,4},{4,0},{8,12},{12,8},{16,20},{20,16},{24,28},{28,24},{1,5},{5... | collective-permute-start | bytes 786440 | tf_op jit(solution)/shard_map/ppermute | solution.py:356

commit v5 on v4

--- a/solution.py
+++ b/solution.py
@@ -201,51 +201,60 @@
     lax.fori_loop(0, count // ROWS, chunk, 0)
 
 
-def final_kernel(
-    gather, pick, inputs, aliased, q_ref, k_ref, v_ref, g_ref, a_ref, dq_ref, dk_ref, dv_ref,
-    inner_kv_ref, inner_qg_ref, scale_ref, first_ref, *refs
-):
-    taken = refs[:inputs]
-    outs = refs[inputs + aliased : inputs + aliased + 4]
-    *kept, kv_ref, qg_ref, sems = refs[inputs + aliased + 4 :]
-    out_a, out_q, out_k, out_v = kept
-    gather(kv_ref, qg_ref, *taken)
-    count, width = out_a.shape
-    chunks = count // ROWS
-    heads = kv_ref.shape[0]
-    part = pick()
-
-    def carried(rows, state, axis):
-        both = jnp.concatenate(split(state), axis=axis)
-        return dot(jnp.concatenate([rows, rows], axis=1), both, NT if axis else NN)
-
-    copies = []
-    for c in range(chunks):
+def carried(rows, state, axis):
+    both = jnp.concatenate(split(state), axis=axis)
+    return dot(jnp.concatenate([rows, rows], axis=1), both, NT if axis else NN)
+
+
+class Pair:
+    def __init__(self, forward, part, rows, inner, layout, parts, state, kept, outs, sems):
+        self.forward, self.part, self.rows, self.inner = forward, part, rows, inner
+        self.layout, self.parts, self.state, self.kept = layout, parts, state, kept
+        self.count, self.width = kept[0].shape
+        self.copies = []
+        column = pl.ds(pl.multiple_of(part * self.width, DH), self.width)
+        for c in range(self.count // ROWS):
+            span = slice(c * ROWS, (c + 1) * ROWS)
+            for n in range(2):
+                self.copies.append(pltpu.make_async_copy(kept[n].at[span], outs[n].at[span, column], sems.at[n, c]))
+
+    def chunk(self, c):
+        scale_ref, first_ref = self.layout
+        heads = self.width // DH
         base = c * ROWS
         rows = slice(base, base + ROWS)
-        first = first_ref[rows]
-        scale = jnp.where(first < base, scale_ref[rows], 0.0)
-        tail = row_index(ROWS, base) >= first_ref[base + ROWS - 1 : base + ROWS]
+        if self.forward:
+            factor = jnp.where(first_ref[rows] < base, scale_ref[rows], 0.0)
+        else:
+            tail = row_index(ROWS, base) >= first_ref[base + ROWS - 1 : base + ROWS]
         for h in range(heads):
-            cols = part_columns(part, width, h)
+            cols = part_columns(self.part, self.width, h)
             to = columns(h)
-            kv, qg = kv_ref[h], qg_ref[h]
-            if c:
-                kept_on = jnp.where(first_ref[base - 1 : base] < 0, 1.0, 0.0)
-                kv = kv * kept_on + inner_kv_ref[c - 1, part * heads + h]
-            if c < chunks - 1:
-                kept_on = jnp.where(first_ref[count - 1 : count] < base + ROWS, 1.0, 0.0)
-                qg = qg * kept_on + inner_qg_ref[c, part * heads + h]
-            out_a[rows, to] = (a_ref[rows, to] + scale * carried(q_ref[rows, cols], kv, 0)).astype(LOW)
-            out_q[rows, to] = (dq_ref[rows, to] + scale * carried(g_ref[rows, cols], kv, 1)).astype(LOW)
-            out_k[rows, to] = (dk_ref[rows, to] + jnp.where(tail, carried(v_ref[rows, cols], qg, 1), 0.0)).astype(LOW)
-            out_v[rows, to] = (dv_ref[rows, to] + jnp.where(tail, carried(k_ref[rows, cols], qg, 0), 0.0)).astype(LOW)
-        for n, (kept_ref, out) in enumerate(zip(kept, outs)):
-            target = out.at[rows, pl.ds(pl.multiple_of(part * width, DH), width)]
-            copies.append(pltpu.make_async_copy(kept_ref.at[rows], target, sems.at[n, c]))
-            copies[-1].start()
-    for copy in copies:
-        copy.wait()
+            state = self.state[h]
+            if self.forward and c:
+                keep = jnp.where(first_ref[base - 1 : base] < 0, 1.0, 0.0)
+                state = state * keep + self.inner[c - 1, self.part * heads + h]
+            if not self.forward and base + ROWS < self.count:
+                keep = jnp.where(first_ref[self.count - 1 : self.count] < base + ROWS, 1.0, 0.0)
+                state = state * keep + self.inner[c, self.part * heads + h]
+            for n, axis in enumerate((0, 1) if self.forward else (1, 0)):
+                more = carried(self.rows[n][rows, cols], state, axis)
+                more = factor * more if self.forward else jnp.where(tail, more, 0.0)
+                self.kept[n][rows, to] = (self.parts[n][rows, to] + more).astype(LOW)
+        for copy in self.copies[2 * c : 2 * c + 2]:
+            copy.start()
+
+    def run(self):
+        for c in range(self.count // ROWS):
+            self.chunk(c)
+
+    def wait(self):
+        for copy in self.copies:
+            copy.wait()
+
+
+def final_kernel(body, inputs, scratch, *refs):
+    body(refs[:inputs], refs[-scratch - 4 : -scratch], refs[-scratch:])
 
 
 IN_VMEM = pl.BlockSpec(memory_space=pltpu.VMEM)
@@ -315,23 +324,27 @@
     )(*arrays, *layout, tie)
 
 
-def final(arrays, parts, inner, layout, gather, pick, taken, outs):
-    count, width = arrays[0].shape
-    chunks, part_width = count // ROWS, parts[0].shape[1]
-    heads = part_width // DH
+def final(body, inputs, shape, width, pairs, outs=None):
+    count = shape[0]
+    chunks, heads = count // ROWS, width // DH
     extra = tuple(outs or ())
-    at = 12 + len(taken)
+    scratch = [pltpu.VMEM((heads, DH, DH), F32)] * pairs
+    scratch += [pltpu.VMEM((count, width), LOW)] * (2 * pairs)
+    scratch += [pltpu.SemaphoreType.DMA((2, chunks))] * pairs
     return call(
-        functools.partial(final_kernel, gather, pick, len(taken), len(extra)),
+        functools.partial(final_kernel, body, len(inputs), len(scratch)),
         "final",
-        [jax.ShapeDtypeStruct((count, width), LOW)] * 4,
-        [IN_VMEM] * at + [IN_HBM] * len(extra),
+        [jax.ShapeDtypeStruct(shape, LOW)] * 4,
+        [IN_VMEM] * len(inputs) + [IN_HBM] * len(extra),
         [IN_HBM] * 4,
-        [pltpu.VMEM((count, part_width), LOW)] * 4
-        + [pltpu.VMEM((heads, DH, DH), F32)] * 2
-        + [pltpu.SemaphoreType.DMA((4, chunks))],
-        {at + i: i for i in range(len(extra))},
-    )(*arrays, *parts, *inner, *layout, *taken, *extra)
+        scratch,
+        {len(inputs) + i: i for i in range(len(extra))},
+    )(*inputs, *extra)
+
+
+def make_pairs(scratch, pairs):
+    states, kept, sems = scratch[:pairs], scratch[pairs : 3 * pairs], scratch[3 * pairs :]
+    return [(states[n], kept[2 * n : 2 * n + 2], sems[n]) for n in range(pairs)]
 
 
 PAIRS = [(d, d ^ 1) for d in range(8)]
@@ -356,8 +369,7 @@
     return lax.ppermute(value, "seq", pairs)
 
 
-def select(kernel, name, outs, *taken):
-    heads = taken[0].shape[0]
+def select(kernel, name, outs, heads, *taken):
     return call(kernel, name, [sums_shape(heads)] * outs, [IN_VMEM] * len(taken), [IN_VMEM] * outs)(*taken)
 
 
@@ -375,25 +387,27 @@
     half = heads // 2
     low, high = slice(0, half), slice(half, heads)
 
-    def select_1(x0, link, kv, qg, up, down, send):
-        put(
-            up,
-            ((0,), lambda: x0[...] + link[...] * kv[low]),
-            ((2, 4), lambda: x0[...] + kv[low]),
-            ((3, 5), lambda: x0[...] + kv[high]),
-        )
-        put(
-            down,
-            ((2,), lambda: qg[high]),
-            ((6,), lambda: x0[...] + qg[low]),
-            ((7,), lambda: x0[...] + qg[high]),
-        )
+    def select_0(kv, qg, send):
         put(
             send,
             ((0, 1, 6), lambda: kv[high]),
             ((2,), lambda: kv[low]),
             ((3, 5), lambda: qg[low]),
             ((4, 7), lambda: qg[high]),
+        )
+
+    def select_1(x0, link, kv, qg, up, down):
+        put(
+            up,
+            ((0,), lambda: x0[...] + link[...] * kv[low]),
+            ((2, 4), lambda: x0[...] + kv[low]),
+            ((3, 5), lambda: x0[...] + kv[high]),
+        )
+        put(
+            down,
+            ((2,), lambda: qg[high]),
+            ((6,), lambda: x0[...] + qg[low]),
+            ((7,), lambda: x0[...] + qg[high]),
         )
 
     def select_2(x0, x1, link, up1, down1, kv, qg, up, down, send):
@@ -429,7 +443,19 @@
             ((7,), lambda: up2[...]),
         )
 
-    def gather_own(kv, qg, link, x0, x1, x2, up1, down1, up2, down2):
+    def pair(forward, part, taken, outs, made):
+        rows, inner, layout, parts = taken
+        state, kept, sems = made
+        q, k, v, g = rows
+        if forward:
+            return Pair(True, part, (q, g), inner[0], layout, parts[:2], state, kept, outs[:2], sems)
+        return Pair(False, part, (v, k), inner[1], layout, parts[2:], state, kept, outs[2:], sems)
+
+    def final_1(inputs, outs, scratch):
+        rows, inner, layout, mine, others = inputs[:4], inputs[4:6], inputs[6:8], inputs[8:12], inputs[12:16]
+        link, x0, x1, x2, up1, down1, up2, down2 = inputs[16:]
+        made = make_pairs(scratch, 3)
+        kv, qg, more = (m[0] for m in made)
         put(
             kv,
             ((0,), lambda: jnp.zeros_like(kv)),
@@ -451,48 +477,88 @@
             ((6,), lambda: x0[...]),
             ((7,), lambda: jnp.zeros_like(qg)),
         )
-
-    def gather_other(kv, qg, link, x0, x1, x2, x3, down1, up2):
-        put(
-            kv,
-            ((0,), lambda: jnp.zeros_like(kv)),
+        put(
+            more,
+            ((0, 7), lambda: jnp.zeros_like(more)),
             ((1,), lambda: x0[...]),
             ((2,), lambda: up2[...]),
-            ((3,), lambda: x1[...]),
+            ((3, 6), lambda: x1[...]),
             ((4, 5), lambda: x2[...]),
-            ((6, 7), lambda: x3[...]),
-        )
-        put(
-            qg,
+        )
+        ahead = [pair(f, other(), (rows, inner, layout, others), outs, made[2]) for f in (True, False)]
+        pairs = [pair(f, own(), (rows, inner, layout, mine), outs, m) for f, m in zip((True, False), made)]
+        forward = lax.axis_index("seq") < 6
+
+        @pl.when(forward)
+        def _():
+            ahead[0].run()
+
+        @pl.when(jnp.logical_not(forward))
+        def _():
+            ahead[1].run()
+
+        for p in pairs:
+            p.run()
+
+        @pl.when(forward)
+        def _():
+            ahead[0].wait()
+
+        @pl.when(jnp.logical_not(forward))
+        def _():
+            ahead[1].wait()
+
+        for p in pairs:
+            p.wait()
+
+    def final_2(inputs, outs, scratch):
+        rows, inner, layout, others = inputs[:4], inputs[4:6], inputs[6:8], inputs[8:12]
+        link, x3, down1 = inputs[12:]
+        (made,) = make_pairs(scratch, 1)
+        state = made[0]
+        put(
+            state,
             ((0,), lambda: x3[...] + link[...] * down1[...]),
-            ((1, 2, 3, 4, 5), lambda: x3[...]),
-            ((6,), lambda: x1[...]),
-            ((7,), lambda: jnp.zeros_like(qg)),
-        )
-
+            ((1, 2, 3, 4, 5, 6, 7), lambda: x3[...]),
+        )
+        forward = lax.axis_index("seq") >= 6
+
+        @pl.when(forward)
+        def _():
+            p = pair(True, other(), (rows, inner, layout, others), outs, made)
+            p.run()
+            p.wait()
+
+        @pl.when(jnp.logical_not(forward))
+        def _():
+            p = pair(False, other(), (rows, inner, layout, others), outs, made)
+            p.run()
+            p.wait()
+
+    shape, part_width = (count, width), half * DH
     send, *layout, link = first_send(arrays, lengths, half)
     x0 = permute(send, PAIRS)
     (kv, qg, *inner), arrays = states(arrays, layout)
+    (send,) = select(select_0, "select0", 1, half, kv, qg)
+    x1 = permute(send, PAIRS)
     x0, kv, qg = lax.optimization_barrier((x0, kv, qg))
-    up, down, send = select(select_1, "select1", 3, x0, link, kv, qg)
-    x1, up1, down1 = permute(send, PAIRS), permute(up, UP_1), permute(down, DOWN_1)
-    own_parts = local(arrays, layout, half, own, send)
-    x1, up1, down1, *own_parts = lax.optimization_barrier((x1, up1, down1, *own_parts))
-    up, down, send = select(select_2, "select2", 3, x0, x1, link, up1, down1, kv, qg)
-    x2, up2, down2 = permute(send, PAIRS_2), permute(up, UP_2), permute(down, DOWN_2)
-    other_parts = local(arrays, layout, half, other, send)
-    x2, up2, down2, *other_parts = lax.optimization_barrier((x2, up2, down2, *other_parts))
-    (send,) = select(select_3, "select3", 1, down1, up2, down2, kv, qg)
+    up, down = select(select_1, "select1", 2, half, x0, link, kv, qg)
+    up1, down1 = permute(up, UP_1), permute(down, DOWN_1)
+    mine = local(arrays, layout, half, own, up)
+    x1, up1, down1, *mine = lax.optimization_barrier((x1, up1, down1, *mine))
+    up, down, send = select(select_2, "select2", 3, half, x0, x1, link, up1, down1, kv, qg)
+    up2, down2 = permute(up, UP_2), permute(down, DOWN_2)
+    x2 = permute(send, PAIRS_2)
+    others = local(arrays, layout, half, other, send)
+    up2, down2, *others = lax.optimization_barrier((up2, down2, *others))
+    (send,) = select(select_3, "select3", 1, half, down1, up2, down2, kv, qg)
     x3 = permute(send, PAIRS)
+    fixed = (*arrays, *inner, *layout)
     outs = final(
-        arrays, own_parts, inner, layout, gather_own, own, (link, x0, x1, x2, up1, down1, up2, down2), None
+        final_1, (*fixed, *mine, *others, link, x0, x1, x2, up1, down1, up2, down2), shape, part_width, 3
     )
     x3, *outs = lax.optimization_barrier((x3, *outs))
-    return tuple(
-        final(
-            arrays, other_parts, inner, layout, gather_other, other, (link, x0, x1, x2, x3, down1, up2), outs
-        )
-    )
+    return tuple(final(final_2, (*fixed, *others, link, x3, down1), shape, part_width, 1, outs))
 
 
 def on_any(arrays, lengths):
@@ -512,13 +578,21 @@
     def total(pick, values):
         return jnp.sum(jnp.where(pick[:, None, None, None], values, 0.0), axis=0)
 
-    def gather(kv_ref, qg_ref, before, after):
-        kv_ref[...] = before[...]
-        qg_ref[...] = after[...]
-
     before = total((order < place) & (order >= last_start), kv_all)
     after = total((order > place) & (order <= next_start), qg_all)
-    return tuple(final(arrays, parts, inner, layout, gather, lambda: jnp.int32(0), (before, after), None))
+
+    def body(inputs, outs, scratch):
+        q, k, v, g, inner_kv, inner_qg, scale, first, a, dq, dk, dv, kv_ref, qg_ref = inputs
+        made = make_pairs(scratch, 2)
+        zero = jnp.int32(0)
+        for p in (
+            Pair(True, zero, (q, g), inner_kv, (scale, first), (a, dq), kv_ref, made[0][1], outs[:2], made[0][2]),
+            Pair(False, zero, (v, k), inner_qg, (scale, first), (dk, dv), qg_ref, made[1][1], outs[2:], made[1][2]),
+        ):
+            p.run()
+            p.wait()
+
+    return tuple(final(body, (*arrays, *inner, *layout, *parts, before, after), (count, width), width, 2))
 
 
 def per_device(query_rows, key_rows, value_rows, grad_out, doc_lengths):

time: 47 us -> 44.3 us (0.943)
  waiting for transfers between devices: 11 us -> 4.58 us
  starting transfers between devices: 14.2 us -> 17.9 us
    ppermute x8, waiting for transfers between devices: 11 us -> 4.58 us  [permute(): return lax.ppermute(value, 'seq', pairs)]
    ppermute x8, starting transfers between devices: 14.2 us -> 17.9 us  [permute(): return lax.ppermute(value, 'seq', pairs)]
  transfers between devices with their start and end apart: 8 -> 8, of which waited for: 4 -> 3; matrix products, arithmetic and copies ran while one was open for 0% -> 0% of each run, Pallas kernels for 34% -> 38%
where the time goes in v5:
time: 44.3 us; the launch traced here: 44.1 us
  Pallas kernels  20.8 us (47%)
  starting transfers between devices  17.9 us (40%)
  waiting for transfers between devices  4.58 us (10%)
  between operations  0.78 us (2%)
    ppermute x8, starting transfers between devices, permute(): return lax.ppermute(value, 'seq', pairs)  17.9 us
    pallas_call x2, Pallas kernels, local(): call(functools.partial(local_kernel, pick), 'local', [shape] * 4, [IN_VME...  9.02 us
    pallas_call x2, Pallas kernels, final(): call(functools.partial(final_kernel, body, len(inputs), len(scratch)), 'f...  5.98 us
    ppermute x8, waiting for transfers between devices, permute(): return lax.ppermute(value, 'seq', pairs)  4.58 us
    pallas_call x1, Pallas kernels, states(): call(states_kernel, 'states', [sums_shape(heads)] * 2 + [sums_shape(heads...  3.75 us
    pallas_call x1, Pallas kernels, first_send(): call(first_kernel, 'first', [sums_shape(heads), row, row, jax.ShapeDtypeS...  1.83 us
  transfers between devices with their start and end apart: 8, of which 3 were waited for; matrix products, arithmetic and copies ran while one was open for 0% of the time, Pallas kernels for 38%

profile of v5, /device:TPU:0, one launch (start us, length us, event | category | flops | bytes accessed | tf_op | source)
XLA Modules:
  0.0 44.1 jit_solution(12204369367370114191)
XLA Ops:
  0.6 1.8 %first.1 = (f32[4,128,128]{2,1,0:T(8,128)S(1)}, f32[768,128]{1,0:T(8,128)S(1)}, f32[768,128]{1,0:T(8,128)S(1)}, f32[128,128]{1,0:T(8,128)S(1)}) custom-call(s32[16]{0:T(128)} %lengths_hbm.1, bf16[768,1024]{1,0:T(8,128)(2,1)} %q_hbm.3, bf16[768,1024]{1,0:T(8,128)(2,1)} %k_hbm.3, bf16[768,1024]{1,0:T(8,128)(2,1)} %v_hbm.3, bf16[768,1024]{1,0:T(8,128)(2,1)} %g_hbm.3), custom_call_target="tpu_custom_call" | custom-call | tf_op jit(solution)/shard_map/first/pallas_call | solution.py:286
  2.5 3.0 %collective-permute-start = (f32[4,128,128]{2,1,0:T(8,128)S(1)}, f32[4,128,128]{2,1,0:T(8,128)S(1)}, u32[]{:S(2)}, u32[]{:S(2)}) collective-permute-start(f32[4,128,128]{2,1,0:T(8,128)S(1)} %get-tuple-element.62), channel_id=1, source_target_pairs={{0,4},{4,0},{8,12},{12,8},{16,20},{20,16},{24,28},{28,24},{1,5},{5... | collective-permute-start | bytes 786440 | tf_op jit(solution)/shard_map/ppermute | solution.py:369
  5.5 3.8 %states.1 = (f32[8,128,128]{2,1,0:T(8,128)S(1)}, f32[8,128,128]{2,1,0:T(8,128)S(1)}, f32[2,8,128,128]{3,2,1,0:T(8,128)S(1)}, f32[2,8,128,128]{3,2,1,0:T(8,128)S(...) custom-call(bf16[768,1024]{1,0:T(8,128)(2,1)} %q_hbm.3, ...), custom_call_target="tpu_custom_call" | custom-call | tf_op jit(solution)/shard_map/states/pallas_call | solution.py:302
  9.3 0.1 collective-permute-start.1
  9.4 2.8 %collective-permute-done.x0.refs_17_ = f32[4,128,128]{2,1,0:T(8,128)S(1)} collective-permute-done((f32[4,128,128]{2,1,0:T(8,128)S(1)}, f32[4,128,128]{2,1,0:T(8,128)S(1)}, u32[]{:S(2)}, u32[]{:S(2)}) %collective-permute-start) | collective-permute-done | bytes 262176 | tf_op jit(solution)/shard_map/ppermute | solution.py:369
  12.2 0.1 select1.1
  12.3 1.3 %collective-permute-start.3 = (f32[4,128,128]{2,1,0:T(8,128)S(1)}, f32[4,128,128]{2,1,0:T(8,128)S(1)}, u32[]{:S(2)}, u32[]{:S(2)}) collective-permute-start(f32[4,128,128]{2,1,0:T(8,128)S(1)} %get-tuple-element.70), channel_id=1, source_target_pairs={{8,0},{24,16},{28,20},{9,1},{25,17},{29,21},{10,2},{26,18},{30,22}... | collective-permute-start | bytes 786440 | tf_op jit(solution)/shard_map/ppermute | solution.py:369
  13.6 4.6 %collective-permute-start.2 = (f32[4,128,128]{2,1,0:T(8,128)S(1)}, f32[4,128,128]{2,1,0:T(8,128)S(1)}, u32[]{:S(2)}, u32[]{:S(2)}) collective-permute-start(f32[4,128,128]{2,1,0:T(8,128)S(1)} %get-tuple-element.69.tie_ref), channel_id=1, source_target_pairs={{0,8},{8,16},{12,20},{1,9},{9,17},{13,21},{2,10},{10,18},{14,22},{... | collective-permute-start | bytes 786440 | tf_op jit(solution)/shard_map/ppermute | solution.py:369
  18.1 4.5 %local.2 = (f32[768,512]{1,0:T(8,128)S(1)}, f32[768,512]{1,0:T(8,128)S(1)}, f32[768,512]{1,0:T(8,128)S(1)}, f32[768,512]{1,0:T(8,128)S(1)}) custom-call(bf16[768,1024]{1,0:T(8,128)(2,1)S(1)} %get-tuple-element.56.q_ref.refs_0_, bf16[768,1024]{1,0:T(8,128)(2,1)S(1)} %get-tuple-element.57.k_ref.refs_1_, bf16[768,1024]{1,0:T(8,128)(2,1)S(1)} %get-tuple-element.58.v_ref.refs_2_, ...), custom_call_target="tpu_custom_call" | custom-call | tf_op jit(solution)/shard_map/local/pallas_call | solution.py:318
  22.6 0.0 collective-permute-done.1.x1.refs_18_
  22.7 0.0 collective-permute-done.3.down1.refs_21_.refs_14_
  22.7 0.0 collective-permute-done.2.up1.refs_20_
  22.7 0.1 select2.1
  22.8 4.1 %collective-permute-start.4 = (f32[4,128,128]{2,1,0:T(8,128)S(1)}, f32[4,128,128]{2,1,0:T(8,128)S(1)}, u32[]{:S(2)}, u32[]{:S(2)}) collective-permute-start(f32[4,128,128]{2,1,0:T(8,128)S(1)} %get-tuple-element.78), channel_id=1, source_target_pairs={{0,8},{16,24},{20,28},{1,9},{17,25},{21,29},{2,10},{18,26},{22,30}... | collective-permute-start | bytes 786440 | tf_op jit(solution)/shard_map/ppermute | solution.py:369
  26.9 1.3 %collective-permute-start.5 = (f32[4,128,128]{2,1,0:T(8,128)S(1)}, f32[4,128,128]{2,1,0:T(8,128)S(1)}, u32[]{:S(2)}, u32[]{:S(2)}) collective-permute-start(f32[4,128,128]{2,1,0:T(8,128)S(1)} %get-tuple-element.79), channel_id=1, source_target_pairs={{8,0},{16,8},{20,12},{9,1},{17,9},{21,13},{10,2},{18,10},{22,14},{... | collective-permute-start | bytes 786440 | tf_op jit(solution)/shard_map/ppermute | solution.py:369
  28.2 1.9 %collective-permute-start.7 = (f32[4,128,128]{2,1,0:T(8,128)S(1)}, f32[4,128,128]{2,1,0:T(8,128)S(1)}, u32[]{:S(2)}, u32[]{:S(2)}) collective-permute-start(f32[4,128,128]{2,1,0:T(8,128)S(1)} %get-tuple-element.80.tie_ref), channel_id=1, source_target_pairs={{0,4},{4,0},{16,20},{20,16},{1,5},{5,1},{17,21},{21,17},{2,6},{6,2... | collective-permute-start | bytes 786440 | tf_op jit(solution)/shard_map/ppermute | solution.py:369
  30.1 4.5 %local.3 = (f32[768,512]{1,0:T(8,128)S(1)}, f32[768,512]{1,0:T(8,128)S(1)}, f32[768,512]{1,0:T(8,128)S(1)}, f32[768,512]{1,0:T(8,128)S(1)}) custom-call(bf16[768,1024]{1,0:T(8,128)(2,1)S(1)} %get-tuple-element.56.q_ref.refs_0_, bf16[768,1024]{1,0:T(8,128)(2,1)S(1)} %get-tuple-element.57.k_ref.refs_1_, bf16[768,1024]{1,0:T(8,128)(2,1)S(1)} %get-tuple-element.58.v_ref.refs_2_, ...), custom_call_target="tpu_custom_call" | custom-call | tf_op jit(solution)/shard_map/local/pallas_call | solution.py:318
  34.6 0.0 collective-permute-done.4.up2.refs_22_
  34.6 0.5 %collective-permute-done.5.down2.refs_23_ = f32[4,128,128]{2,1,0:T(8,128)S(1)} collective-permute-done((f32[4,128,128]{2,1,0:T(8,128)S(1)}, f32[4,128,128]{2,1,0:T(8,128)S(1)}, u32[]{:S(2)}, u32[]{:S(2)}) %collective-permute-start.5) | collective-permute-done | bytes 262176 | tf_op jit(solution)/shard_map/ppermute | solution.py:369
  35.2 1.6 %collective-permute-start.6 = (f32[4,128,128]{2,1,0:T(8,128)S(1)}, f32[4,128,128]{2,1,0:T(8,128)S(1)}, u32[]{:S(2)}, u32[]{:S(2)}) collective-permute-start(f32[4,128,128]{2,1,0:T(8,128)S(1)} %select3.1), channel_id=1, source_target_pairs={{0,4},{4,0},{8,12},{12,8},{16,20},{20,16},{24,28},{28,24},{1,5},{5... | collective-permute-start | bytes 786440 | tf_op jit(solution)/shard_map/ppermute | solution.py:369
  36.8 1.3 %collective-permute-done.7.refs_19_ = f32[4,128,128]{2,1,0:T(8,128)S(1)} collective-permute-done((f32[4,128,128]{2,1,0:T(8,128)S(1)}, f32[4,128,128]{2,1,0:T(8,128)S(1)}, u32[]{:S(2)}, u32[]{:S(2)}) %collective-permute-start.7) | collective-permute-done | bytes 262176 | tf_op jit(solution)/shard_map/ppermute | solution.py:369
  38.1 4.1 %final.2 = (bf16[768,1024]{1,0:T(8,128)(2,1)}, bf16[768,1024]{1,0:T(8,128)(2,1)}, bf16[768,1024]{1,0:T(8,128)(2,1)}, bf16[768,1024]{1,0:T(8,128)(2,1)}) custom-call(bf16[768,1024]{1,0:T(8,128)(2,1)S(1)} %get-tuple-element.56.q_ref.refs_0_, bf16[768,1024]{1,0:T(8,128)(2,1)S(1)} %get-tuple-element.57.k_ref.refs_1_, ...), custom_call_target="tpu_custom_call" | custom-call | tf_op jit(solution)/shard_map/final/pallas_call | solution.py:334
  42.1 0.0 collective-permute-done.6.refs_13_
  42.1 1.9 %final.3 = (bf16[768,1024]{1,0:T(8,128)(2,1)}, bf16[768,1024]{1,0:T(8,128)(2,1)}, bf16[768,1024]{1,0:T(8,128)(2,1)}, bf16[768,1024]{1,0:T(8,128)(2,1)}) custom-call(bf16[768,1024]{1,0:T(8,128)(2,1)S(1)} %get-tuple-element.56.q_ref.refs_0_, ...), custom_call_target="tpu_custom_call", output_to_operand_aliasing={{0}: (15, {}), {1}: (16, {}), {2}: (17, {}), {3}: (18, {})} | custom-call | tf_op jit(solution)/shard_map/final/pallas_call | solution.py:334
  (2 shorter events, 0.1 us)
Async XLA Ops:
  2.5 9.7 %collective-permute-start = (f32[4,128,128]{2,1,0:T(8,128)S(1)}, f32[4,128,128]{2,1,0:T(8,128)S(1)}, u32[]{:S(2)}, u32[]{:S(2)}) collective-permute-start(f32[4,128,128]{2,1,0:T(8,128)S(1)} %get-tuple-element.62), channel_id=1, source_target_pairs={{0,4},{4,0},{8,12},{12,8},{16,20},{20,16},{24,28},{28,24},{1,5},{5... | collective-permute-start | bytes 786440 | tf_op jit(solution)/shard_map/ppermute | solution.py:369
  9.3 13.3 %collective-permute-start.1 = (f32[4,128,128]{2,1,0:T(8,128)S(1)}, f32[4,128,128]{2,1,0:T(8,128)S(1)}, u32[]{:S(2)}, u32[]{:S(2)}) collective-permute-start(f32[4,128,128]{2,1,0:T(8,128)S(1)} %select0.1), channel_id=1, source_target_pairs={{0,4},{4,0},{8,12},{12,8},{16,20},{20,16},{24,28},{28,24},{1,5},{5... | collective-permute-start | bytes 786440 | tf_op jit(solution)/shard_map/ppermute | solution.py:369
  12.3 10.4 %collective-permute-start.3 = (f32[4,128,128]{2,1,0:T(8,128)S(1)}, f32[4,128,128]{2,1,0:T(8,128)S(1)}, u32[]{:S(2)}, u32[]{:S(2)}) collective-permute-start(f32[4,128,128]{2,1,0:T(8,128)S(1)} %get-tuple-element.70), channel_id=1, source_target_pairs={{8,0},{24,16},{28,20},{9,1},{25,17},{29,21},{10,2},{26,18},{30,22}... | collective-permute-start | bytes 786440 | tf_op jit(solution)/shard_map/ppermute | solution.py:369
  13.6 9.1 %collective-permute-start.2 = (f32[4,128,128]{2,1,0:T(8,128)S(1)}, f32[4,128,128]{2,1,0:T(8,128)S(1)}, u32[]{:S(2)}, u32[]{:S(2)}) collective-permute-start(f32[4,128,128]{2,1,0:T(8,128)S(1)} %get-tuple-element.69.tie_ref), channel_id=1, source_target_pairs={{0,8},{8,16},{12,20},{1,9},{9,17},{13,21},{2,10},{10,18},{14,22},{... | collective-permute-start | bytes 786440 | tf_op jit(solution)/shard_map/ppermute | solution.py:369
  22.8 11.8 %collective-permute-start.4 = (f32[4,128,128]{2,1,0:T(8,128)S(1)}, f32[4,128,128]{2,1,0:T(8,128)S(1)}, u32[]{:S(2)}, u32[]{:S(2)}) collective-permute-start(f32[4,128,128]{2,1,0:T(8,128)S(1)} %get-tuple-element.78), channel_id=1, source_target_pairs={{0,8},{16,24},{20,28},{1,9},{17,25},{21,29},{2,10},{18,26},{22,30}... | collective-permute-start | bytes 786440 | tf_op jit(solution)/shard_map/ppermute | solution.py:369
  26.9 8.3 %collective-permute-start.5 = (f32[4,128,128]{2,1,0:T(8,128)S(1)}, f32[4,128,128]{2,1,0:T(8,128)S(1)}, u32[]{:S(2)}, u32[]{:S(2)}) collective-permute-start(f32[4,128,128]{2,1,0:T(8,128)S(1)} %get-tuple-element.79), channel_id=1, source_target_pairs={{8,0},{16,8},{20,12},{9,1},{17,9},{21,13},{10,2},{18,10},{22,14},{... | collective-permute-start | bytes 786440 | tf_op jit(solution)/shard_map/ppermute | solution.py:369
  28.2 9.9 %collective-permute-start.7 = (f32[4,128,128]{2,1,0:T(8,128)S(1)}, f32[4,128,128]{2,1,0:T(8,128)S(1)}, u32[]{:S(2)}, u32[]{:S(2)}) collective-permute-start(f32[4,128,128]{2,1,0:T(8,128)S(1)} %get-tuple-element.80.tie_ref), channel_id=1, source_target_pairs={{0,4},{4,0},{16,20},{20,16},{1,5},{5,1},{17,21},{21,17},{2,6},{6,2... | collective-permute-start | bytes 786440 | tf_op jit(solution)/shard_map/ppermute | solution.py:369
  35.2 6.9 %collective-permute-start.6 = (f32[4,128,128]{2,1,0:T(8,128)S(1)}, f32[4,128,128]{2,1,0:T(8,128)S(1)}, u32[]{:S(2)}, u32[]{:S(2)}) collective-permute-start(f32[4,128,128]{2,1,0:T(8,128)S(1)} %select3.1), channel_id=1, source_target_pairs={{0,4},{4,0},{8,12},{12,8},{16,20},{20,16},{24,28},{28,24},{1,5},{5... | collective-permute-start | bytes 786440 | tf_op jit(solution)/shard_map/ppermute | solution.py:369

commit v6 on v5

--- a/solution.py
+++ b/solution.py
@@ -349,10 +349,10 @@
 
 PAIRS = [(d, d ^ 1) for d in range(8)]
 PAIRS_2 = [(0, 1), (1, 0), (4, 5), (5, 4)]
-UP_1 = [(0, 2), (2, 4), (3, 5)]
-UP_2 = [(0, 2), (4, 6), (5, 7)]
-DOWN_1 = [(2, 0), (6, 4), (7, 5)]
-DOWN_2 = [(2, 0), (4, 2), (5, 3)]
+UP_1 = [(2, 4), (3, 5)]
+UP_2 = [(0, 2), (2, 0), (4, 6), (5, 7)]
+DOWN_1 = [(0, 2), (2, 0), (6, 4), (7, 5)]
+DOWN_2 = [(4, 2), (5, 3)]
 
 
 def put(ref, *cases):
@@ -399,12 +399,12 @@
     def select_1(x0, link, kv, qg, up, down):
         put(
             up,
-            ((0,), lambda: x0[...] + link[...] * kv[low]),
             ((2, 4), lambda: x0[...] + kv[low]),
             ((3, 5), lambda: x0[...] + kv[high]),
         )
         put(
             down,
+            ((0,), lambda: x0[...] + link[...] * kv[low]),
             ((2,), lambda: qg[high]),
             ((6,), lambda: x0[...] + qg[low]),
             ((7,), lambda: x0[...] + qg[high]),
@@ -414,12 +414,12 @@
         put(
             up,
             ((0,), lambda: x1[...] + link[...] * kv[high]),
+            ((2,), lambda: qg[low]),
             ((4,), lambda: up1[...] + (x0[...] + kv[low])),
             ((5,), lambda: up1[...] + (x0[...] + kv[high])),
         )
         put(
             down,
-            ((2,), lambda: qg[low]),
             ((4,), lambda: down1[...] + (x1[...] + qg[low])),
             ((5,), lambda: down1[...] + (x1[...] + qg[high])),
         )
@@ -434,7 +434,8 @@
     def select_3(down1, up2, down2, kv, qg, send):
         put(
             send,
-            ((0, 2), lambda: down2[...]),
+            ((0,), lambda: up2[...]),
+            ((2,), lambda: down2[...]),
             ((1,), lambda: qg[high]),
             ((3,), lambda: down2[...] + qg[high]),
             ((4,), lambda: down1[...]),
@@ -460,7 +461,8 @@
             kv,
             ((0,), lambda: jnp.zeros_like(kv)),
             ((1,), lambda: x1[...]),
-            ((2, 4), lambda: up1[...]),
+            ((2,), lambda: down1[...]),
+            ((4,), lambda: up1[...]),
             ((3,), lambda: x0[...]),
             ((5,), lambda: up1[...] + x0[...]),
             ((6,), lambda: up2[...]),
@@ -468,7 +470,7 @@
         )
         put(
             qg,
-            ((0,), lambda: x2[...] + link[...] * down2[...]),
+            ((0,), lambda: x2[...] + link[...] * up2[...]),
             ((1,), lambda: x2[...]),
             ((2,), lambda: x1[...] + down2[...]),
             ((3,), lambda: down2[...]),

time: 44.3 us -> 42.3 us (0.955)
  starting transfers between devices: 17.9 us -> 16.4 us
  waiting for transfers between devices: 4.58 us -> 4.01 us
    ppermute x8, starting transfers between devices: 17.9 us -> 16.4 us  [permute(): return lax.ppermute(value, 'seq', pairs)]
    ppermute x8, waiting for transfers between devices: 4.58 us -> 4.01 us  [permute(): return lax.ppermute(value, 'seq', pairs)]
  transfers between devices with their start and end apart: 8 -> 8, of which waited for: 3 -> 3; matrix products, arithmetic and copies ran while one was open for 0% -> 0% of each run, Pallas kernels for 38% -> 40%
where the time goes in v6:
time: 42.3 us; the launch traced here: 42 us
  Pallas kernels  20.8 us (49%)
  starting transfers between devices  16.4 us (39%)
  waiting for transfers between devices  4.01 us (9%)
  between operations  0.78 us (2%)
    ppermute x8, starting transfers between devices, permute(): return lax.ppermute(value, 'seq', pairs)  16.4 us
    pallas_call x2, Pallas kernels, local(): call(functools.partial(local_kernel, pick), 'local', [shape] * 4, [IN_VME...  9.02 us
    pallas_call x2, Pallas kernels, final(): call(functools.partial(final_kernel, body, len(inputs), len(scratch)), 'f...  5.96 us
    ppermute x8, waiting for transfers between devices, permute(): return lax.ppermute(value, 'seq', pairs)  4.01 us
    pallas_call x1, Pallas kernels, states(): call(states_kernel, 'states', [sums_shape(heads)] * 2 + [sums_shape(heads...  3.75 us
    pallas_call x1, Pallas kernels, first_send(): call(first_kernel, 'first', [sums_shape(heads), row, row, jax.ShapeDtypeS...  1.83 us
  transfers between devices with their start and end apart: 8, of which 3 were waited for; matrix products, arithmetic and copies ran while one was open for 0% of the time, Pallas kernels for 40%

profile of v6, /device:TPU:0, one launch (start us, length us, event | category | flops | bytes accessed | tf_op | source)
XLA Modules:
  0.0 42.0 jit_solution(16207767309723940221)
XLA Ops:
  0.6 1.8 %first.1 = (f32[4,128,128]{2,1,0:T(8,128)S(1)}, f32[768,128]{1,0:T(8,128)S(1)}, f32[768,128]{1,0:T(8,128)S(1)}, f32[128,128]{1,0:T(8,128)S(1)}) custom-call(s32[16]{0:T(128)} %lengths_hbm.1, bf16[768,1024]{1,0:T(8,128)(2,1)} %q_hbm.3, bf16[768,1024]{1,0:T(8,128)(2,1)} %k_hbm.3, bf16[768,1024]{1,0:T(8,128)(2,1)} %v_hbm.3, bf16[768,1024]{1,0:T(8,128)(2,1)} %g_hbm.3), custom_call_target="tpu_custom_call" | custom-call | tf_op jit(solution)/shard_map/first/pallas_call | solution.py:286
  2.5 3.0 %collective-permute-start = (f32[4,128,128]{2,1,0:T(8,128)S(1)}, f32[4,128,128]{2,1,0:T(8,128)S(1)}, u32[]{:S(2)}, u32[]{:S(2)}) collective-permute-start(f32[4,128,128]{2,1,0:T(8,128)S(1)} %get-tuple-element.62), channel_id=1, source_target_pairs={{0,4},{4,0},{8,12},{12,8},{16,20},{20,16},{24,28},{28,24},{1,5},{5... | collective-permute-start | bytes 786440 | tf_op jit(solution)/shard_map/ppermute | solution.py:369
  5.5 3.8 %states.1 = (f32[8,128,128]{2,1,0:T(8,128)S(1)}, f32[8,128,128]{2,1,0:T(8,128)S(1)}, f32[2,8,128,128]{3,2,1,0:T(8,128)S(1)}, f32[2,8,128,128]{3,2,1,0:T(8,128)S(...) custom-call(bf16[768,1024]{1,0:T(8,128)(2,1)} %q_hbm.3, ...), custom_call_target="tpu_custom_call" | custom-call | tf_op jit(solution)/shard_map/states/pallas_call | solution.py:302
  9.3 0.1 collective-permute-start.1
  9.4 2.8 %collective-permute-done.x0.refs_17_ = f32[4,128,128]{2,1,0:T(8,128)S(1)} collective-permute-done((f32[4,128,128]{2,1,0:T(8,128)S(1)}, f32[4,128,128]{2,1,0:T(8,128)S(1)}, u32[]{:S(2)}, u32[]{:S(2)}) %collective-permute-start) | collective-permute-done | bytes 262176 | tf_op jit(solution)/shard_map/ppermute | solution.py:369
  12.2 3.9 %collective-permute-start.3 = (f32[4,128,128]{2,1,0:T(8,128)S(1)}, f32[4,128,128]{2,1,0:T(8,128)S(1)}, u32[]{:S(2)}, u32[]{:S(2)}) collective-permute-start(f32[4,128,128]{2,1,0:T(8,128)S(1)} %get-tuple-element.70), channel_id=1, source_target_pairs={{0,8},{8,0},{24,16},{28,20},{1,9},{9,1},{25,17},{29,21},{2,10},{10... | collective-permute-start | bytes 786440 | tf_op jit(solution)/shard_map/ppermute | solution.py:369
  16.1 0.7 %collective-permute-start.2 = (f32[4,128,128]{2,1,0:T(8,128)S(1)}, f32[4,128,128]{2,1,0:T(8,128)S(1)}, u32[]{:S(2)}, u32[]{:S(2)}) collective-permute-start(f32[4,128,128]{2,1,0:T(8,128)S(1)} %get-tuple-element.69.tie_ref), channel_id=1, source_target_pairs={{8,16},{12,20},{9,17},{13,21},{10,18},{14,22},{11,19},{15,23}} | collective-permute-start | bytes 786440 | tf_op jit(solution)/shard_map/ppermute | solution.py:369
  16.8 4.5 %local.2 = (f32[768,512]{1,0:T(8,128)S(1)}, f32[768,512]{1,0:T(8,128)S(1)}, f32[768,512]{1,0:T(8,128)S(1)}, f32[768,512]{1,0:T(8,128)S(1)}) custom-call(bf16[768,1024]{1,0:T(8,128)(2,1)S(1)} %get-tuple-element.56.q_ref.refs_0_, bf16[768,1024]{1,0:T(8,128)(2,1)S(1)} %get-tuple-element.57.k_ref.refs_1_, bf16[768,1024]{1,0:T(8,128)(2,1)S(1)} %get-tuple-element.58.v_ref.refs_2_, ...), custom_call_target="tpu_custom_call" | custom-call | tf_op jit(solution)/shard_map/local/pallas_call | solution.py:318
  21.3 0.0 collective-permute-done.1.x1.refs_18_
  21.3 0.0 collective-permute-done.3.down1.refs_21_.refs_14_
  21.4 0.0 collective-permute-done.2.up1.refs_20_
  21.4 0.1 select2.1
  21.5 4.1 %collective-permute-start.4 = (f32[4,128,128]{2,1,0:T(8,128)S(1)}, f32[4,128,128]{2,1,0:T(8,128)S(1)}, u32[]{:S(2)}, u32[]{:S(2)}) collective-permute-start(f32[4,128,128]{2,1,0:T(8,128)S(1)} %get-tuple-element.78), channel_id=1, source_target_pairs={{0,8},{8,0},{16,24},{20,28},{1,9},{9,1},{17,25},{21,29},{2,10},{10... | collective-permute-start | bytes 786440 | tf_op jit(solution)/shard_map/ppermute | solution.py:369
  25.6 0.7 %collective-permute-start.5 = (f32[4,128,128]{2,1,0:T(8,128)S(1)}, f32[4,128,128]{2,1,0:T(8,128)S(1)}, u32[]{:S(2)}, u32[]{:S(2)}) collective-permute-start(f32[4,128,128]{2,1,0:T(8,128)S(1)} %get-tuple-element.79), channel_id=1, source_target_pairs={{16,8},{20,12},{17,9},{21,13},{18,10},{22,14},{19,11},{23,15}} | collective-permute-start | bytes 786440 | tf_op jit(solution)/shard_map/ppermute | solution.py:369
  26.2 1.9 %collective-permute-start.7 = (f32[4,128,128]{2,1,0:T(8,128)S(1)}, f32[4,128,128]{2,1,0:T(8,128)S(1)}, u32[]{:S(2)}, u32[]{:S(2)}) collective-permute-start(f32[4,128,128]{2,1,0:T(8,128)S(1)} %get-tuple-element.80.tie_ref), channel_id=1, source_target_pairs={{0,4},{4,0},{16,20},{20,16},{1,5},{5,1},{17,21},{21,17},{2,6},{6,2... | collective-permute-start | bytes 786440 | tf_op jit(solution)/shard_map/ppermute | solution.py:369
  28.2 4.5 %local.3 = (f32[768,512]{1,0:T(8,128)S(1)}, f32[768,512]{1,0:T(8,128)S(1)}, f32[768,512]{1,0:T(8,128)S(1)}, f32[768,512]{1,0:T(8,128)S(1)}) custom-call(bf16[768,1024]{1,0:T(8,128)(2,1)S(1)} %get-tuple-element.56.q_ref.refs_0_, bf16[768,1024]{1,0:T(8,128)(2,1)S(1)} %get-tuple-element.57.k_ref.refs_1_, bf16[768,1024]{1,0:T(8,128)(2,1)S(1)} %get-tuple-element.58.v_ref.refs_2_, ...), custom_call_target="tpu_custom_call" | custom-call | tf_op jit(solution)/shard_map/local/pallas_call | solution.py:318
  32.7 0.0 collective-permute-done.4.up2.refs_22_
  32.7 0.0 collective-permute-done.5.down2.refs_23_
  32.7 0.1 select3.1
  32.8 2.1 %collective-permute-start.6 = (f32[4,128,128]{2,1,0:T(8,128)S(1)}, f32[4,128,128]{2,1,0:T(8,128)S(1)}, u32[]{:S(2)}, u32[]{:S(2)}) collective-permute-start(f32[4,128,128]{2,1,0:T(8,128)S(1)} %select3.1), channel_id=1, source_target_pairs={{0,4},{4,0},{8,12},{12,8},{16,20},{20,16},{24,28},{28,24},{1,5},{5... | collective-permute-start | bytes 786440 | tf_op jit(solution)/shard_map/ppermute | solution.py:369
  34.8 0.8 %collective-permute-done.7.refs_19_ = f32[4,128,128]{2,1,0:T(8,128)S(1)} collective-permute-done((f32[4,128,128]{2,1,0:T(8,128)S(1)}, f32[4,128,128]{2,1,0:T(8,128)S(1)}, u32[]{:S(2)}, u32[]{:S(2)}) %collective-permute-start.7) | collective-permute-done | bytes 262176 | tf_op jit(solution)/shard_map/ppermute | solution.py:369
  35.7 4.1 %final.2 = (bf16[768,1024]{1,0:T(8,128)(2,1)}, bf16[768,1024]{1,0:T(8,128)(2,1)}, bf16[768,1024]{1,0:T(8,128)(2,1)}, bf16[768,1024]{1,0:T(8,128)(2,1)}) custom-call(bf16[768,1024]{1,0:T(8,128)(2,1)S(1)} %get-tuple-element.56.q_ref.refs_0_, bf16[768,1024]{1,0:T(8,128)(2,1)S(1)} %get-tuple-element.57.k_ref.refs_1_, ...), custom_call_target="tpu_custom_call" | custom-call | tf_op jit(solution)/shard_map/final/pallas_call | solution.py:334
  39.8 0.4 collective-permute-done.6.refs_13_
  40.1 1.9 %final.3 = (bf16[768,1024]{1,0:T(8,128)(2,1)}, bf16[768,1024]{1,0:T(8,128)(2,1)}, bf16[768,1024]{1,0:T(8,128)(2,1)}, bf16[768,1024]{1,0:T(8,128)(2,1)}) custom-call(bf16[768,1024]{1,0:T(8,128)(2,1)S(1)} %get-tuple-element.56.q_ref.refs_0_, ...), custom_call_target="tpu_custom_call", output_to_operand_aliasing={{0}: (15, {}), {1}: (16, {}), {2}: (17, {}), {3}: (18, {})} | custom-call | tf_op jit(solution)/shard_map/final/pallas_call | solution.py:334
  (2 shorter events, 0.1 us)
Async XLA Ops:
  2.5 9.7 %collective-permute-start = (f32[4,128,128]{2,1,0:T(8,128)S(1)}, f32[4,128,128]{2,1,0:T(8,128)S(1)}, u32[]{:S(2)}, u32[]{:S(2)}) collective-permute-start(f32[4,128,128]{2,1,0:T(8,128)S(1)} %get-tuple-element.62), channel_id=1, source_target_pairs={{0,4},{4,0},{8,12},{12,8},{16,20},{20,16},{24,28},{28,24},{1,5},{5... | collective-permute-start | bytes 786440 | tf_op jit(solution)/shard_map/ppermute | solution.py:369
  9.3 12.0 %collective-permute-start.1 = (f32[4,128,128]{2,1,0:T(8,128)S(1)}, f32[4,128,128]{2,1,0:T(8,128)S(1)}, u32[]{:S(2)}, u32[]{:S(2)}) collective-permute-start(f32[4,128,128]{2,1,0:T(8,128)S(1)} %select0.1), channel_id=1, source_target_pairs={{0,4},{4,0},{8,12},{12,8},{16,20},{20,16},{24,28},{28,24},{1,5},{5... | collective-permute-start | bytes 786440 | tf_op jit(solution)/shard_map/ppermute | solution.py:369
  12.2 9.1 %collective-permute-start.3 = (f32[4,128,128]{2,1,0:T(8,128)S(1)}, f32[4,128,128]{2,1,0:T(8,128)S(1)}, u32[]{:S(2)}, u32[]{:S(2)}) collective-permute-start(f32[4,128,128]{2,1,0:T(8,128)S(1)} %get-tuple-element.70), channel_id=1, source_target_pairs={{0,8},{8,0},{24,16},{28,20},{1,9},{9,1},{25,17},{29,21},{2,10},{10... | collective-permute-start | bytes 786440 | tf_op jit(solution)/shard_map/ppermute | solution.py:369
  16.1 5.2 %collective-permute-start.2 = (f32[4,128,128]{2,1,0:T(8,128)S(1)}, f32[4,128,128]{2,1,0:T(8,128)S(1)}, u32[]{:S(2)}, u32[]{:S(2)}) collective-permute-start(f32[4,128,128]{2,1,0:T(8,128)S(1)} %get-tuple-element.69.tie_ref), channel_id=1, source_target_pairs={{8,16},{12,20},{9,17},{13,21},{10,18},{14,22},{11,19},{15,23}} | collective-permute-start | bytes 786440 | tf_op jit(solution)/shard_map/ppermute | solution.py:369
  21.5 11.2 %collective-permute-start.4 = (f32[4,128,128]{2,1,0:T(8,128)S(1)}, f32[4,128,128]{2,1,0:T(8,128)S(1)}, u32[]{:S(2)}, u32[]{:S(2)}) collective-permute-start(f32[4,128,128]{2,1,0:T(8,128)S(1)} %get-tuple-element.78), channel_id=1, source_target_pairs={{0,8},{8,0},{16,24},{20,28},{1,9},{9,1},{17,25},{21,29},{2,10},{10... | collective-permute-start | bytes 786440 | tf_op jit(solution)/shard_map/ppermute | solution.py:369
  25.6 7.2 %collective-permute-start.5 = (f32[4,128,128]{2,1,0:T(8,128)S(1)}, f32[4,128,128]{2,1,0:T(8,128)S(1)}, u32[]{:S(2)}, u32[]{:S(2)}) collective-permute-start(f32[4,128,128]{2,1,0:T(8,128)S(1)} %get-tuple-element.79), channel_id=1, source_target_pairs={{16,8},{20,12},{17,9},{21,13},{18,10},{22,14},{19,11},{23,15}} | collective-permute-start | bytes 786440 | tf_op jit(solution)/shard_map/ppermute | solution.py:369
  26.2 9.4 %collective-permute-start.7 = (f32[4,128,128]{2,1,0:T(8,128)S(1)}, f32[4,128,128]{2,1,0:T(8,128)S(1)}, u32[]{:S(2)}, u32[]{:S(2)}) collective-permute-start(f32[4,128,128]{2,1,0:T(8,128)S(1)} %get-tuple-element.80.tie_ref), channel_id=1, source_target_pairs={{0,4},{4,0},{16,20},{20,16},{1,5},{5,1},{17,21},{21,17},{2,6},{6,2... | collective-permute-start | bytes 786440 | tf_op jit(solution)/shard_map/ppermute | solution.py:369
  32.8 7.3 %collective-permute-start.6 = (f32[4,128,128]{2,1,0:T(8,128)S(1)}, f32[4,128,128]{2,1,0:T(8,128)S(1)}, u32[]{:S(2)}, u32[]{:S(2)}) collective-permute-start(f32[4,128,128]{2,1,0:T(8,128)S(1)} %select3.1), channel_id=1, source_target_pairs={{0,4},{4,0},{8,12},{12,8},{16,20},{20,16},{24,28},{28,24},{1,5},{5... | collective-permute-start | bytes 786440 | tf_op jit(solution)/shard_map/ppermute | solution.py:369
